TPU v7x, 256 devices: a whole 4x4x8 slice. The times are simulated.
256 devices in a mesh: dp: 32 (over z_hi, y, core), rows: 8 (over z_lo, x).
Axes of the slice: x: 4, y: 4, z: 8 (z_hi: 4, z_lo: 2; z = z_hi * 2 + z_lo), core: 2. Of those that a mesh axis runs over, the one named last changes fastest.
Arguments:
- latent: bfloat16 [32, 320, 16, 128], P('dp', None, 'rows'), may hold values from -14 to 14
- hint_field: bfloat16 [32, 320, 16, 128], P('dp', None, 'rows'), may hold values from -6 to 6
- from_below: bfloat16 [32, 320, 16, 128], P('dp', None, 'rows'), may hold values from -6 to 6
- cotangent: bfloat16 [32, 320, 16, 128], P('dp', None, 'rows'), may hold values from -6 to 6
- timesteps: int32 [32], P('dp'), may hold values from 0 to 999
- time_weight: bfloat16 [320, 1280], replicated, may hold values from -0.3125 to 0.3125
- enc_proj: bfloat16 [1280, 320], replicated, may hold values from -0.4375 to 0.4375
- ctl_proj: bfloat16 [1280, 320], replicated, may hold values from -0.15625 to 0.15625
- dec_proj: bfloat16 [1280, 320], replicated, may hold values from -0.15625 to 0.15625
- enc_conv_one: bfloat16 [320, 3, 3, 320], replicated, may hold values from -0.109375 to 0.109375
- enc_conv_two: bfloat16 [320, 3, 3, 320], replicated, may hold values from -0.109375 to 0.109375
- ctl_conv_one: bfloat16 [320, 3, 3, 320], P('dp'), may hold values from -0.109375 to 0.109375
- ctl_conv_two: bfloat16 [320, 3, 3, 320], P('dp'), may hold values from -0.109375 to 0.109375
- dec_conv_one: bfloat16 [320, 3, 3, 640], P('dp'), may hold values from -0.078125 to 0.078125
- dec_conv_two: bfloat16 [320, 3, 3, 320], P('dp'), may hold values from -0.109375 to 0.109375
- dec_shortcut: bfloat16 [320, 640], P('dp'), may hold values from -0.25 to 0.25
- zero_conv: bfloat16 [320, 320], P('dp'), may hold values from -0.3125 to 0.3125
Outputs:
- ctl_conv_one_grad: float32 [320, 3, 3, 320], P('dp')
- ctl_conv_two_grad: float32 [320, 3, 3, 320], P('dp')
- zero_conv_grad: float32 [320, 320], P('dp')
All inputs are finite; a program needn't handle non-finite values.
Results may differ from a plain program's by a relative error of at most 0.009.
Values may be sent and summed in bfloat16 or wider, within the bound.
A program may use at most 128 MiB of HBM per device.

v0:
```python
import math

import jax
import jax.numpy as jnp
from jax import lax
from jax.sharding import PartitionSpec as P

C = 320
GROUPS = 32


EPSILON = 1e-05
LAYOUT = ("NCHW", "OHWI", "NCHW")


def extended(x, sides, width):
    for axis, dim in sides:
        peers, length = (lax.axis_size(axis), x.shape[dim])
        up = [(i, (i + 1) % peers) for i in range(peers - 1)]
        down = [(j, i) for i, j in up]
        last = lax.slice_in_dim(x, length - width, length, axis=dim)
        first = lax.slice_in_dim(x, 0, width, axis=dim)
        before = lax.ppermute(last, axis, up)
        after = lax.ppermute(first, axis, down)
        x = jnp.concatenate([before, x, after], axis=dim)
    return x


def shifted(value, axis, steps):
    count = lax.axis_size(axis)
    first, last = (max(0, -steps), min(count, count - steps))
    return lax.ppermute(value, axis, [(source, source + steps) for source in range(first, last)])


def conv_rows(padded, weight):
    return lax.conv_general_dilated(
        padded,
        weight,
        (1, 1),
        ((0, 0), (1, 1)),
        dimension_numbers=LAYOUT,
        preferred_element_type=jnp.float32,
    )


def with_halo(source):
    return extended(source, (("rows", 2),), 1)


def mix_channels(matrix, source):
    return jnp.einsum("oi,bihw->bohw", matrix, source, preferred_element_type=jnp.float32)


def mix_back(matrix, upstream):
    return jnp.einsum("oi,bohw->bihw", matrix, upstream, preferred_element_type=jnp.float32)


def flip_kernel(weight):
    return jnp.transpose(weight[:, ::-1, ::-1, :], (3, 1, 2, 0))


def group_norm(source):
    full_shape = source.shape
    grouped = source.reshape(
        full_shape[0], GROUPS, full_shape[1] // GROUPS, full_shape[2], full_shape[3]
    )
    group_count = full_shape[1] // GROUPS * full_shape[2] * full_shape[3] * lax.axis_size("rows")
    group_total, group_square = lax.psum(
        (jnp.sum(grouped, axis=(2, 3, 4)), jnp.sum(grouped * grouped, axis=(2, 3, 4))), "rows"
    )
    average = group_total / group_count
    inv_spread = lax.rsqrt(group_square / group_count - average * average + EPSILON)
    normed = (grouped - average[:, :, None, None, None]) * inv_spread[:, :, None, None, None]
    return (normed.reshape(full_shape), inv_spread)


def norm_back(upstream, normed, inv_spread):
    full_shape = upstream.shape
    groups_here = inv_spread.shape[1]
    grouped = upstream.reshape(
        full_shape[0], groups_here, full_shape[1] // groups_here, full_shape[2], full_shape[3]
    )
    normed_grouped = normed.reshape(grouped.shape)
    group_count = (
        full_shape[1] // groups_here * full_shape[2] * full_shape[3] * lax.axis_size("rows")
    )
    group_total, group_cross = lax.psum(
        (jnp.sum(grouped, axis=(2, 3, 4)), jnp.sum(grouped * normed_grouped, axis=(2, 3, 4))),
        "rows",
    )
    first_mean = (group_total / group_count)[:, :, None, None, None]
    cross_mean = (group_cross / group_count)[:, :, None, None, None]
    result = inv_spread[:, :, None, None, None] * (
        grouped - first_mean - normed_grouped * cross_mean
    )
    return result.reshape(full_shape)


def silu_slope(values):
    sigma = jax.nn.sigmoid(values)
    return sigma * (1.0 + values * (1.0 - sigma))


def input_grad(upstream, weight):
    flipped = flip_kernel(weight)
    padded = jnp.pad(upstream, ((0, 0), (0, 0), (2, 2), (0, 0)))
    spilled = conv_rows(padded, flipped)
    from_next = shifted(spilled[:, :, :1], "rows", -1)
    from_prev = shifted(spilled[:, :, -1:], "rows", 1)
    result = spilled[:, :, 1:-1]
    result = result.at[:, :, :1].add(from_prev)
    result = result.at[:, :, -1:].add(from_next)
    return result


def kernel_grad(upstream, padded):
    wide = jnp.pad(padded, ((0, 0), (0, 0), (0, 0), (1, 1)))
    row_count = upstream.shape[2]
    col_count = upstream.shape[3]
    return jnp.stack(
        [
            jnp.stack(
                [
                    jnp.einsum(
                        "bohw,bihw->oi",
                        upstream,
                        wide[:, :, row_tap : row_tap + row_count, col_tap : col_tap + col_count],
                        preferred_element_type=jnp.float32,
                    )
                    for col_tap in range(3)
                ],
                1,
            )
            for row_tap in range(3)
        ],
        1,
    )


def block_front(source, conv_one, time_term):
    normed_in, spread_in = group_norm(source.astype(jnp.float32))
    first_halo = with_halo(jax.nn.silu(normed_in).astype(jnp.bfloat16))
    inner_sum = conv_rows(first_halo, conv_one) + time_term[:, :, None, None]
    normed, spread = group_norm(inner_sum)
    second_act = jax.nn.silu(normed).astype(jnp.bfloat16)
    return (normed_in, spread_in, first_halo, normed, spread, second_act)


def per_device(
    latent,
    hint_field,
    from_below,
    cotangent,
    timesteps,
    time_weight,
    enc_proj,
    ctl_proj,
    dec_proj,
    enc_conv_one,
    enc_conv_two,
    ctl_conv_one,
    ctl_conv_two,
    dec_conv_one,
    dec_conv_two,
    dec_shortcut,
    zero_conv,
):
    ctl_one, ctl_two, dec_one, dec_two, dec_short, zero_full = (
        lax.all_gather(ctl_conv_one, "dp", axis=0, tiled=True),
        lax.all_gather(ctl_conv_two, "dp", axis=0, tiled=True),
        lax.all_gather(dec_conv_one, "dp", axis=0, tiled=True),
        lax.all_gather(dec_conv_two, "dp", axis=0, tiled=True),
        lax.all_gather(dec_shortcut, "dp", axis=0, tiled=True),
        lax.all_gather(zero_conv, "dp", axis=0, tiled=True),
    )
    half_width = C // 2
    frequency = jnp.exp(-math.log(10000.0) * jnp.arange(half_width, dtype=jnp.float32) / half_width)
    angles = timesteps.astype(jnp.float32)[:, None] * frequency[None, :]
    sinusoid = jnp.concatenate([jnp.cos(angles), jnp.sin(angles)], axis=1).astype(jnp.bfloat16)
    time_embed = jnp.dot(sinusoid, time_weight, preferred_element_type=jnp.float32)
    time_act = jax.nn.silu(time_embed).astype(jnp.bfloat16)
    enc_term = jnp.dot(time_act, enc_proj, preferred_element_type=jnp.float32)
    ctl_term = jnp.dot(time_act, ctl_proj, preferred_element_type=jnp.float32)
    dec_term = jnp.dot(time_act, dec_proj, preferred_element_type=jnp.float32)
    enc_parts = block_front(latent, enc_conv_one, enc_term)
    enc_out = (
        latent.astype(jnp.float32) + conv_rows(with_halo(enc_parts[5]), enc_conv_two)
    ).astype(jnp.bfloat16)
    ctl_in = (latent.astype(jnp.float32) + hint_field.astype(jnp.float32)).astype(jnp.bfloat16)
    ctl_parts = block_front(ctl_in, ctl_one, ctl_term)
    ctl_halo = with_halo(ctl_parts[5])
    ctl_out = (ctl_in.astype(jnp.float32) + conv_rows(ctl_halo, ctl_two)).astype(jnp.bfloat16)
    skip_sum = (enc_out.astype(jnp.float32) + mix_channels(zero_full, ctl_out)).astype(jnp.bfloat16)
    joined = jnp.concatenate([from_below, skip_sum], axis=1)
    dec_parts = block_front(joined, dec_one, dec_term)
    loss_scale = float(
        cotangent.shape[0]
        * lax.axis_size("dp")
        * cotangent.shape[2]
        * lax.axis_size("rows")
        * cotangent.shape[3]
    ) ** (-0.5)
    out_grad = (cotangent.astype(jnp.float32) * loss_scale).astype(jnp.bfloat16)
    dec_second_grad = input_grad(out_grad, dec_two)
    dec_inner_grad = norm_back(
        dec_second_grad * silu_slope(dec_parts[3]), dec_parts[3], dec_parts[4]
    ).astype(jnp.bfloat16)
    skip_first_grad = input_grad(dec_inner_grad, dec_one[:, :, :, C:])
    skip_normed = dec_parts[0][:, C:]
    skip_spread = dec_parts[1][:, GROUPS // 2 :]
    skip_grad = norm_back(
        skip_first_grad * silu_slope(skip_normed), skip_normed, skip_spread
    ) + mix_back(dec_short[:, C:], out_grad)
    skip_grad = skip_grad.astype(jnp.bfloat16)
    zero_local = jnp.einsum("bohw,bihw->oi", skip_grad, ctl_out, preferred_element_type=jnp.float32)
    ctl_out_grad = mix_back(zero_full, skip_grad).astype(jnp.bfloat16)
    two_local = kernel_grad(ctl_out_grad, ctl_halo)
    ctl_second_grad = input_grad(ctl_out_grad, ctl_two)
    ctl_inner_grad = norm_back(
        ctl_second_grad * silu_slope(ctl_parts[3]), ctl_parts[3], ctl_parts[4]
    ).astype(jnp.bfloat16)
    one_local = kernel_grad(ctl_inner_grad, ctl_parts[2])
    owned = (
        lax.psum_scatter(one_local, "dp", scatter_dimension=0, tiled=True),
        lax.psum_scatter(two_local, "dp", scatter_dimension=0, tiled=True),
        lax.psum_scatter(zero_local, "dp", scatter_dimension=0, tiled=True),
    )
    one_grad, two_grad, zero_grad = lax.psum((owned[0], owned[1], owned[2]), "rows")
    return (one_grad, two_grad, zero_grad)


def solution(mesh):
    in_specs = (
        P("dp", None, "rows", None),
        P("dp", None, "rows", None),
        P("dp", None, "rows", None),
        P("dp", None, "rows", None),
        P("dp"),
        P(),
        P(),
        P(),
        P(),
        P(),
        P(),
        P("dp", None, None, None),
        P("dp", None, None, None),
        P("dp", None, None, None),
        P("dp", None, None, None),
        P("dp", None),
        P("dp", None),
    )
    out_specs = (P("dp", None, None, None), P("dp", None, None, None), P("dp", None))
    return jax.shard_map(
        per_device, mesh=mesh, in_specs=in_specs, out_specs=out_specs, check_vma=False
    )
```

profile of v0, /device:TPU:1, one launch (start us, length us, event | category | flops | bytes accessed | tf_op | source)
XLA Modules:
  0.0 864.4 jit_solution(10912018785608878271)
XLA Ops:
  11.7 17.2 %all-reduce.12 = (f32[1,32]{1,0:T(1,128)S(1)}, f32[1,32]{1,0:T(1,128)S(1)}, f32[1,32]{1,0:T(1,128)S(1)}, f32[1,32]{1,0:T(1,128)S(1)}) all-reduce(f32[1,32]{1,0:T(1,128)S(1)} %bitcast.481, f32[1,32]{1,0:T(1,128)S(1)} %bitcast.476, f32[1,32]{1,0:T(1,128)S(1)} %bitcast.479, ...), channel_id=1, replica_groups=mesh['dp'=32,'rows'=8] {'rows'}, use_global_device_ids=true, to_apply=%region_5.6 | all-reduce | flops 128 | bytes 1024 | tf_op jit(solution)/shard_map/psum | solution.py:68
  34.9 4.7 collective-permute-start.2
  41.0 54.0 %all-gather = bf16[32,10,320]{2,1,0:T(8,128)(2,1)S(1)} all-gather(bf16[1,10,320]{2,1,0:T(8,128)(2,1)S(1)} %bitcast.473), channel_id=1, replica_groups=mesh['dp'=32,'rows'=8] {'dp'}, dimensions={0}, use_global_device_ids=true | all-gather | bytes 211200 | tf_op jit(solution)/shard_map/all_gather | solution.py:174
  98.9 2.1 convolution_reduce_fusion.3
  106.0 43.3 %all-gather.1 = bf16[32,10,640]{2,1,0:T(8,128)(2,1)S(1)} all-gather(bf16[1,10,640]{2,1,0:T(8,128)(2,1)S(1)} %bitcast.472), channel_id=1, replica_groups=mesh['dp'=32,'rows'=8] {'dp'}, dimensions={0}, use_global_device_ids=true | all-gather | bytes 422400 | tf_op jit(solution)/shard_map/all_gather | solution.py:173
  159.6 3.1 fusion.27
  162.7 2.0 select_reduce_fusion.3
  165.7 18.9 %all-reduce.11 = (f32[1,32]{1,0:T(1,128)S(1)}, f32[1,32]{1,0:T(1,128)S(1)}, f32[1,32]{1,0:T(1,128)S(1)}, f32[1,32]{1,0:T(1,128)S(1)}) all-reduce(f32[1,32]{1,0:T(1,128)S(1)} %bitcast.480, f32[1,32]{1,0:T(1,128)S(1)} %bitcast.482, f32[1,32]{1,0:T(1,128)S(1)} %bitcast.478, ...), channel_id=1, replica_groups=mesh['dp'=32,'rows'=8] {'rows'}, use_global_device_ids=true, to_apply=%region_8.9 | all-reduce | flops 128 | bytes 1024 | tf_op jit(solution)/shard_map/psum | solution.py:68
  195.9 6.0 collective-permute-start.4
  201.9 3.7 fusion.14
  206.7 4.1 collective-permute-start.10
  216.1 3.1 fusion.20
  227.4 18.3 %all-reduce.10 = (f32[1,32]{1,0:T(1,128)S(1)}, f32[1,32]{1,0:T(1,128)S(1)}) all-reduce(f32[1,32]{1,0:T(1,128)S(1)} %bitcast.484, f32[1,32]{1,0:T(1,128)S(1)} %bitcast.489), channel_id=1, replica_groups=mesh['dp'=32,'rows'=8] {'rows'}, use_global_device_ids=true, to_apply=%region_26.27 | all-reduce | flops 64 | bytes 512 | tf_op jit(solution)/shard_map/psum | solution.py:68
  248.0 3.9 collective-permute-start.8
  255.2 4.0 scatter-add.20
  260.4 2.8 scatter-add.21
  267.1 2.9 copy.236
  270.1 2.7 select_reduce_fusion.1
  273.2 16.7 %all-reduce.9 = (f32[1,32]{1,0:T(1,128)S(1)}, f32[1,32]{1,0:T(1,128)S(1)}) all-reduce(f32[1,32]{1,0:T(1,128)S(1)} %bitcast.486, f32[1,32]{1,0:T(1,128)S(1)} %bitcast.490), channel_id=1, replica_groups=mesh['dp'=32,'rows'=8] {'rows'}, use_global_device_ids=true, to_apply=%region_32.33 | all-reduce | flops 64 | bytes 512 | tf_op jit(solution)/shard_map/psum | solution.py:68
  292.7 15.9 %all-reduce.8 = (f32[1,32]{1,0:T(1,128)S(1)}, f32[1,32]{1,0:T(1,128)S(1)}) all-reduce(f32[1,32]{1,0:T(1,128)S(1)} %bitcast.491, f32[1,32]{1,0:T(1,128)S(1)} %bitcast.485), channel_id=1, replica_groups=mesh['dp'=32,'rows'=8] {'rows'}, use_global_device_ids=true, to_apply=%region_41.42 | all-reduce | flops 64 | bytes 512 | tf_op jit(solution)/shard_map/psum | solution.py:87
  309.8 3.5 fusion.17
  323.9 3.7 collective-permute-done.13
  329.0 16.5 %all-reduce.7 = (f32[1,16]{1,0:T(1,128)S(1)}, f32[1,16]{1,0:T(1,128)S(1)}) all-reduce(f32[1,16]{1,0:T(1,128)S(1)} %bitcast.492, f32[1,16]{1,0:T(1,128)S(1)} %bitcast.487), channel_id=1, replica_groups=mesh['dp'=32,'rows'=8] {'rows'}, use_global_device_ids=true, to_apply=%region_47.48 | all-reduce | flops 32 | bytes 256 | tf_op jit(solution)/shard_map/psum | solution.py:87
  356.2 3.7 fusion.11
  365.4 5.5 copy.283
  374.0 2.8 scatter-add.26
  378.4 2.8 scatter-add.29
  382.0 18.1 %all-reduce.6 = (f32[1,32]{1,0:T(1,128)S(1)}, f32[1,32]{1,0:T(1,128)S(1)}) all-reduce(f32[1,32]{1,0:T(1,128)S(1)} %bitcast.488, f32[1,32]{1,0:T(1,128)S(1)} %bitcast.483), channel_id=1, replica_groups=mesh['dp'=32,'rows'=8] {'rows'}, use_global_device_ids=true, to_apply=%region_53.54 | all-reduce | flops 64 | bytes 512 | tf_op jit(solution)/shard_map/psum | solution.py:87
  405.7 5.5 copy.282
  413.2 363.5 %all-reduce.17.cloned.1.call-done = (f32[320,3,3,320]{3,2,1,0:T(4,128)}, f32[320,3,3,320]{3,2,1,0:T(4,128)}, f32[320,320]{1,0:T(8,128)}) async-done(((f32[320,3,3,320]{3,2,1,0:T(4,128)}, f32[320,3,3,320]{3,2,1,0:T(4,128)}, f32[320,320]{1,0:T(8,128)}), (f32[320,3,3,320]{3,2,1,0:T(4,128)}, f32[320,3,3,320]{3,2,1,0:T(4,128)}, f32[320,320]{1,0:T(8,128)})) %all-reduce.17.cloned.1.call-update) | async-done | bytes 7782416
  780.7 26.2 %psum.167 = f32[10,320]{1,0:T(8,128)} all-reduce(f32[10,320]{1,0:T(8,128)S(1)} %constant_dynamic-slice_fusion), channel_id=1, replica_groups=mesh['dp'=32,'rows'=8] {'rows'}, use_global_device_ids=true, to_apply=%region_59.60 | all-reduce | flops 3200 | bytes 25600 | tf_op jit(solution)/shard_map/psum | solution.py:228
  807.0 47.1 %all-reduce.19.cloned.1.call-done = (f32[10,3,3,320]{3,2,1,0:T(4,128)}, f32[10,3,3,320]{3,2,1,0:T(4,128)}) async-done(((f32[10,3,3,320]{3,2,1,0:T(4,128)}, f32[10,3,3,320]{3,2,1,0:T(4,128)}), (f32[10,3,3,320]{3,2,1,0:T(4,128)}, f32[10,3,3,320]{3,2,1,0:T(4,128)})) %all-reduce.19.cloned.1.call-update) | async-done | bytes 230416 | tf_op jit(solution)/shard_map/psum | solution.py:228
  (386 shorter events, 118.4 us)
Async XLA Ops:
  7.2 155.6 %copy-start = (bf16[320,3,3,320]{3,0,2,1:T(8,128)(2,1)S(1)}, bf16[320,3,3,320]{3,0,2,1:T(8,128)(2,1)}, u32[]{:S(2)}) copy-start(bf16[320,3,3,320]{3,0,2,1:T(8,128)(2,1)} %param.38) | copy-start | bytes 5529604
  7.2 33.8 %copy-start.34 = (bf16[10,320]{1,0:T(8,128)(2,1)S(1)}, bf16[10,320]{1,0:T(8,128)(2,1)}, u32[]{:S(2)}) copy-start(bf16[10,320]{1,0:T(8,128)(2,1)} %param.45) | copy-start | bytes 19204
  7.2 152.4 %all-gather.7.cloned.1.call-start = ((), (), s32[]{:S(2)}) async-start(), calls=%async_computation | async-start | bytes 3041280 | tf_op jit(solution)/shard_map/all_gather | solution.py:169
  7.9 194.0 %all-gather.13.cloned.1.call-start = ((), (), s32[]{:S(2)}) async-start(), calls=%async_computation.3 | async-start | bytes 3041280 | tf_op jit(solution)/shard_map/all_gather | solution.py:172
  8.7 207.4 %all-gather.9.cloned.1.call-start = ((), (), s32[]{:S(2)}) async-start(), calls=%async_computation.1 | async-start | bytes 3041280 | tf_op jit(solution)/shard_map/all_gather | solution.py:170
  9.4 257.7 %all-gather.11.cloned.1.call-start = ((), (), s32[]{:S(2)}) async-start(), calls=%async_computation.2 | async-start | bytes 5068800 | tf_op jit(solution)/shard_map/all_gather | solution.py:171
  10.7 214.6 %copy-start.3 = (bf16[1,320,2,128]{3,1,2,0:T(8,128)(2,1)}, bf16[1,320,2,128]{3,1,2,0:T(8,128)(2,1)S(1)}, u32[]{:S(2)}) copy-start(bf16[1,320,2,128]{3,1,2,0:T(8,128)(2,1)S(1)} %get-tuple-element.159) | copy-start | bytes 491524
  30.1 121.7 %collective-permute-start = (bf16[1,320,1,128]{3,1,2,0:T(8,128)(2,1)}, bf16[1,320,1,128]{3,1,2,0:T(8,128)(2,1)S(1)}, u32[]{:S(2)}, u32[]{:S(2)}) collective-permute-start(bf16[1,320,1,128]{3,1,2,0:T(8,128)(2,1)} %get-tuple-element.153), channel_id=1, source_target_pairs={{0,1},{1,2},{2,3},{3,4},{4,5},{5,6},{6,7},{8,9},{9,10},{10,11},{11... | collective-permute-start | bytes 245768 | tf_op jit(solution)/shard_map/ppermute | solution.py:23
  31.4 121.0 %collective-permute-start.1 = (bf16[1,320,1,128]{3,1,2,0:T(8,128)(2,1)}, bf16[1,320,1,128]{3,1,2,0:T(8,128)(2,1)}, u32[]{:S(2)}, u32[]{:S(2)}) collective-permute-start(bf16[1,320,1,128]{3,1,2,0:T(8,128)(2,1)} %get-tuple-element.154), channel_id=1, source_target_pairs={{1,0},{2,1},{3,2},{4,3},{5,4},{6,5},{7,6},{9,8},{10,9},{11,10},{12... | collective-permute-start | bytes 245768 | tf_op jit(solution)/shard_map/ppermute | solution.py:24
  34.2 68.3 %copy-start.13 = (bf16[1,320,2,128]{3,1,2,0:T(8,128)(2,1)}, bf16[1,320,2,128]{3,1,2,0:T(8,128)(2,1)S(1)}, u32[]{:S(2)}) copy-start(bf16[1,320,2,128]{3,1,2,0:T(8,128)(2,1)S(1)} %fusion.104) | copy-start | bytes 491524
  34.9 67.6 %copy-start.30 = (bf16[1,320,2,128]{3,2,1,0:T(2,128)(2,1)S(1)}, bf16[1,320,2,128]{3,2,1,0:T(2,128)(2,1)}, u32[]{:S(2)}) copy-start(bf16[1,320,2,128]{3,2,1,0:T(2,128)(2,1)} %param.31) | copy-start | bytes 491524
  34.9 120.8 %collective-permute-start.2 = (bf16[1,320,1,128]{3,1,2,0:T(8,128)(2,1)}, bf16[1,320,1,128]{3,1,2,0:T(8,128)(2,1)}, u32[]{:S(2)}, u32[]{:S(2)}) collective-permute-start(bf16[1,320,1,128]{3,1,2,0:T(8,128)(2,1)} %get-tuple-element.155), channel_id=1, source_target_pairs={{0,1},{1,2},{2,3},{3,4},{4,5},{5,6},{6,7},{8,9},{9,10},{10,11},{11... | collective-permute-start | bytes 245768 | tf_op jit(solution)/shard_map/ppermute | solution.py:23
  39.6 116.0 %collective-permute-start.3 = (bf16[1,320,1,128]{3,1,2,0:T(8,128)(2,1)}, bf16[1,320,1,128]{3,1,2,0:T(8,128)(2,1)}, u32[]{:S(2)}, u32[]{:S(2)}) collective-permute-start(bf16[1,320,1,128]{3,1,2,0:T(8,128)(2,1)} %get-tuple-element.156), channel_id=1, source_target_pairs={{1,0},{2,1},{3,2},{4,3},{5,4},{6,5},{7,6},{9,8},{10,9},{11,10},{12... | collective-permute-start | bytes 245768 | tf_op jit(solution)/shard_map/ppermute | solution.py:24
  40.9 735.8 %all-reduce.17.cloned.1.call-start = ((), (), s32[]{:S(2)}) async-start(), calls=%async_computation.4 | async-start | bytes 24576000
  188.3 25.0 %collective-permute-start.6 = (bf16[1,320,1,128]{3,1,2,0:T(8,128)(2,1)}, bf16[1,320,1,128]{3,1,2,0:T(8,128)(2,1)S(1)}, u32[]{:S(2)}, u32[]{:S(2)}) collective-permute-start(bf16[1,320,1,128]{3,1,2,0:T(8,128)(2,1)} %bitcast.32), channel_id=1, source_target_pairs={{0,1},{1,2},{2,3},{3,4},{4,5},{5,6},{6,7},{8,9},{9,10},{10,11},{11... | collective-permute-start | bytes 245768 | tf_op jit(solution)/shard_map/ppermute | solution.py:23
  189.7 12.2 %copy-start.29 = (bf16[320,2,1,8,17]{0,3,4,1,2:T(8,128)(2,1)S(1)}, bf16[320,2,1,8,17]{0,3,4,1,2:T(8,128)(2,1)}, u32[]{:S(2)}) copy-start(bf16[320,2,1,8,17]{0,3,4,1,2:T(8,128)(2,1)} %copy-done.28) | copy-start | bytes 522244
  189.7 12.2 %copy-start.38 = (pred[8,17]{0,1:T(8,128)(4,1)S(1)}, pred[8,17]{0,1:T(8,128)(4,1)}, u32[]{:S(2)}) copy-start(pred[8,17]{0,1:T(8,128)(4,1)} %constant.237) | copy-start | bytes 412
  190.5 24.2 %collective-permute-start.7 = (bf16[1,320,1,128]{3,1,2,0:T(8,128)(2,1)}, bf16[1,320,1,128]{3,1,2,0:T(8,128)(2,1)S(1)}, u32[]{:S(2)}, u32[]{:S(2)}) collective-permute-start(bf16[1,320,1,128]{3,1,2,0:T(8,128)(2,1)} %bitcast.35), channel_id=1, source_target_pairs={{1,0},{2,1},{3,2},{4,3},{5,4},{6,5},{7,6},{9,8},{10,9},{11,10},{12... | collective-permute-start | bytes 245768 | tf_op jit(solution)/shard_map/ppermute | solution.py:24
  193.8 27.1 %collective-permute-start.5 = (bf16[1,320,1,128]{1,2,3,0:T(2,128)(2,1)}, bf16[1,320,1,128]{1,2,3,0:T(2,128)(2,1)}, u32[]{:S(2)}, u32[]{:S(2)}) collective-permute-start(bf16[1,320,1,128]{1,2,3,0:T(2,128)(2,1)} %slice_bitcast_fusion.16), channel_id=1, source_target_pairs={{1,0},{2,1},{3,2},{4,3},{5,4},{6,5},{7,6},{9,8},{10,9},{11,10},{12... | collective-permute-start | bytes 245768 | tf_op jit(solution)/shard_map/ppermute | solution.py:24
  195.9 23.9 %collective-permute-start.4 = (bf16[1,320,1,128]{1,3,0,2:T(8,128)(2,1)}, bf16[1,320,1,128]{1,3,0,2:T(8,128)(2,1)}, u32[]{:S(2)}, u32[]{:S(2)}) collective-permute-start(bf16[1,320,1,128]{1,3,0,2:T(8,128)(2,1)} %slice_bitcast_fusion.18), channel_id=1, source_target_pairs={{0,1},{1,2},{2,3},{3,4},{4,5},{5,6},{6,7},{8,9},{9,10},{10,11},{11... | collective-permute-start | bytes 245768 | tf_op jit(solution)/shard_map/ppermute | solution.py:23
  206.7 46.6 %collective-permute-start.10 = (f32[1,320,1,128]{1,2,3,0:T(1,128)}, f32[1,320,1,128]{1,2,3,0:T(1,128)}, u32[]{:S(2)}, u32[]{:S(2)}) collective-permute-start(f32[1,320,1,128]{1,2,3,0:T(1,128)} %slice_bitcast_fusion.14), channel_id=1, source_target_pairs={{0,1},{1,2},{2,3},{3,4},{4,5},{5,6},{6,7},{8,9},{9,10},{10,11},{11... | collective-permute-start | bytes 491528 | tf_op jit(solution)/shard_map/ppermute | solution.py:32
  213.4 45.8 %collective-permute-start.11 = (f32[1,320,1,128]{1,2,3,0:T(1,128)}, f32[1,320,1,128]{1,2,3,0:T(1,128)}, u32[]{:S(2)}, u32[]{:S(2)}) collective-permute-start(f32[1,320,1,128]{1,2,3,0:T(1,128)} %slice_bitcast_fusion.13), channel_id=1, source_target_pairs={{1,0},{2,1},{3,2},{4,3},{5,4},{6,5},{7,6},{9,8},{10,9},{11,10},{12... | collective-permute-start | bytes 491528 | tf_op jit(solution)/shard_map/ppermute | solution.py:32
  226.7 26.6 %copy-start.17 = (f32[1,8,17,320]{3,0,2,1:T(1,128)S(1)}, f32[1,8,17,320]{3,0,2,1:T(1,128)}, u32[]{:S(2)}) copy-start(f32[1,8,17,320]{3,0,2,1:T(1,128)} %copy.242) | copy-start | bytes 522244
  248.0 15.3 %collective-permute-start.8 = (bf16[1,640,1,128]{3,1,2,0:T(8,128)(2,1)}, bf16[1,640,1,128]{3,1,2,0:T(8,128)(2,1)S(1)}, u32[]{:S(2)}, u32[]{:S(2)}) collective-permute-start(bf16[1,640,1,128]{3,1,2,0:T(8,128)(2,1)} %get-tuple-element.145), channel_id=1, source_target_pairs={{0,1},{1,2},{2,3},{3,4},{4,5},{5,6},{6,7},{8,9},{9,10},{10,11},{11... | collective-permute-start | bytes 491528 | tf_op jit(solution)/shard_map/ppermute | solution.py:23
  251.8 11.4 %collective-permute-start.9 = (bf16[1,640,1,128]{3,1,2,0:T(8,128)(2,1)}, bf16[1,640,1,128]{3,1,2,0:T(8,128)(2,1)}, u32[]{:S(2)}, u32[]{:S(2)}) collective-permute-start(bf16[1,640,1,128]{3,1,2,0:T(8,128)(2,1)} %get-tuple-element.146), channel_id=1, source_target_pairs={{1,0},{2,1},{3,2},{4,3},{5,4},{6,5},{7,6},{9,8},{10,9},{11,10},{12... | collective-permute-start | bytes 491528 | tf_op jit(solution)/shard_map/ppermute | solution.py:24
  315.3 7.6 collective-permute-start.12
  321.5 6.1 collective-permute-start.13
  360.3 13.5 %collective-permute-start.14 = (f32[1,320,1,128]{1,2,3,0:T(1,128)S(1)}, f32[1,320,1,128]{1,2,3,0:T(1,128)S(1)}, u32[]{:S(2)}, u32[]{:S(2)}) collective-permute-start(f32[1,320,1,128]{1,2,3,0:T(1,128)S(1)} %slice_bitcast_fusion.11), channel_id=1, source_target_pairs={{0,1},{1,2},{2,3},{3,4},{4,5},{5,6},{6,7},{8,9},{9,10},{10,11},{11... | collective-permute-start | bytes 491528 | tf_op jit(solution)/shard_map/ppermute | solution.py:32
  371.2 6.9 collective-permute-start.15
  374.0 26.8 %copy-start.33 = (f32[320]{0:T(512)S(1)}, f32[320]{0:T(512)}, u32[]{:S(2)}) copy-start(f32[320]{0:T(512)} %copy-done.32) | copy-start | bytes 3844
  411.3 446.1 %copy-start.1 = (bf16[320,3,3,320]{3,0,2,1:T(8,128)(2,1)S(1)}, bf16[320,3,3,320]{3,0,2,1:T(8,128)(2,1)}, u32[]{:S(2)}) copy-start(bf16[320,3,3,320]{3,0,2,1:T(8,128)(2,1)} %param.38) | copy-start | bytes 5529604
  411.3 442.8 %all-reduce.19.cloned.1.call-start = ((), (), s32[]{:S(2)}) async-start(), calls=%async_computation.5 | async-start | bytes 737280 | tf_op jit(solution)/shard_map/psum | solution.py:228
  (30 other events, 98.6 us)
Sparse Core Ops, SparseCore 0:
  10.6 60.6 all-gather.6
  73.9 55.5 all-gather.12
  132.1 53.6 all-gather.8
  188.3 60.7 all-gather.10
  411.4 365.1 all-reduce.16
  780.1 74.0 all-reduce.18
where the time goes:
time: 879 us; the launch traced here: 864 us
  waiting for transfers between devices  418 us (48%)
  blocking collectives  245 us (28%)
  local copies, waits for them, and re-layouts  76.4 us (9%)
  matrix products  46.1 us (5%)
  starting transfers between devices  35.8 us (4%)
  other arithmetic  25.6 us (3%)
  between operations  17.4 us (2%)
    unnamed x7, waiting for transfers between devices  366 us
    psum x4, blocking collectives, group_norm(): lax.psum((jnp.sum(grouped, axis=(2, 3, 4)), jnp.sum(grouped * grouped, ax...  71.1 us
    all_gather x1, blocking collectives, per_device(): lax.all_gather(zero_conv, 'dp', axis=0, tiled=True)  54 us
    psum x3, blocking collectives, norm_back(): lax.psum((jnp.sum(grouped, axis=(2, 3, 4)), jnp.sum(grouped * normed_grou...  50.5 us
    psum x1, waiting for transfers between devices, per_device(): lax.psum((owned[0], owned[1], owned[2]), 'rows')  47.1 us
    all_gather x1, blocking collectives, per_device(): lax.all_gather(dec_shortcut, 'dp', axis=0, tiled=True)  43.3 us
    psum x1, blocking collectives, per_device(): lax.psum((owned[0], owned[1], owned[2]), 'rows')  26.2 us
    unnamed x105, local copies, waits for them, and re-layouts  24.9 us
  transfers between devices with their start and end apart: 22, of which 4 were waited for; matrix products, arithmetic and copies ran while one was open for 11% of the time, Pallas kernels for 0%

commit v1 on v0

--- a/solution.py
+++ b/solution.py
@@ -3,6 +3,8 @@
 import jax
 import jax.numpy as jnp
 from jax import lax
+from jax.experimental import pallas as pl
+from jax.experimental.pallas import tpu as pltpu
 from jax.sharding import PartitionSpec as P
 
 C = 320
@@ -11,6 +13,424 @@
 
 EPSILON = 1e-05
 LAYOUT = ("NCHW", "OHWI", "NCHW")
+
+
+MESH = pl.DeviceIdType.MESH
+LANES = 16384
+GLANES = 8192
+BF = jnp.bfloat16
+F32 = jnp.float32
+
+
+def place():
+    d = lax.axis_index("dp")
+    r = lax.axis_index("rows")
+    return (d // 8, (d // 2) % 4, d % 2, r // 4, r % 4)
+
+
+def device_of(zh, y, c, zl, x):
+    return (zh * 8 + y * 2 + c, zl * 4 + x)
+
+
+def remote(src, dst, send, recv, where):
+    return pltpu.make_async_remote_copy(
+        src_ref=src, dst_ref=dst, send_sem=send, recv_sem=recv, device_id=where, device_id_type=MESH
+    )
+
+
+def torus_peers(me):
+    zh, y, c, zl, x = me
+    found = []
+    for k in range(1, 8):
+        s = (y * 2 + c + k) % 8
+        found.append(device_of(zh, s // 2, s % 2, zl, x))
+    for k in range(1, 4):
+        found.append(device_of((zh + k) % 4, y, c, zl, x))
+        found.append(device_of(zh, y, c, zl, (x + k) % 4))
+    return found
+
+
+def greet(peers):
+    barrier = pltpu.get_barrier_semaphore()
+    for where in peers:
+        pl.semaphore_signal(barrier, inc=1, device_id=where, device_id_type=MESH)
+    pl.semaphore_wait(barrier, len(peers))
+
+
+def gather_kernel(
+    src, out, parts, column, wide, own_sem, send1, recv1, send2, recv2, send3, recv3, send4, recv4, send5, recv5
+):
+    me = place()
+    zh, y, c, zl, x = me
+    slot = y * 2 + c
+    greet(torus_peers(me))
+    first = []
+    for k in range(1, 8):
+        s = (slot + k) % 8
+        first.append(
+            remote(src.at[s], parts.at[slot], send1.at[k - 1], recv1.at[k - 1], device_of(zh, s // 2, s % 2, zl, x))
+        )
+        first[-1].start()
+    mine = pltpu.make_async_copy(src.at[slot], parts.at[slot], own_sem.at[0])
+    mine.start()
+    mine.wait()
+    for copy in first:
+        copy.wait_recv()
+    for s in range(8):
+        column[10 * s : 10 * s + 10, :] = parts[s, 0:10, :].astype(F32)
+    home = pl.multiple_of(zh * 80, 80)
+    wide[pl.ds(home, 80), :] = column[...].astype(BF)
+    second = []
+    for k in range(1, 4):
+        second.append(
+            remote(
+                wide.at[pl.ds(home, 80)],
+                wide.at[pl.ds(home, 80)],
+                send2.at[k - 1],
+                recv2.at[k - 1],
+                device_of((zh + k) % 4, y, c, zl, x),
+            )
+        )
+        second[-1].start()
+    for copy in second:
+        copy.wait_recv()
+    spot_a = pl.multiple_of(((y * 2 + c) * 4 + x) * 256, 256)
+    spot_b = pl.multiple_of(8192 + ((x * 2 + c) * 4 + y) * 256, 256)
+    third = []
+    for k in range(1, 4):
+        third.append(
+            remote(
+                wide.at[:, 0:256],
+                out.at[:, pl.ds(spot_a, 256)],
+                send3.at[0, k - 1],
+                recv3.at[0, k - 1],
+                device_of(zh, y, c, zl, (x + k) % 4),
+            )
+        )
+        third.append(
+            remote(
+                wide.at[:, 256:512],
+                out.at[:, pl.ds(spot_b, 256)],
+                send3.at[1, k - 1],
+                recv3.at[1, k - 1],
+                device_of(zh, (y + k) % 4, c, zl, x),
+            )
+        )
+    for copy in third:
+        copy.start()
+    mine_a = pltpu.make_async_copy(wide.at[:, 0:256], out.at[:, pl.ds(spot_a, 256)], own_sem.at[1])
+    mine_b = pltpu.make_async_copy(wide.at[:, 256:512], out.at[:, pl.ds(spot_b, 256)], own_sem.at[2])
+    mine_a.start()
+    mine_b.start()
+    mine_a.wait()
+    mine_b.wait()
+    for copy in third:
+        copy.wait_recv()
+    partner = device_of(zh, y, 1 - c, zl, x)
+    row_a = pl.multiple_of((y * 2 + c) * 1024, 1024)
+    row_b = pl.multiple_of(8192 + (x * 2 + c) * 1024, 1024)
+    fourth = []
+    fifth = []
+    for k in range(1, 4):
+        fourth.append(
+            remote(
+                out.at[:, pl.ds(row_a, 1024)],
+                out.at[:, pl.ds(row_a, 1024)],
+                send4.at[0, k - 1],
+                recv4.at[0, k - 1],
+                device_of(zh, (y + k) % 4, c, zl, x),
+            )
+        )
+        fourth.append(
+            remote(
+                out.at[:, pl.ds(row_b, 1024)],
+                out.at[:, pl.ds(row_b, 1024)],
+                send4.at[1, k - 1],
+                recv4.at[1, k - 1],
+                device_of(zh, y, c, zl, (x + k) % 4),
+            )
+        )
+    for copy in fourth:
+        copy.start()
+    for k in range(4):
+        if k > 0:
+            fourth[2 * k - 2].wait_recv()
+            fourth[2 * k - 1].wait_recv()
+        from_a = pl.multiple_of(((y + 4 - k) % 4 * 2 + c) * 1024, 1024)
+        from_b = pl.multiple_of(8192 + ((x + 4 - k) % 4 * 2 + c) * 1024, 1024)
+        for which, spot in ((0, from_a), (1, from_b)):
+            copy = remote(
+                out.at[:, pl.ds(spot, 1024)],
+                out.at[:, pl.ds(spot, 1024)],
+                send5.at[which, k],
+                recv5.at[which, k],
+                partner,
+            )
+            copy.start()
+            fifth.append(copy)
+    for copy in fifth:
+        copy.wait_recv()
+    for copy in first + second + third + fourth + fifth:
+        copy.wait_send()
+
+
+def gather_weights(shard):
+    x = lax.axis_index("rows") % 4
+    half_a = shard[:, :8192].reshape(10, 4, 2, 4, 256)
+    half_b = shard[:, 8192:].reshape(10, 4, 2, 4, 256)
+    part_a = lax.dynamic_index_in_dim(half_a, x, 3, keepdims=False)
+    part_b = lax.dynamic_index_in_dim(half_b, x, 1, keepdims=False)
+    part_b = jnp.transpose(part_b, (0, 2, 1, 3))
+    both = jnp.concatenate([part_a, part_b], axis=3)
+    both = jnp.transpose(both, (1, 2, 0, 3)).reshape(8, 10, 512)
+    both = jnp.pad(both, ((0, 0), (0, 6), (0, 0)))
+    dma = pltpu.SemaphoreType.DMA
+    return pl.pallas_call(
+        gather_kernel,
+        out_shape=jax.ShapeDtypeStruct((320, LANES), BF),
+        in_specs=[pl.BlockSpec(memory_space=pltpu.VMEM)],
+        out_specs=pl.BlockSpec(memory_space=pl.ANY),
+        scratch_shapes=[
+            pltpu.VMEM((8, 16, 512), BF),
+            pltpu.VMEM((80, 512), F32),
+            pltpu.VMEM((320, 512), BF),
+            dma((3,)),
+            dma((7,)),
+            dma((7,)),
+            dma((3,)),
+            dma((3,)),
+            dma((2, 3)),
+            dma((2, 3)),
+            dma((2, 3)),
+            dma((2, 3)),
+            dma((2, 4)),
+            dma((2, 4)),
+        ],
+        compiler_params=pltpu.CompilerParams(collective_id=0, has_side_effects=True),
+        name="gather_weights",
+    )(both)
+
+
+def reduce_kernel(
+    grads,
+    out,
+    swap,
+    half,
+    far,
+    near,
+    near_in,
+    last,
+    deep,
+    deep_in,
+    plane,
+    plane_in,
+    spread,
+    own_sem,
+    send1,
+    recv1,
+    send2,
+    recv2,
+    send3,
+    recv3,
+    send4,
+    recv4,
+    send5,
+    recv5,
+    send6,
+    recv6,
+    send7,
+    recv7,
+):
+    me = place()
+    zh, y, c, zl, x = me
+    slot = y * 2 + c
+    other_z = device_of(zh, y, c, 1 - zl, x)
+    greet(torus_peers(me) + [other_z])
+    partner = device_of(zh, y, 1 - c, zl, x)
+    theirs = pl.multiple_of((1 - c) * 4096, 4096)
+    ours = pl.multiple_of(c * 4096, 4096)
+    one = remote(grads.at[:, pl.ds(theirs, 4096)], swap, send1.at[0], recv1.at[0], partner)
+    one.start()
+    one.wait_recv()
+
+    @pl.loop(0, 20)
+    def _(i):
+        rows = pl.ds(pl.multiple_of(i * 16, 16), 16)
+        total = grads[rows, pl.ds(ours, 4096)].astype(F32) + swap[rows, :].astype(F32)
+        half[rows, :] = total.astype(BF)
+
+    second = []
+    for k in range(1, 4):
+        ya = (y + k) % 4
+        xb = (x + k) % 4
+        second.append(
+            remote(
+                half.at[:, pl.ds(pl.multiple_of(ya * 512, 512), 512)],
+                far.at[0, k - 1],
+                send2.at[0, k - 1],
+                recv2.at[0, k - 1],
+                device_of(zh, ya, c, zl, x),
+            )
+        )
+        second.append(
+            remote(
+                half.at[:, pl.ds(pl.multiple_of(2048 + xb * 512, 512), 512)],
+                far.at[1, k - 1],
+                send2.at[1, k - 1],
+                recv2.at[1, k - 1],
+                device_of(zh, y, c, zl, xb),
+            )
+        )
+    for copy in second:
+        copy.start()
+    for copy in second:
+        copy.wait_recv()
+    mine_a = pl.ds(pl.multiple_of(y * 512, 512), 512)
+    mine_b = pl.ds(pl.multiple_of(2048 + x * 512, 512), 512)
+
+    @pl.loop(0, 20)
+    def _(i):
+        rows = pl.ds(pl.multiple_of(i * 16, 16), 16)
+        for which, lanes in ((0, mine_a), (1, mine_b)):
+            total = half[rows, lanes].astype(F32)
+            for k in range(3):
+                total = total + far[which, k, rows, :].astype(F32)
+            near[which, rows, :] = total.astype(BF)
+
+    third = []
+    for k in range(1, 4):
+        xa = (x + k) % 4
+        yb = (y + k) % 4
+        third.append(
+            remote(
+                near.at[0, :, pl.ds(pl.multiple_of(xa * 128, 128), 128)],
+                near_in.at[0, k - 1],
+                send3.at[0, k - 1],
+                recv3.at[0, k - 1],
+                device_of(zh, y, c, zl, xa),
+            )
+        )
+        third.append(
+            remote(
+                near.at[1, :, pl.ds(pl.multiple_of(yb * 128, 128), 128)],
+                near_in.at[1, k - 1],
+                send3.at[1, k - 1],
+                recv3.at[1, k - 1],
+                device_of(zh, yb, c, zl, x),
+            )
+        )
+    for copy in third:
+        copy.start()
+    for copy in third:
+        copy.wait_recv()
+    for which, where in ((0, x), (1, y)):
+        total = near[which, :, pl.ds(pl.multiple_of(where * 128, 128), 128)].astype(F32)
+        for k in range(3):
+            total = total + near_in[which, k].astype(F32)
+        deep[:, which * 128 : which * 128 + 128] = total.astype(BF)
+
+    fourth = []
+    for k in range(1, 4):
+        zt = (zh + k) % 4
+        fourth.append(
+            remote(
+                deep.at[pl.ds(pl.multiple_of(zt * 80, 80), 80)],
+                deep_in.at[k - 1],
+                send4.at[k - 1],
+                recv4.at[k - 1],
+                device_of(zt, y, c, zl, x),
+            )
+        )
+        fourth[-1].start()
+    for copy in fourth:
+        copy.wait_recv()
+    total = deep[pl.ds(pl.multiple_of(zh * 80, 80), 80), :].astype(F32)
+    for k in range(3):
+        total = total + deep_in[k].astype(F32)
+    plane[...] = total
+    five = remote(plane, plane_in, send5.at[0], recv5.at[0], other_z)
+    five.start()
+    five.wait_recv()
+    last[...] = plane[...] + plane_in[...]
+    for s in range(8):
+        spread[s, 0:10, :] = last[10 * s : 10 * s + 10, :]
+        spread[s, 10:16, :] = jnp.zeros((6, 256), F32)
+    sixth = []
+    for k in range(1, 8):
+        s = (slot + k) % 8
+        sixth.append(
+            remote(
+                spread.at[s],
+                out.at[x, slot],
+                send6.at[k - 1],
+                recv6.at[k - 1],
+                device_of(zh, s // 2, s % 2, zl, x),
+            )
+        )
+        sixth[-1].start()
+    mine = pltpu.make_async_copy(spread.at[slot], out.at[x, slot], own_sem.at[0])
+    mine.start()
+    mine.wait()
+    for copy in sixth:
+        copy.wait_recv()
+    seventh = []
+    for k in range(1, 4):
+        seventh.append(
+            remote(out.at[x], out.at[x], send7.at[k - 1], recv7.at[k - 1], device_of(zh, y, c, zl, (x + k) % 4))
+        )
+        seventh[-1].start()
+    for copy in seventh:
+        copy.wait_recv()
+    for copy in [one] + second + third + fourth + [five] + sixth + seventh:
+        copy.wait_send()
+
+
+def reduce_grads(grads):
+    dma = pltpu.SemaphoreType.DMA
+    pieces = pl.pallas_call(
+        reduce_kernel,
+        out_shape=jax.ShapeDtypeStruct((4, 8, 16, 256), F32),
+        in_specs=[pl.BlockSpec(memory_space=pltpu.VMEM)],
+        out_specs=pl.BlockSpec(memory_space=pltpu.VMEM),
+        scratch_shapes=[
+            pltpu.VMEM((320, 4096), BF),
+            pltpu.VMEM((320, 4096), BF),
+            pltpu.VMEM((2, 3, 320, 512), BF),
+            pltpu.VMEM((2, 320, 512), BF),
+            pltpu.VMEM((2, 3, 320, 128), BF),
+            pltpu.VMEM((80, 256), F32),
+            pltpu.VMEM((320, 256), BF),
+            pltpu.VMEM((3, 80, 256), BF),
+            pltpu.VMEM((80, 256), F32),
+            pltpu.VMEM((80, 256), F32),
+            pltpu.VMEM((8, 16, 256), F32),
+            dma((1,)),
+            dma((1,)),
+            dma((1,)),
+            dma((2, 3)),
+            dma((2, 3)),
+            dma((2, 3)),
+            dma((2, 3)),
+            dma((3,)),
+            dma((3,)),
+            dma((1,)),
+            dma((1,)),
+            dma((7,)),
+            dma((7,)),
+            dma((3,)),
+            dma((3,)),
+        ],
+        compiler_params=pltpu.CompilerParams(collective_id=1, has_side_effects=True),
+        name="reduce_grads",
+    )(grads)
+    return spread_back(pieces)
+
+
+def spread_back(pieces):
+    pieces = pieces[:, :, :10, :].reshape(4, 4, 2, 10, 2, 128)
+    part_a = jnp.transpose(pieces[:, :, :, :, 0], (3, 2, 1, 0, 4)).reshape(10, 2, 2048)
+    part_b = jnp.transpose(pieces[:, :, :, :, 1], (3, 2, 0, 1, 4)).reshape(10, 2, 2048)
+    return jnp.concatenate([part_a, part_b], axis=2).reshape(10, GLANES)
 
 
 def extended(x, sides, width):
@@ -165,14 +585,28 @@
     dec_shortcut,
     zero_conv,
 ):
-    ctl_one, ctl_two, dec_one, dec_two, dec_short, zero_full = (
-        lax.all_gather(ctl_conv_one, "dp", axis=0, tiled=True),
-        lax.all_gather(ctl_conv_two, "dp", axis=0, tiled=True),
-        lax.all_gather(dec_conv_one, "dp", axis=0, tiled=True),
-        lax.all_gather(dec_conv_two, "dp", axis=0, tiled=True),
-        lax.all_gather(dec_shortcut, "dp", axis=0, tiled=True),
-        lax.all_gather(zero_conv, "dp", axis=0, tiled=True),
-    )
+    def flat(kernel, width):
+        kernel = kernel.reshape(kernel.shape[0], -1)
+        return jnp.pad(kernel, ((0, 0), (0, width - kernel.shape[1])))
+
+    shard = jnp.concatenate(
+        [
+            flat(ctl_conv_one, 2944),
+            flat(ctl_conv_two, 2944),
+            flat(zero_conv, 384),
+            flat(dec_shortcut, 640),
+            flat(dec_conv_two, 2944),
+            flat(dec_conv_one, LANES - 9856),
+        ],
+        axis=1,
+    )
+    weights = gather_weights(shard)
+    ctl_one = weights[:, :2880].reshape(C, 3, 3, C)
+    ctl_two = weights[:, 2944:5824].reshape(C, 3, 3, C)
+    zero_full = weights[:, 5888:6208]
+    dec_short = weights[:, 6272:6912]
+    dec_two = weights[:, 6912:9792].reshape(C, 3, 3, C)
+    dec_one = weights[:, 9856:15616].reshape(C, 3, 3, 2 * C)
     half_width = C // 2
     frequency = jnp.exp(-math.log(10000.0) * jnp.arange(half_width, dtype=jnp.float32) / half_width)
     angles = timesteps.astype(jnp.float32)[:, None] * frequency[None, :]
@@ -220,13 +654,20 @@
         ctl_second_grad * silu_slope(ctl_parts[3]), ctl_parts[3], ctl_parts[4]
     ).astype(jnp.bfloat16)
     one_local = kernel_grad(ctl_inner_grad, ctl_parts[2])
-    owned = (
-        lax.psum_scatter(one_local, "dp", scatter_dimension=0, tiled=True),
-        lax.psum_scatter(two_local, "dp", scatter_dimension=0, tiled=True),
-        lax.psum_scatter(zero_local, "dp", scatter_dimension=0, tiled=True),
-    )
-    one_grad, two_grad, zero_grad = lax.psum((owned[0], owned[1], owned[2]), "rows")
-    return (one_grad, two_grad, zero_grad)
+    grads = jnp.concatenate(
+        [
+            flat(one_local.astype(BF), 2944),
+            flat(two_local.astype(BF), 2944),
+            flat(zero_local.astype(BF), GLANES - 5888),
+        ],
+        axis=1,
+    )
+    owned = reduce_grads(grads)
+    return (
+        owned[:, :2880].reshape(10, 3, 3, C),
+        owned[:, 2944:5824].reshape(10, 3, 3, C),
+        owned[:, 5888:6208],
+    )
 
 
 def solution(mesh):

time: 879 us -> 540 us (0.61)
  waiting for transfers between devices: 418 us -> 7.37 us
  Pallas kernels: 0 us -> 162 us
  blocking collectives: 245 us -> 111 us
  matrix products: 46.1 us -> 96.2 us
  between operations: 17.4 us -> 2.91 us
  starting transfers between devices: 35.8 us -> 45.2 us
    unnamed x7 -> x0, waiting for transfers between devices: 366 us -> none
    pallas_call x0 -> x2, Pallas kernels: none -> 162 us  [the longest x1 90.8 us: reduce_grads(): pl.pallas_call(reduce_kernel, out_shape=jax.ShapeDtypeStruct((4, 8, 16, 2...]
    all_gather x2 -> x0, blocking collectives: 97.3 us -> none  [the longest x1 54 us: per_device(): lax.all_gather(zero_conv, 'dp', axis=0, tiled=True)]
    conv_general_dilated x8, matrix products: 23 us -> 75.3 us  [conv_rows(): lax.conv_general_dilated(padded, weight, (1, 1), ((0, 0), (1, 1)), dimens...]
    psum x1 -> x0, waiting for transfers between devices: 47.1 us -> none  [per_device(): lax.psum((owned[0], owned[1], owned[2]), 'rows')]
    slice x3 -> x12, local copies, waits for them, and re-layouts: 1.74 us -> 28.7 us  [the longest x2 10.4 us: per_device(): dec_one = weights[:, 9856:15616].reshape(C, 3, 3, 2 * C)]
    psum x1 -> x0, blocking collectives: 26.2 us -> none  [per_device(): lax.psum((owned[0], owned[1], owned[2]), 'rows')]
    scatter-add x4 -> x0, local copies, waits for them, and re-layouts: 12.4 us -> none  [the longest x2 6.8 us: input_grad(): result = result.at[:, :, :1].add(from_prev)]
  transfers between devices with their start and end apart: 22 -> 16, of which waited for: 4 -> 2; matrix products, arithmetic and copies ran while one was open for 11% -> 18% of each run, Pallas kernels for 0% -> 0%
where the time goes in v1:
time: 540 us; the launch traced here: 534 us
  Pallas kernels  162 us (30%)
  blocking collectives  111 us (21%)
  matrix products  96.2 us (18%)
  local copies, waits for them, and re-layouts  82.7 us (15%)
  starting transfers between devices  45.2 us (8%)
  other arithmetic  25.9 us (5%)
  waiting for transfers between devices  7.37 us (1%)
    pallas_call x1, Pallas kernels, reduce_grads(): pl.pallas_call(reduce_kernel, out_shape=jax.ShapeDtypeStruct((4, 8, 16, 2...  90.8 us
    conv_general_dilated x8, matrix products, conv_rows(): lax.conv_general_dilated(padded, weight, (1, 1), ((0, 0), (1, 1)), dimens...  75.3 us
    pallas_call x1, Pallas kernels, gather_weights(): pl.pallas_call(gather_kernel, out_shape=jax.ShapeDtypeStruct((320, LANES)...  71.5 us
    psum x4, blocking collectives, group_norm(): lax.psum((jnp.sum(grouped, axis=(2, 3, 4)), jnp.sum(grouped * grouped, ax...  64.7 us
    psum x3, blocking collectives, norm_back(): lax.psum((jnp.sum(grouped, axis=(2, 3, 4)), jnp.sum(grouped * normed_grou...  46.6 us
    ppermute x5, starting transfers between devices, extended(): before = lax.ppermute(last, axis, up)  17.4 us
    ppermute x5, starting transfers between devices, extended(): after = lax.ppermute(first, axis, down)  15.2 us
    unnamed x65, local copies, waits for them, and re-layouts  14 us
  transfers between devices with their start and end apart: 16, of which 2 were waited for; matrix products, arithmetic and copies ran while one was open for 18% of the time, Pallas kernels for 0%

profile of v1, /device:TPU:1, one launch (start us, length us, event | category | flops | bytes accessed | tf_op | source)
XLA Modules:
  0.0 533.8 jit_solution(16453717232650153340)
XLA Ops:
  6.7 71.5 %gather_weights.1 = bf16[320,16384]{1,0:T(8,128)(2,1)} custom-call(bf16[8,16,512]{2,1,0:T(8,128)(2,1)} %pad.61.src), custom_call_target="tpu_custom_call" | custom-call | tf_op jit(solution)/shard_map/gather_weights/pallas_call | solution.py:188
  78.2 5.2 fusion.155
  83.4 4.0 copy.236
  89.2 12.7 %fusion.171 = f32[1,320,4,128]{1,0,3,2:T(1,128)S(1)} fusion(bf16[1,320,2,128]{1,0,3,2:T(2,128)(2,1)S(1)} %copy.237, bf16[320,3,3,320]{0,3,2,1:T(8,128)(2,1)} %bitcast.403), kind=kOutput, calls=%fused_computation.289 | convolution fusion | flops 469401600 | bytes 2662400 | tf_op jit(solution)/shard_map/conv_general_dilated | solution.py:456
  110.7 15.8 %all-reduce.17 = (f32[1,32]{1,0:T(1,128)S(1)}, f32[1,32]{1,0:T(1,128)S(1)}, f32[1,32]{1,0:T(1,128)S(1)}, f32[1,32]{1,0:T(1,128)S(1)}) all-reduce(f32[1,32]{1,0:T(1,128)S(1)} %bitcast.419, f32[1,32]{1,0:T(1,128)S(1)} %bitcast.417, f32[1,32]{1,0:T(1,128)S(1)} %bitcast.420, ...), channel_id=1, replica_groups=mesh['dp'=32,'rows'=8] {'rows'}, use_global_device_ids=true, to_apply=%region_17.18 | all-reduce | flops 128 | bytes 1024 | tf_op jit(solution)/shard_map/psum | solution.py:488
  132.2 4.8 collective-permute-start.2
  137.0 4.1 slice.365
  142.4 4.0 copy.222
  151.6 4.0 copy.229
  156.3 6.2 %copy.233 = bf16[320,5760]{0,1:T(8,128)(2,1)} copy(bf16[320,5760]{1,0:T(8,128)(2,1)} %slice.365) | data formatting | bytes 7372800 | tf_op jit(solution)/shard_map/slice | solution.py:609
  168.1 6.5 %fusion.166 = f32[1,320,2,128]{1,0,3,2:T(1,128)} fusion(bf16[1,320,4,128]{1,0,3,2:T(2,128)(2,1)} %copy.223, bf16[320,3,3,320]{0,3,2,1:T(8,128)(2,1)} %bitcast.402), kind=kOutput, calls=%fused_computation.284 | convolution fusion | flops 469401600 | bytes 2498560 | tf_op jit(solution)/shard_map/conv_general_dilated | solution.py:456
  183.0 7.9 %fusion.167 = f32[1,320,2,128]{1,0,3,2:T(1,128)} fusion(bf16[1,320,4,128]{1,0,3,2:T(2,128)(2,1)} %copy.225, bf16[320,3,3,320]{3,0,2,1:T(8,128)(2,1)S(1)} %copy-done), kind=kOutput, calls=%fused_computation.285 | convolution fusion | flops 469401600 | bytes 2498560 | tf_op jit(solution)/shard_map/conv_general_dilated | solution.py:456
  192.8 15.5 %all-reduce.16 = (f32[1,32]{1,0:T(1,128)S(1)}, f32[1,32]{1,0:T(1,128)S(1)}, f32[1,32]{1,0:T(1,128)S(1)}, f32[1,32]{1,0:T(1,128)S(1)}) all-reduce(f32[1,32]{1,0:T(1,128)S(1)} %bitcast.421, f32[1,32]{1,0:T(1,128)S(1)} %bitcast.418, f32[1,32]{1,0:T(1,128)S(1)} %bitcast.414, ...), channel_id=1, replica_groups=mesh['dp'=32,'rows'=8] {'rows'}, use_global_device_ids=true, to_apply=%region_23.24 | all-reduce | flops 128 | bytes 1024 | tf_op jit(solution)/shard_map/psum | solution.py:488
  211.7 10.0 %collective-permute-start.7 = (bf16[1,320,1,128]{3,1,2,0:T(8,128)(2,1)S(1)}, bf16[1,320,1,128]{3,1,2,0:T(8,128)(2,1)S(1)}, u32[]{:S(2)}, u32[]{:S(2)}) collective-permute-start(bf16[1,320,1,128]{3,1,2,0:T(8,128)(2,1)S(1)} %get-tuple-element.137), channel_id=1, source_target_pairs={{1,0},{2,1},{3,2},{4,3},{5,4},{6,5},{7,6},{9,8},{10,9},{11,10},{12... | collective-permute-start | bytes 245768 | tf_op jit(solution)/shard_map/ppermute | solution.py:444
  222.4 4.5 collective-permute-start.4
  230.1 5.5 %fusion.169 = f32[1,320,2,128]{1,0,3,2:T(1,128)S(1)} fusion(bf16[1,320,4,128]{1,0,3,2:T(2,128)(2,1)S(1)} %copy.230, bf16[320,3,3,320]{0,3,2,1:T(8,128)(2,1)} %bitcast.400), kind=kOutput, calls=%fused_computation.287 | convolution fusion | flops 469401600 | bytes 2498560 | tf_op jit(solution)/shard_map/conv_general_dilated | solution.py:456
  237.9 7.9 %fusion.168 = f32[1,320,2,128]{1,0,3,2:T(1,128)S(1)} fusion(bf16[1,320,4,128]{1,0,3,2:T(2,128)(2,1)} %copy.227, bf16[320,3,3,320]{3,0,2,1:T(8,128)(2,1)} %param.39), kind=kOutput, calls=%fused_computation.286 | convolution fusion | flops 469401600 | bytes 2498560 | tf_op jit(solution)/shard_map/conv_general_dilated | solution.py:456
  248.2 17.3 %all-reduce.15 = (f32[1,32]{1,0:T(1,128)S(1)}, f32[1,32]{1,0:T(1,128)S(1)}) all-reduce(f32[1,32]{1,0:T(1,128)S(1)} %bitcast.422, f32[1,32]{1,0:T(1,128)S(1)} %bitcast.427), channel_id=1, replica_groups=mesh['dp'=32,'rows'=8] {'rows'}, use_global_device_ids=true, to_apply=%region_26.27 | all-reduce | flops 64 | bytes 512 | tf_op jit(solution)/shard_map/psum | solution.py:488
  266.2 3.4 collective-permute-start.8
  272.8 3.5 collective-permute-done.9
  277.3 3.7 copy.234
  281.0 9.4 %fusion.170 = f32[1,320,2,128]{1,0,3,2:T(1,128)S(1)} fusion(bf16[1,640,4,128]{1,0,3,2:T(2,128)(2,1)} %copy.234, bf16[320,3,3,640]{0,3,2,1:T(8,128)(2,1)} %bitcast.398), kind=kOutput, calls=%fused_computation.288 | convolution fusion | flops 938803200 | bytes 4669440 | tf_op jit(solution)/shard_map/conv_general_dilated | solution.py:456
  291.5 16.0 %all-reduce.14 = (f32[1,32]{1,0:T(1,128)S(1)}, f32[1,32]{1,0:T(1,128)S(1)}) all-reduce(f32[1,32]{1,0:T(1,128)S(1)} %bitcast.428, f32[1,32]{1,0:T(1,128)S(1)} %bitcast.423), channel_id=1, replica_groups=mesh['dp'=32,'rows'=8] {'rows'}, use_global_device_ids=true, to_apply=%region_35.36 | all-reduce | flops 64 | bytes 512 | tf_op jit(solution)/shard_map/psum | solution.py:488
  308.7 13.0 %all-reduce.13 = (f32[1,32]{1,0:T(1,128)S(1)}, f32[1,32]{1,0:T(1,128)S(1)}) all-reduce(f32[1,32]{1,0:T(1,128)S(1)} %bitcast.429, f32[1,32]{1,0:T(1,128)S(1)} %bitcast.425), channel_id=1, replica_groups=mesh['dp'=32,'rows'=8] {'rows'}, use_global_device_ids=true, to_apply=%region_41.42 | all-reduce | flops 64 | bytes 512 | tf_op jit(solution)/shard_map/psum | solution.py:507
  322.7 12.7 %fusion.6 = f32[1,320,4,128]{1,0,3,2:T(1,128)S(1)} fusion(bf16[1,320,2,128]{1,0,3,2:T(2,128)(2,1)S(1)} %copy.243, bf16[320,3,3,640]{0,3,2,1:T(8,128)(2,1)} %bitcast.399), kind=kOutput, calls=%fused_computation.12 | convolution fusion | flops 469401600 | bytes 3031040 | tf_op jit(solution)/shard_map/conv_general_dilated | solution.py:456
  337.6 4.2 collective-permute-start.12
  346.1 3.8 collective-permute-done.13
  350.7 16.1 %all-reduce.12 = (f32[1,16]{1,0:T(1,128)S(1)}, f32[1,16]{1,0:T(1,128)S(1)}) all-reduce(f32[1,16]{1,0:T(1,128)S(1)} %bitcast.430, f32[1,16]{1,0:T(1,128)S(1)} %bitcast.426), channel_id=1, replica_groups=mesh['dp'=32,'rows'=8] {'rows'}, use_global_device_ids=true, to_apply=%region_47.48 | all-reduce | flops 32 | bytes 256 | tf_op jit(solution)/shard_map/psum | solution.py:507
  370.4 12.7 %fusion.172 = f32[1,320,4,128]{1,0,3,2:T(1,128)S(1)} fusion(bf16[1,2,128,320]{3,0,2,1:T(2,128)(2,1)S(1)} %copy.251, bf16[320,3,3,320]{0,3,2,1:T(8,128)(2,1)} %bitcast.401), kind=kOutput, calls=%fused_computation.290 | convolution fusion | flops 469401600 | bytes 2662400 | tf_op jit(solution)/shard_map/conv_general_dilated | solution.py:456
  406.7 17.5 %all-reduce.11 = (f32[1,32]{1,0:T(1,128)S(1)}, f32[1,32]{1,0:T(1,128)S(1)}) all-reduce(f32[1,32]{1,0:T(1,128)S(1)} %bitcast.431, f32[1,32]{1,0:T(1,128)S(1)} %bitcast.424), channel_id=1, replica_groups=mesh['dp'=32,'rows'=8] {'rows'}, use_global_device_ids=true, to_apply=%region_53.54 | all-reduce | flops 64 | bytes 512 | tf_op jit(solution)/shard_map/psum | solution.py:507
  432.8 5.0 fusion.5.grads
  437.8 90.8 %reduce_grads.1 = f32[4,8,16,256]{3,2,1,0:T(8,128)} custom-call(bf16[320,8192]{1,0:T(8,128)(2,1)} %fusion.5.grads), custom_call_target="tpu_custom_call" | custom-call | tf_op jit(solution)/shard_map/reduce_grads/pallas_call | solution.py:390
  (297 shorter events, 111.5 us)
Async XLA Ops:
  0.6 182.3 %copy-start = (bf16[320,3,3,320]{3,0,2,1:T(8,128)(2,1)S(1)}, bf16[320,3,3,320]{3,0,2,1:T(8,128)(2,1)}, u32[]{:S(2)}) copy-start(bf16[320,3,3,320]{3,0,2,1:T(8,128)(2,1)} %param.38) | copy-start | bytes 5529604
  0.6 5.1 copy-start.21
  83.4 4.0 copy-start.20
  89.2 19.3 %copy-start.8 = (bf16[1,320,2,128]{3,2,1,0:T(2,128)(2,1)S(1)}, bf16[1,320,2,128]{3,2,1,0:T(2,128)(2,1)}, u32[]{:S(2)}) copy-start(bf16[1,320,2,128]{3,2,1,0:T(2,128)(2,1)} %param.29) | copy-start | bytes 491524
  104.1 166.8 %collective-permute-start.10 = (f32[1,320,1,128]{3,1,2,0:T(8,128)}, f32[1,320,1,128]{3,1,2,0:T(8,128)}, u32[]{:S(2)}, u32[]{:S(2)}) collective-permute-start(f32[1,320,1,128]{3,1,2,0:T(8,128)} %copy.270), channel_id=1, source_target_pairs={{0,1},{1,2},{2,3},{3,4},{4,5},{5,6},{6,7},{8,9},{9,10},{10,11},{11... | collective-permute-start | bytes 491528 | tf_op jit(solution)/shard_map/ppermute | solution.py:452
  107.2 164.6 %collective-permute-start.11 = (f32[1,320,1,128]{3,1,2,0:T(8,128)}, f32[1,320,1,128]{3,1,2,0:T(8,128)}, u32[]{:S(2)}, u32[]{:S(2)}) collective-permute-start(f32[1,320,1,128]{3,1,2,0:T(8,128)} %copy.271), channel_id=1, source_target_pairs={{1,0},{2,1},{3,2},{4,3},{5,4},{6,5},{7,6},{9,8},{10,9},{11,10},{12... | collective-permute-start | bytes 491528 | tf_op jit(solution)/shard_map/ppermute | solution.py:452
  127.7 36.3 %collective-permute-start = (bf16[1,320,1,128]{3,1,2,0:T(8,128)(2,1)}, bf16[1,320,1,128]{3,1,2,0:T(8,128)(2,1)}, u32[]{:S(2)}, u32[]{:S(2)}) collective-permute-start(bf16[1,320,1,128]{3,1,2,0:T(8,128)(2,1)} %get-tuple-element.140), channel_id=1, source_target_pairs={{0,1},{1,2},{2,3},{3,4},{4,5},{5,6},{6,7},{8,9},{9,10},{10,11},{11... | collective-permute-start | bytes 245768 | tf_op jit(solution)/shard_map/ppermute | solution.py:443
  129.6 35.7 %collective-permute-start.1 = (bf16[1,320,1,128]{3,1,2,0:T(8,128)(2,1)}, bf16[1,320,1,128]{3,1,2,0:T(8,128)(2,1)}, u32[]{:S(2)}, u32[]{:S(2)}) collective-permute-start(bf16[1,320,1,128]{3,1,2,0:T(8,128)(2,1)} %get-tuple-element.141), channel_id=1, source_target_pairs={{1,0},{2,1},{3,2},{4,3},{5,4},{6,5},{7,6},{9,8},{10,9},{11,10},{12... | collective-permute-start | bytes 245768 | tf_op jit(solution)/shard_map/ppermute | solution.py:444
  131.5 9.7 %copy-start.6 = (bf16[1,320,2,128]{3,1,2,0:T(8,128)(2,1)}, bf16[1,320,2,128]{3,1,2,0:T(8,128)(2,1)S(1)}, u32[]{:S(2)}) copy-start(bf16[1,320,2,128]{3,1,2,0:T(8,128)(2,1)S(1)} %fusion.69) | copy-start | bytes 491524
  132.2 46.1 %collective-permute-start.2 = (bf16[1,320,1,128]{3,1,2,0:T(8,128)(2,1)}, bf16[1,320,1,128]{3,1,2,0:T(8,128)(2,1)}, u32[]{:S(2)}, u32[]{:S(2)}) collective-permute-start(bf16[1,320,1,128]{3,1,2,0:T(8,128)(2,1)} %get-tuple-element.142), channel_id=1, source_target_pairs={{0,1},{1,2},{2,3},{3,4},{4,5},{5,6},{6,7},{8,9},{9,10},{10,11},{11... | collective-permute-start | bytes 245768 | tf_op jit(solution)/shard_map/ppermute | solution.py:443
  137.0 5.0 slice-start.1
  151.5 4.0 copy-start.19
  164.0 14.3 %collective-permute-start.3 = (bf16[1,320,1,128]{3,1,2,0:T(8,128)(2,1)}, bf16[1,320,1,128]{3,1,2,0:T(8,128)(2,1)}, u32[]{:S(2)}, u32[]{:S(2)}) collective-permute-start(bf16[1,320,1,128]{3,1,2,0:T(8,128)(2,1)} %get-tuple-element.143), channel_id=1, source_target_pairs={{1,0},{2,1},{3,2},{4,3},{5,4},{6,5},{7,6},{9,8},{10,9},{11,10},{12... | collective-permute-start | bytes 245768 | tf_op jit(solution)/shard_map/ppermute | solution.py:444
  183.0 9.8 %copy-start.22 = (f32[32]{0:T(128)S(1)}, f32[32]{0:T(128)}, u32[]{:S(2)}) copy-start(f32[32]{0:T(128)} %reduce_sum.247) | copy-start | bytes 388
  209.0 17.9 %collective-permute-start.6 = (bf16[1,320,1,128]{3,1,2,0:T(8,128)(2,1)S(1)}, bf16[1,320,1,128]{3,1,2,0:T(8,128)(2,1)S(1)}, u32[]{:S(2)}, u32[]{:S(2)}) collective-permute-start(bf16[1,320,1,128]{3,1,2,0:T(8,128)(2,1)S(1)} %get-tuple-element.136), channel_id=1, source_target_pairs={{0,1},{1,2},{2,3},{3,4},{4,5},{5,6},{6,7},{8,9},{9,10},{10,11},{11... | collective-permute-start | bytes 245768 | tf_op jit(solution)/shard_map/ppermute | solution.py:443
  211.7 16.5 %collective-permute-start.7 = (bf16[1,320,1,128]{3,1,2,0:T(8,128)(2,1)S(1)}, bf16[1,320,1,128]{3,1,2,0:T(8,128)(2,1)S(1)}, u32[]{:S(2)}, u32[]{:S(2)}) collective-permute-start(bf16[1,320,1,128]{3,1,2,0:T(8,128)(2,1)S(1)} %get-tuple-element.137), channel_id=1, source_target_pairs={{1,0},{2,1},{3,2},{4,3},{5,4},{6,5},{7,6},{9,8},{10,9},{11,10},{12... | collective-permute-start | bytes 245768 | tf_op jit(solution)/shard_map/ppermute | solution.py:444
  222.4 13.6 %collective-permute-start.4 = (bf16[1,320,1,128]{3,1,2,0:T(8,128)(2,1)S(1)}, bf16[1,320,1,128]{3,1,2,0:T(8,128)(2,1)S(1)}, u32[]{:S(2)}, u32[]{:S(2)}) collective-permute-start(bf16[1,320,1,128]{3,1,2,0:T(8,128)(2,1)S(1)} %get-tuple-element.138), channel_id=1, source_target_pairs={{0,1},{1,2},{2,3},{3,4},{4,5},{5,6},{6,7},{8,9},{9,10},{10,11},{11... | collective-permute-start | bytes 245768 | tf_op jit(solution)/shard_map/ppermute | solution.py:443
  226.9 9.0 %collective-permute-start.5 = (bf16[1,320,1,128]{3,1,2,0:T(8,128)(2,1)S(1)}, bf16[1,320,1,128]{3,1,2,0:T(8,128)(2,1)S(1)}, u32[]{:S(2)}, u32[]{:S(2)}) collective-permute-start(bf16[1,320,1,128]{3,1,2,0:T(8,128)(2,1)S(1)} %get-tuple-element.139), channel_id=1, source_target_pairs={{1,0},{2,1},{3,2},{4,3},{5,4},{6,5},{7,6},{9,8},{10,9},{11,10},{12... | collective-permute-start | bytes 245768 | tf_op jit(solution)/shard_map/ppermute | solution.py:444
  235.9 10.3 %copy-start.2 = (f32[1,320,2,128]{3,1,2,0:T(8,128)}, f32[1,320,2,128]{3,1,2,0:T(8,128)S(1)}, u32[]{:S(2)}) copy-start(f32[1,320,2,128]{3,1,2,0:T(8,128)S(1)} %copy.231) | copy-start | bytes 983044
  237.9 8.4 %copy-start.9 = (bf16[1,320,2,128]{3,2,1,0:T(2,128)(2,1)S(1)}, bf16[1,320,2,128]{3,2,1,0:T(2,128)(2,1)}, u32[]{:S(2)}) copy-start(bf16[1,320,2,128]{3,2,1,0:T(2,128)(2,1)} %param.29) | copy-start | bytes 491524
  245.9 25.0 %copy-start.14 = (f32[1,320,1,128]{3,1,2,0:T(8,128)S(1)}, f32[1,320,1,128]{3,1,2,0:T(8,128)}, u32[]{:S(2)}) copy-start(f32[1,320,1,128]{3,1,2,0:T(8,128)} %copy.269) | copy-start | bytes 491524
  266.2 6.6 %collective-permute-start.8 = (bf16[1,640,1,128]{3,1,2,0:T(8,128)(2,1)S(1)}, bf16[1,640,1,128]{3,1,2,0:T(8,128)(2,1)S(1)}, u32[]{:S(2)}, u32[]{:S(2)}) collective-permute-start(bf16[1,640,1,128]{3,1,2,0:T(8,128)(2,1)S(1)} %get-tuple-element.132), channel_id=1, source_target_pairs={{0,1},{1,2},{2,3},{3,4},{4,5},{5,6},{6,7},{8,9},{9,10},{10,11},{11... | collective-permute-start | bytes 491528 | tf_op jit(solution)/shard_map/ppermute | solution.py:443
  269.6 6.8 %collective-permute-start.9 = (bf16[1,640,1,128]{3,1,2,0:T(8,128)(2,1)S(1)}, bf16[1,640,1,128]{3,1,2,0:T(8,128)(2,1)S(1)}, u32[]{:S(2)}, u32[]{:S(2)}) collective-permute-start(bf16[1,640,1,128]{3,1,2,0:T(8,128)(2,1)S(1)} %get-tuple-element.133), channel_id=1, source_target_pairs={{1,0},{2,1},{3,2},{4,3},{5,4},{6,5},{7,6},{9,8},{10,9},{11,10},{12... | collective-permute-start | bytes 491528 | tf_op jit(solution)/shard_map/ppermute | solution.py:444
  337.6 29.6 %copy-start.13 = (bf16[320,2,128]{2,1,0:T(2,128)(2,1)S(1)}, bf16[320,2,128]{2,1,0:T(2,128)(2,1)}, u32[]{:S(2)}) copy-start(bf16[320,2,128]{2,1,0:T(2,128)(2,1)} %get-tuple-element.134) | copy-start | bytes 491524
  337.6 7.6 %collective-permute-start.12 = (f32[1,320,1,128]{3,1,2,0:T(8,128)}, f32[1,320,1,128]{3,1,2,0:T(8,128)}, u32[]{:S(2)}, u32[]{:S(2)}) collective-permute-start(f32[1,320,1,128]{3,1,2,0:T(8,128)} %copy.275), channel_id=1, source_target_pairs={{0,1},{1,2},{2,3},{3,4},{4,5},{5,6},{6,7},{8,9},{9,10},{10,11},{11... | collective-permute-start | bytes 491528 | tf_op jit(solution)/shard_map/ppermute | solution.py:452
  343.9 6.1 %collective-permute-start.13 = (f32[1,320,1,128]{3,1,2,0:T(8,128)S(1)}, f32[1,320,1,128]{3,1,2,0:T(8,128)S(1)}, u32[]{:S(2)}, u32[]{:S(2)}) collective-permute-start(f32[1,320,1,128]{3,1,2,0:T(8,128)S(1)} %copy.276), channel_id=1, source_target_pairs={{1,0},{2,1},{3,2},{4,3},{5,4},{6,5},{7,6},{9,8},{10,9},{11,10},{12... | collective-permute-start | bytes 491528 | tf_op jit(solution)/shard_map/ppermute | solution.py:452
  386.6 10.2 %copy-start.18 = (bf16[1,320,1,128]{3,1,2,0:T(8,128)(2,1)S(1)}, bf16[1,320,1,128]{3,1,2,0:T(8,128)(2,1)}, u32[]{:S(2)}) copy-start(bf16[1,320,1,128]{3,1,2,0:T(8,128)(2,1)} %copy-done.17) | copy-start | bytes 245764
  387.9 5.5 %slice-start = ((f32[1,320,4,128]{1,0,3,2:T(1,128)}), f32[1,320,2,128]{1,0,3,2:T(1,128)S(1)}, s32[]{:S(2)}) async-start(f32[1,320,4,128]{1,0,3,2:T(1,128)} %copy-done.3), calls=%async_computation | async-start | bytes 786432 | tf_op jit(solution)/shard_map/slice | solution.py:530
  388.5 9.8 %copy-start.12 = (bf16[320,1,320]{0,2,1:T(8,128)(2,1)S(1)}, bf16[320,1,320]{0,2,1:T(8,128)(2,1)}, u32[]{:S(2)}) copy-start(bf16[320,1,320]{0,2,1:T(8,128)(2,1)} %fusion.34) | copy-start | bytes 614404
  390.3 13.6 %collective-permute-start.14 = (f32[1,320,1,128]{3,1,2,0:T(8,128)}, f32[1,320,1,128]{3,1,2,0:T(8,128)}, u32[]{:S(2)}, u32[]{:S(2)}) collective-permute-start(f32[1,320,1,128]{3,1,2,0:T(8,128)} %copy.279), channel_id=1, source_target_pairs={{0,1},{1,2},{2,3},{3,4},{4,5},{5,6},{6,7},{8,9},{9,10},{10,11},{11... | collective-permute-start | bytes 491528 | tf_op jit(solution)/shard_map/ppermute | solution.py:452
  393.4 5.0 copy-start.16
  395.5 9.4 %collective-permute-start.15 = (f32[1,320,1,128]{3,1,2,0:T(8,128)}, f32[1,320,1,128]{3,1,2,0:T(8,128)}, u32[]{:S(2)}, u32[]{:S(2)}) collective-permute-start(f32[1,320,1,128]{3,1,2,0:T(8,128)} %copy.280), channel_id=1, source_target_pairs={{1,0},{2,1},{3,2},{4,3},{5,4},{6,5},{7,6},{9,8},{10,9},{11,10},{12... | collective-permute-start | bytes 491528 | tf_op jit(solution)/shard_map/ppermute | solution.py:452
  (9 other events, 16.1 us)

commit v2 on v1

--- a/solution.py
+++ b/solution.py
@@ -8,12 +8,7 @@
 from jax.sharding import PartitionSpec as P
 
 C = 320
-GROUPS = 32
-
-
 EPSILON = 1e-05
-LAYOUT = ("NCHW", "OHWI", "NCHW")
-
 
 MESH = pl.DeviceIdType.MESH
 LANES = 16384
@@ -433,137 +428,571 @@
     return jnp.concatenate([part_a, part_b], axis=2).reshape(10, GLANES)
 
 
-def extended(x, sides, width):
-    for axis, dim in sides:
-        peers, length = (lax.axis_size(axis), x.shape[dim])
-        up = [(i, (i + 1) % peers) for i in range(peers - 1)]
-        down = [(j, i) for i, j in up]
-        last = lax.slice_in_dim(x, length - width, length, axis=dim)
-        first = lax.slice_in_dim(x, 0, width, axis=dim)
-        before = lax.ppermute(last, axis, up)
-        after = lax.ppermute(first, axis, down)
-        x = jnp.concatenate([before, x, after], axis=dim)
-    return x
-
-
-def shifted(value, axis, steps):
-    count = lax.axis_size(axis)
-    first, last = (max(0, -steps), min(count, count - steps))
-    return lax.ppermute(value, axis, [(source, source + steps) for source in range(first, last)])
-
-
-def conv_rows(padded, weight):
-    return lax.conv_general_dilated(
-        padded,
-        weight,
-        (1, 1),
-        ((0, 0), (1, 1)),
-        dimension_numbers=LAYOUT,
-        preferred_element_type=jnp.float32,
+ROWS = 16
+STEPS = C // ROWS
+NT = (((1,), (1,)), ((), ()))
+TN = (((0,), (0,)), ((), ()))
+EXACT = lax.Precision.HIGHEST
+AT_CTL_ONE = 0
+AT_CTL_TWO = 2944
+AT_ZERO = 5888
+AT_SHORT = 6272
+AT_DEC_TWO = 6656
+AT_DEC_ONE = 9600
+
+
+def band(i):
+    return pl.ds(pl.multiple_of(i * ROWS, ROWS), ROWS)
+
+
+def put_columns(col, base_of, i, strips):
+    lane = lax.broadcasted_iota(jnp.int32, (ROWS, 128), 1)
+    shifted_of = []
+    for strip in strips:
+        left = jnp.where(lane == 0, 0.0, pltpu.roll(strip, 1, axis=1))
+        right = jnp.where(lane == 127, 0.0, pltpu.roll(strip, 127, axis=1))
+        shifted_of.append([left.astype(BF), strip.astype(BF), right.astype(BF)])
+    for p in range(3):
+        for q in range(3):
+            start = pl.multiple_of(base_of(3 * p + q) + i * ROWS, ROWS)
+            col[pl.ds(start, ROWS), 0:128] = shifted_of[p][q]
+            col[pl.ds(start, ROWS), 128:256] = shifted_of[p + 1][q]
+
+
+def sig(v):
+    return jax.nn.sigmoid(v)
+
+
+def slope(v):
+    s = sig(v)
+    return s * (1.0 + v * (1.0 - s))
+
+
+def dot(a, b):
+    return jnp.dot(a, b, preferred_element_type=F32)
+
+
+def put_sums(cols, at, i, pairs):
+    for k, value in enumerate(pairs):
+        cols[band(i), at + k : at + k + 1] = jnp.sum(value, axis=1, keepdims=True)
+
+
+def mid_kernel(
+    acts,
+    terms,
+    enc_one,
+    enc_two,
+    weights,
+    grads,
+    member,
+    ten,
+    twenty,
+    cols,
+    coef,
+    halo,
+    halo_cot,
+    inner,
+    inner_halo,
+    edge,
+    col_t,
+    col_a,
+    col_b,
+    col_d,
+    col_g,
+    back_dec_two,
+    back_dec_one,
+    back_ctl_two,
+    zero_t,
+    short_t,
+    enc_raw,
+    ctl_raw,
+    ctl_out,
+    skip,
+    skip_halo,
+    dec_raw,
+    dec_halo,
+    dec_edge,
+    up_grad,
+    sfg,
+    sfg_edge,
+    sfg_halo,
+    keep_n,
+    keep_skip,
+    keep_dec,
+    mixed,
+    wide,
+    wide_two,
+    note,
+    note_in,
+    note_send,
+    note_recv,
+    halo_send,
+    halo_recv,
+):
+    d = lax.axis_index("dp")
+    r = lax.axis_index("rows")
+    peers = [(d, (r + k) % 8) for k in range(1, 8)]
+    greet(peers)
+    before = (d, (r + 7) % 8)
+    after = (d, (r + 1) % 8)
+    waiting = []
+
+    def send_rows(event, top, bottom, above, below):
+        first = remote(top, below, halo_send.at[event, 0], halo_recv.at[event, 0], before)
+        second = remote(bottom, above, halo_send.at[event, 1], halo_recv.at[event, 1], after)
+        first.start()
+        second.start()
+        waiting.extend([first, second])
+        return (first, second)
+
+    def arrive(pair):
+        pair[0].wait_recv()
+        pair[1].wait_recv()
+
+    raw = send_rows(
+        0, acts.at[0:2, :, 0:128], acts.at[0:2, :, 128:256], halo.at[0, 0:2], halo.at[1, 0:2]
     )
-
-
-def with_halo(source):
-    return extended(source, (("rows", 2),), 1)
-
-
-def mix_channels(matrix, source):
-    return jnp.einsum("oi,bihw->bohw", matrix, source, preferred_element_type=jnp.float32)
-
-
-def mix_back(matrix, upstream):
-    return jnp.einsum("oi,bohw->bihw", matrix, upstream, preferred_element_type=jnp.float32)
-
-
-def flip_kernel(weight):
-    return jnp.transpose(weight[:, ::-1, ::-1, :], (3, 1, 2, 0))
-
-
-def group_norm(source):
-    full_shape = source.shape
-    grouped = source.reshape(
-        full_shape[0], GROUPS, full_shape[1] // GROUPS, full_shape[2], full_shape[3]
-    )
-    group_count = full_shape[1] // GROUPS * full_shape[2] * full_shape[3] * lax.axis_size("rows")
-    group_total, group_square = lax.psum(
-        (jnp.sum(grouped, axis=(2, 3, 4)), jnp.sum(grouped * grouped, axis=(2, 3, 4))), "rows"
-    )
-    average = group_total / group_count
-    inv_spread = lax.rsqrt(group_square / group_count - average * average + EPSILON)
-    normed = (grouped - average[:, :, None, None, None]) * inv_spread[:, :, None, None, None]
-    return (normed.reshape(full_shape), inv_spread)
-
-
-def norm_back(upstream, normed, inv_spread):
-    full_shape = upstream.shape
-    groups_here = inv_spread.shape[1]
-    grouped = upstream.reshape(
-        full_shape[0], groups_here, full_shape[1] // groups_here, full_shape[2], full_shape[3]
-    )
-    normed_grouped = normed.reshape(grouped.shape)
-    group_count = (
-        full_shape[1] // groups_here * full_shape[2] * full_shape[3] * lax.axis_size("rows")
-    )
-    group_total, group_cross = lax.psum(
-        (jnp.sum(grouped, axis=(2, 3, 4)), jnp.sum(grouped * normed_grouped, axis=(2, 3, 4))),
-        "rows",
-    )
-    first_mean = (group_total / group_count)[:, :, None, None, None]
-    cross_mean = (group_cross / group_count)[:, :, None, None, None]
-    result = inv_spread[:, :, None, None, None] * (
-        grouped - first_mean - normed_grouped * cross_mean
-    )
-    return result.reshape(full_shape)
-
-
-def silu_slope(values):
-    sigma = jax.nn.sigmoid(values)
-    return sigma * (1.0 + values * (1.0 - sigma))
-
-
-def input_grad(upstream, weight):
-    flipped = flip_kernel(weight)
-    padded = jnp.pad(upstream, ((0, 0), (0, 0), (2, 2), (0, 0)))
-    spilled = conv_rows(padded, flipped)
-    from_next = shifted(spilled[:, :, :1], "rows", -1)
-    from_prev = shifted(spilled[:, :, -1:], "rows", 1)
-    result = spilled[:, :, 1:-1]
-    result = result.at[:, :, :1].add(from_prev)
-    result = result.at[:, :, -1:].add(from_next)
-    return result
-
-
-def kernel_grad(upstream, padded):
-    wide = jnp.pad(padded, ((0, 0), (0, 0), (0, 0), (1, 1)))
-    row_count = upstream.shape[2]
-    col_count = upstream.shape[3]
-    return jnp.stack(
-        [
-            jnp.stack(
-                [
-                    jnp.einsum(
-                        "bohw,bihw->oi",
-                        upstream,
-                        wide[:, :, row_tap : row_tap + row_count, col_tap : col_tap + col_count],
-                        preferred_element_type=jnp.float32,
-                    )
-                    for col_tap in range(3)
-                ],
-                1,
-            )
-            for row_tap in range(3)
+    late = send_rows(1, acts.at[2, :, 0:128], acts.at[2, :, 128:256], halo.at[0, 2], halo.at[1, 2])
+    late_cot = send_rows(2, acts.at[3], acts.at[3], halo_cot.at[0], halo_cot.at[1])
+
+    lane = lax.broadcasted_iota(jnp.int32, (C, 128), 1)
+    channel = lax.broadcasted_iota(jnp.int32, (C, 128), 0)
+    in_ten = (channel >= 10 * lane) & (channel < 10 * lane + 10)
+    other = lane - 32
+    in_twenty = (channel >= 20 * other) & (channel < 20 * other + 20)
+    ten[...] = jnp.where(in_ten, 1.0, 0.0)
+    twenty[...] = jnp.where(in_twenty, 1.0, 0.0)
+    member[...] = ten[...] + twenty[...]
+    cols[...] = jnp.zeros((C, 128), F32)
+
+    def share(turn):
+        sums = lax.dot_general(cols[...], member[...], TN, precision=EXACT, preferred_element_type=F32)
+        note[turn] = sums[0:8]
+        copies = []
+        for k in range(1, 8):
+            copies.append(
+                remote(
+                    note.at[turn],
+                    note_in.at[turn, k - 1],
+                    note_send.at[turn, k - 1],
+                    note_recv.at[turn, k - 1],
+                    peers[k - 1],
+                )
+            )
+            copies[-1].start()
+        waiting.extend(copies)
+        return copies
+
+    def collect(turn, copies):
+        for copy in copies:
+            copy.wait_recv()
+        total = note[turn]
+        for k in range(7):
+            total = total + note_in[turn, k]
+        return total
+
+    which = lax.broadcasted_iota(jnp.int32, (8, 128), 1)
+    per_group = jnp.where(which < 32, 1.0 / (10 * 2048), 1.0 / (20 * 2048))
+
+    def spread(table, at, rows):
+        padded = jnp.concatenate(rows + [jnp.zeros((8 - len(rows), 128), F32)], axis=0)
+        coef[:, at : at + 8] = lax.dot_general(
+            table[...], padded, NT, precision=EXACT, preferred_element_type=F32
+        )
+
+    def norm_rows(total, k):
+        mean = total[k : k + 1] * per_group[0:1]
+        square = total[k + 1 : k + 2] * per_group[0:1]
+        return [mean, lax.rsqrt(square - mean * mean + EPSILON)]
+
+    def mean_rows(total, k):
+        return [total[k : k + 1] * per_group[0:1], total[k + 1 : k + 2] * per_group[0:1]]
+
+    has_up = r > 0
+    has_down = r < 7
+
+    def masked(strips):
+        return [
+            jnp.where(has_up, strips[0], 0.0),
+            strips[1],
+            strips[2],
+            jnp.where(has_down, strips[3], 0.0),
+        ]
+
+    @pl.loop(0, STEPS)
+    def _(i):
+        latent = acts[0, band(i), :].astype(F32)
+        ctl_in = (latent + acts[1, band(i), :].astype(F32)).astype(BF).astype(F32)
+        under = acts[2, band(i), :].astype(F32)
+        put_sums(cols, 0, i, [latent, latent * latent, ctl_in, ctl_in * ctl_in, under, under * under])
+
+    first_note = share(0)
+
+    for target in (back_dec_two, back_dec_one, back_ctl_two):
+        target[...] = jnp.zeros((C, 3456), BF)
+    for target, start, stride in (
+        (back_dec_two, AT_DEC_TWO, 320),
+        (back_dec_one, AT_DEC_ONE + 320, 640),
+        (back_ctl_two, AT_CTL_TWO, 320),
+    ):
+        for tap in range(9):
+            block = weights[:, start + stride * tap : start + stride * tap + 320].astype(F32)
+            target[:, 384 * (8 - tap) : 384 * (8 - tap) + 320] = block.T.astype(BF)
+    zero_t[...] = weights[:, AT_ZERO : AT_ZERO + 320].astype(F32).T.astype(BF)
+    short_t[...] = weights[:, AT_SHORT : AT_SHORT + 320].astype(F32).T.astype(BF)
+    for tap in range(9):
+        col_g[384 * tap + 320 : 384 * tap + 384, :] = jnp.zeros((64, 256), BF)
+
+    total = collect(0, first_note)
+    spread(ten, 0, norm_rows(total, 0) + norm_rows(total, 2))
+    spread(twenty, 8, norm_rows(total, 4))
+    arrive(raw)
+
+    def plain(tap):
+        return 320 * tap
+
+    def first_act(source_of, at, col, base_of):
+        @pl.loop(0, STEPS)
+        def _(i):
+            mean = coef[band(i), at : at + 1]
+            inv = coef[band(i), at + 1 : at + 2]
+            strips = []
+            for strip in source_of(i):
+                normed = (strip - mean) * inv
+                strips.append(normed * sig(normed))
+            put_columns(col, base_of, i, masked(strips))
+
+    def latent_of(i):
+        own = acts[0, band(i), :].astype(F32)
+        return [halo[0, 0, band(i), :].astype(F32), own[:, 0:128], own[:, 128:256], halo[1, 0, band(i), :].astype(F32)]
+
+    def ctl_in_of(i):
+        own = acts[1, band(i), :].astype(F32)
+        hint = [halo[0, 1, band(i), :].astype(F32), own[:, 0:128], own[:, 128:256], halo[1, 1, band(i), :].astype(F32)]
+        return [(a + b).astype(BF).astype(F32) for a, b in zip(latent_of(i), hint)]
+
+    first_act(latent_of, 0, col_t, plain)
+    enc_raw[...] = dot(enc_one[...], col_t[...])
+    edge[0] = enc_raw[:, 0:128].astype(BF)
+    edge[1] = enc_raw[:, 128:256].astype(BF)
+    enc_rows = send_rows(3, edge.at[0], edge.at[1], inner_halo.at[0], inner_halo.at[1])
+    first_act(ctl_in_of, 2, col_a, plain)
+    ctl_raw[...] = dot(weights[:, AT_CTL_ONE : AT_CTL_ONE + 2880], col_a[...])
+    edge[2] = ctl_raw[:, 0:128].astype(BF)
+    edge[3] = ctl_raw[:, 128:256].astype(BF)
+    ctl_rows = send_rows(4, edge.at[2], edge.at[3], inner_halo.at[2], inner_halo.at[3])
+
+    @pl.loop(0, STEPS)
+    def _(i):
+        enc = enc_raw[band(i), :] + terms[band(i), 0:1]
+        ctl = ctl_raw[band(i), :] + terms[band(i), 1:2]
+        put_sums(cols, 0, i, [enc, enc * enc, ctl, ctl * ctl])
+
+    second_note = share(1)
+
+    def under_of(i):
+        own = acts[2, band(i), :].astype(F32)
+        return [halo[0, 2, band(i), :].astype(F32), own[:, 0:128], own[:, 128:256], halo[1, 2, band(i), :].astype(F32)]
+
+    def joined_low(tap):
+        return 640 * tap
+
+    def joined_high(tap):
+        return 640 * tap + 320
+
+    def spaced(tap):
+        return 384 * tap
+
+    arrive(late)
+    first_act(under_of, 8, col_d, joined_low)
+
+    total = collect(1, second_note)
+    spread(ten, 16, norm_rows(total, 0) + norm_rows(total, 2))
+
+    def second_act(raw_ref, at_halo, term_at, at, col, keep):
+        @pl.loop(0, STEPS)
+        def _(i):
+            mean = coef[band(i), at : at + 1]
+            inv = coef[band(i), at + 1 : at + 2]
+            own = raw_ref[band(i), :]
+            term = terms[band(i), term_at : term_at + 1]
+            strips = []
+            for strip in (
+                inner_halo[at_halo, band(i), :].astype(F32),
+                own[:, 0:128],
+                own[:, 128:256],
+                inner_halo[at_halo + 1, band(i), :].astype(F32),
+            ):
+                strips.append((strip + term - mean) * inv)
+            if keep is not None:
+                keep[band(i), 0:128] = strips[1]
+                keep[band(i), 128:256] = strips[2]
+            put_columns(col, plain, i, masked([v * sig(v) for v in strips]))
+
+    arrive(enc_rows)
+    second_act(enc_raw, 0, 0, 16, col_t, None)
+    enc_raw[...] = dot(enc_two[...], col_t[...])
+    arrive(ctl_rows)
+    second_act(ctl_raw, 2, 1, 18, col_b, keep_n)
+    inner[...] = dot(weights[:, AT_CTL_TWO : AT_CTL_TWO + 2880], col_b[...])
+
+    @pl.loop(0, STEPS)
+    def _(i):
+        latent = acts[0, band(i), :].astype(F32)
+        ctl_in = (latent + acts[1, band(i), :].astype(F32)).astype(BF).astype(F32)
+        ctl_out[band(i), :] = (ctl_in + inner[band(i), :]).astype(BF)
+
+    inner[...] = dot(weights[:, AT_ZERO : AT_ZERO + 320], ctl_out[...])
+
+    @pl.loop(0, STEPS)
+    def _(i):
+        latent = acts[0, band(i), :].astype(F32)
+        enc_out = (latent + enc_raw[band(i), :]).astype(BF).astype(F32)
+        joined = (enc_out + inner[band(i), :]).astype(BF)
+        skip[0, band(i), :] = joined[:, 0:128]
+        skip[1, band(i), :] = joined[:, 128:256]
+        value = joined.astype(F32)
+        put_sums(cols, 0, i, [value, value * value])
+
+    skip_rows = send_rows(5, skip.at[0], skip.at[1], skip_halo.at[0], skip_halo.at[1])
+    third_note = share(2)
+
+    arrive(late_cot)
+    scale = 2.0**-8
+
+    def cot_of(i):
+        far = halo_cot[0, band(i), :].astype(F32)
+        own = acts[3, band(i), :].astype(F32)
+        near = halo_cot[1, band(i), :].astype(F32)
+        far = jnp.where(has_up, far, 0.0) * scale
+        near = jnp.where(has_down, near, 0.0) * scale
+        own = own * scale
+        return [far[:, 0:128], far[:, 128:256], own[:, 0:128], own[:, 128:256], near[:, 0:128], near[:, 128:256]]
+
+    for part in range(2):
+
+        @pl.loop(0, STEPS)
+        def _(i):
+            strips = cot_of(i)[2 * part : 2 * part + 4]
+            put_columns(col_g, spaced, i, strips)
+
+        up_grad[:, 256 * part : 256 * part + 256] = dot(back_dec_two[...], col_g[...])
+
+    @pl.loop(0, STEPS)
+    def _(i):
+        for k, strip in enumerate(cot_of(i)[1:5]):
+            wide[band(i), 128 * k : 128 * k + 128] = strip.astype(BF)
+
+    mixed[...] = dot(short_t[...], wide[...])
+
+    total = collect(2, third_note)
+    spread(twenty, 24, norm_rows(total, 0))
+    arrive(skip_rows)
+
+    @pl.loop(0, STEPS)
+    def _(i):
+        mean = coef[band(i), 24:25]
+        inv = coef[band(i), 25:26]
+        strips = []
+        for k, strip in enumerate(
+            (skip_halo[0, band(i), :], skip[0, band(i), :], skip[1, band(i), :], skip_halo[1, band(i), :])
+        ):
+            normed = (strip.astype(F32) - mean) * inv
+            keep_skip[band(i), 128 * k : 128 * k + 128] = normed
+            strips.append(normed * sig(normed))
+        put_columns(col_d, joined_high, i, masked(strips))
+
+    dec_raw[...] = dot(weights[:, AT_DEC_ONE : AT_DEC_ONE + 5760], col_d[...])
+    dec_edge[0] = dec_raw[:, 0:128].astype(BF)
+    dec_edge[1] = dec_raw[:, 128:256].astype(BF)
+    dec_rows = send_rows(6, dec_edge.at[0], dec_edge.at[1], dec_halo.at[0], dec_halo.at[1])
+
+    @pl.loop(0, STEPS)
+    def _(i):
+        value = dec_raw[band(i), :] + terms[band(i), 2:3]
+        put_sums(cols, 0, i, [value, value * value])
+
+    fourth_note = share(3)
+    total = collect(3, fourth_note)
+    spread(ten, 32, norm_rows(total, 0))
+
+    def keep_dec_rows(i, strip, k):
+        mean = coef[band(i), 32:33]
+        inv = coef[band(i), 33:34]
+        term = terms[band(i), 2:3]
+        normed = (strip + term - mean) * inv
+        keep_dec[band(i), 128 * k : 128 * k + 128] = normed
+        upstream = up_grad[band(i), 128 * k : 128 * k + 128] * slope(normed)
+        up_grad[band(i), 128 * k : 128 * k + 128] = upstream
+        return (normed, upstream)
+
+    @pl.loop(0, STEPS)
+    def _(i):
+        one_n, one_g = keep_dec_rows(i, dec_raw[band(i), 0:128], 1)
+        two_n, two_g = keep_dec_rows(i, dec_raw[band(i), 128:256], 2)
+        put_sums(cols, 0, i, [one_g + two_g, one_g * one_n + two_g * two_n])
+
+    fifth_note = share(4)
+    arrive(dec_rows)
+
+    @pl.loop(0, STEPS)
+    def _(i):
+        keep_dec_rows(i, dec_halo[0, band(i), :].astype(F32), 0)
+        keep_dec_rows(i, dec_halo[1, band(i), :].astype(F32), 3)
+
+    total = collect(4, fifth_note)
+    spread(ten, 40, mean_rows(total, 0))
+
+    @pl.loop(0, STEPS)
+    def _(i):
+        inv = coef[band(i), 33:34]
+        mean = coef[band(i), 40:41]
+        cross = coef[band(i), 41:42]
+        strips = []
+        for k in range(4):
+            lanes = slice(128 * k, 128 * k + 128)
+            strips.append(inv * (up_grad[band(i), lanes] - mean - keep_dec[band(i), lanes] * cross))
+        put_columns(col_g, spaced, i, masked(strips))
+
+    sfg[...] = dot(back_dec_one[...], col_g[...])
+    sfg_edge[0] = sfg[:, 0:128].astype(BF)
+    sfg_edge[1] = sfg[:, 128:256].astype(BF)
+    sfg_rows = send_rows(7, sfg_edge.at[0], sfg_edge.at[1], sfg_halo.at[0], sfg_halo.at[1])
+
+    @pl.loop(0, STEPS)
+    def _(i):
+        normed = keep_skip[band(i), 128:384]
+        value = sfg[band(i), :] * slope(normed)
+        up_grad[band(i), 128:384] = value
+        put_sums(cols, 0, i, [value, value * normed])
+
+    sixth_note = share(5)
+    arrive(sfg_rows)
+
+    @pl.loop(0, STEPS)
+    def _(i):
+        for at, lanes in ((0, slice(0, 128)), (1, slice(384, 512))):
+            up_grad[band(i), lanes] = sfg_halo[at, band(i), :].astype(F32) * slope(keep_skip[band(i), lanes])
+
+    total = collect(5, sixth_note)
+    spread(twenty, 48, mean_rows(total, 0))
+
+    @pl.loop(0, STEPS)
+    def _(i):
+        inv = coef[band(i), 25:26]
+        mean = coef[band(i), 48:49]
+        cross = coef[band(i), 49:50]
+        value = inv * (up_grad[band(i), :] - mean - keep_skip[band(i), :] * cross) + mixed[band(i), :]
+        wide[band(i), :] = value.astype(BF)
+
+    up_grad[...] = dot(zero_t[...], wide[...])
+
+    @pl.loop(0, STEPS)
+    def _(i):
+        strips = []
+        for k in range(4):
+            strips.append(up_grad[band(i), 128 * k : 128 * k + 128].astype(BF).astype(F32))
+        wide_two[band(i), 0:128] = strips[1].astype(BF)
+        wide_two[band(i), 128:256] = strips[2].astype(BF)
+        put_columns(col_g, spaced, i, masked(strips))
+
+    sfg[...] = dot(back_ctl_two[...], col_g[...])
+
+    @pl.loop(0, STEPS)
+    def _(i):
+        normed = keep_n[band(i), :]
+        value = sfg[band(i), :] * slope(normed)
+        sfg[band(i), :] = value
+        put_sums(cols, 0, i, [value, value * normed])
+
+    seventh_note = share(6)
+    grads[:, 2944:5824] = lax.dot_general(
+        wide_two[...], col_b[...], NT, preferred_element_type=F32
+    ).astype(BF)
+    grads[:, 5888:6208] = lax.dot_general(
+        wide[:, 128:384], ctl_out[...], NT, preferred_element_type=F32
+    ).astype(BF)
+    grads[:, 6272:GLANES] = jnp.zeros((C, GLANES - 6272), BF)
+    total = collect(6, seventh_note)
+    spread(ten, 56, mean_rows(total, 0))
+
+    @pl.loop(0, STEPS)
+    def _(i):
+        inv = coef[band(i), 19:20]
+        mean = coef[band(i), 56:57]
+        cross = coef[band(i), 57:58]
+        value = inv * (sfg[band(i), :] - mean - keep_n[band(i), :] * cross)
+        wide_two[band(i), :] = value.astype(BF)
+
+    grads[:, 0:2880] = lax.dot_general(wide_two[...], col_a[...], NT, preferred_element_type=F32).astype(BF)
+    for copy in waiting:
+        copy.wait_send()
+
+
+def middle(acts, terms, enc_one, enc_two, weights):
+    dma = pltpu.SemaphoreType.DMA
+    whole = pl.BlockSpec(memory_space=pltpu.VMEM)
+    return pl.pallas_call(
+        mid_kernel,
+        out_shape=jax.ShapeDtypeStruct((C, GLANES), BF),
+        in_specs=[whole] * 5,
+        out_specs=whole,
+        scratch_shapes=[
+            pltpu.VMEM((C, 128), F32),
+            pltpu.VMEM((C, 128), F32),
+            pltpu.VMEM((C, 128), F32),
+            pltpu.VMEM((C, 128), F32),
+            pltpu.VMEM((C, 128), F32),
+            pltpu.VMEM((2, 3, C, 128), BF),
+            pltpu.VMEM((2, C, 256), BF),
+            pltpu.VMEM((C, 256), F32),
+            pltpu.VMEM((4, C, 128), BF),
+            pltpu.VMEM((4, C, 128), BF),
+            pltpu.VMEM((2880, 256), BF),
+            pltpu.VMEM((2880, 256), BF),
+            pltpu.VMEM((2880, 256), BF),
+            pltpu.VMEM((5760, 256), BF),
+            pltpu.VMEM((3456, 256), BF),
+            pltpu.VMEM((C, 3456), BF),
+            pltpu.VMEM((C, 3456), BF),
+            pltpu.VMEM((C, 3456), BF),
+            pltpu.VMEM((C, C), BF),
+            pltpu.VMEM((C, C), BF),
+            pltpu.VMEM((C, 256), F32),
+            pltpu.VMEM((C, 256), F32),
+            pltpu.VMEM((C, 256), BF),
+            pltpu.VMEM((2, C, 128), BF),
+            pltpu.VMEM((2, C, 128), BF),
+            pltpu.VMEM((C, 256), F32),
+            pltpu.VMEM((2, C, 128), BF),
+            pltpu.VMEM((2, C, 128), BF),
+            pltpu.VMEM((C, 512), F32),
+            pltpu.VMEM((C, 256), F32),
+            pltpu.VMEM((2, C, 128), BF),
+            pltpu.VMEM((2, C, 128), BF),
+            pltpu.VMEM((C, 256), F32),
+            pltpu.VMEM((C, 512), F32),
+            pltpu.VMEM((C, 512), F32),
+            pltpu.VMEM((C, 512), F32),
+            pltpu.VMEM((C, 512), BF),
+            pltpu.VMEM((C, 256), BF),
+            pltpu.VMEM((7, 8, 128), F32),
+            pltpu.VMEM((7, 7, 8, 128), F32),
+            dma((7, 7)),
+            dma((7, 7)),
+            dma((8, 2)),
+            dma((8, 2)),
         ],
-        1,
-    )
-
-
-def block_front(source, conv_one, time_term):
-    normed_in, spread_in = group_norm(source.astype(jnp.float32))
-    first_halo = with_halo(jax.nn.silu(normed_in).astype(jnp.bfloat16))
-    inner_sum = conv_rows(first_halo, conv_one) + time_term[:, :, None, None]
-    normed, spread = group_norm(inner_sum)
-    second_act = jax.nn.silu(normed).astype(jnp.bfloat16)
-    return (normed_in, spread_in, first_halo, normed, spread, second_act)
+        compiler_params=pltpu.CompilerParams(
+            collective_id=2, has_side_effects=True, vmem_limit_bytes=62 * 1024 * 1024
+        ),
+        name="middle",
+    )(acts, terms, enc_one, enc_two, weights)
+
+
+def flat(kernel, width):
+    kernel = kernel.reshape(kernel.shape[0], -1)
+    return jnp.pad(kernel, ((0, 0), (0, width - kernel.shape[1])))
 
 
 def per_device(
@@ -585,83 +1014,31 @@
     dec_shortcut,
     zero_conv,
 ):
-    def flat(kernel, width):
-        kernel = kernel.reshape(kernel.shape[0], -1)
-        return jnp.pad(kernel, ((0, 0), (0, width - kernel.shape[1])))
-
     shard = jnp.concatenate(
         [
             flat(ctl_conv_one, 2944),
             flat(ctl_conv_two, 2944),
             flat(zero_conv, 384),
-            flat(dec_shortcut, 640),
+            flat(dec_shortcut[:, C:], 384),
             flat(dec_conv_two, 2944),
-            flat(dec_conv_one, LANES - 9856),
+            flat(dec_conv_one, LANES - AT_DEC_ONE),
         ],
         axis=1,
     )
     weights = gather_weights(shard)
-    ctl_one = weights[:, :2880].reshape(C, 3, 3, C)
-    ctl_two = weights[:, 2944:5824].reshape(C, 3, 3, C)
-    zero_full = weights[:, 5888:6208]
-    dec_short = weights[:, 6272:6912]
-    dec_two = weights[:, 6912:9792].reshape(C, 3, 3, C)
-    dec_one = weights[:, 9856:15616].reshape(C, 3, 3, 2 * C)
     half_width = C // 2
     frequency = jnp.exp(-math.log(10000.0) * jnp.arange(half_width, dtype=jnp.float32) / half_width)
     angles = timesteps.astype(jnp.float32)[:, None] * frequency[None, :]
     sinusoid = jnp.concatenate([jnp.cos(angles), jnp.sin(angles)], axis=1).astype(jnp.bfloat16)
     time_embed = jnp.dot(sinusoid, time_weight, preferred_element_type=jnp.float32)
     time_act = jax.nn.silu(time_embed).astype(jnp.bfloat16)
-    enc_term = jnp.dot(time_act, enc_proj, preferred_element_type=jnp.float32)
-    ctl_term = jnp.dot(time_act, ctl_proj, preferred_element_type=jnp.float32)
-    dec_term = jnp.dot(time_act, dec_proj, preferred_element_type=jnp.float32)
-    enc_parts = block_front(latent, enc_conv_one, enc_term)
-    enc_out = (
-        latent.astype(jnp.float32) + conv_rows(with_halo(enc_parts[5]), enc_conv_two)
-    ).astype(jnp.bfloat16)
-    ctl_in = (latent.astype(jnp.float32) + hint_field.astype(jnp.float32)).astype(jnp.bfloat16)
-    ctl_parts = block_front(ctl_in, ctl_one, ctl_term)
-    ctl_halo = with_halo(ctl_parts[5])
-    ctl_out = (ctl_in.astype(jnp.float32) + conv_rows(ctl_halo, ctl_two)).astype(jnp.bfloat16)
-    skip_sum = (enc_out.astype(jnp.float32) + mix_channels(zero_full, ctl_out)).astype(jnp.bfloat16)
-    joined = jnp.concatenate([from_below, skip_sum], axis=1)
-    dec_parts = block_front(joined, dec_one, dec_term)
-    loss_scale = float(
-        cotangent.shape[0]
-        * lax.axis_size("dp")
-        * cotangent.shape[2]
-        * lax.axis_size("rows")
-        * cotangent.shape[3]
-    ) ** (-0.5)
-    out_grad = (cotangent.astype(jnp.float32) * loss_scale).astype(jnp.bfloat16)
-    dec_second_grad = input_grad(out_grad, dec_two)
-    dec_inner_grad = norm_back(
-        dec_second_grad * silu_slope(dec_parts[3]), dec_parts[3], dec_parts[4]
-    ).astype(jnp.bfloat16)
-    skip_first_grad = input_grad(dec_inner_grad, dec_one[:, :, :, C:])
-    skip_normed = dec_parts[0][:, C:]
-    skip_spread = dec_parts[1][:, GROUPS // 2 :]
-    skip_grad = norm_back(
-        skip_first_grad * silu_slope(skip_normed), skip_normed, skip_spread
-    ) + mix_back(dec_short[:, C:], out_grad)
-    skip_grad = skip_grad.astype(jnp.bfloat16)
-    zero_local = jnp.einsum("bohw,bihw->oi", skip_grad, ctl_out, preferred_element_type=jnp.float32)
-    ctl_out_grad = mix_back(zero_full, skip_grad).astype(jnp.bfloat16)
-    two_local = kernel_grad(ctl_out_grad, ctl_halo)
-    ctl_second_grad = input_grad(ctl_out_grad, ctl_two)
-    ctl_inner_grad = norm_back(
-        ctl_second_grad * silu_slope(ctl_parts[3]), ctl_parts[3], ctl_parts[4]
-    ).astype(jnp.bfloat16)
-    one_local = kernel_grad(ctl_inner_grad, ctl_parts[2])
-    grads = jnp.concatenate(
-        [
-            flat(one_local.astype(BF), 2944),
-            flat(two_local.astype(BF), 2944),
-            flat(zero_local.astype(BF), GLANES - 5888),
-        ],
-        axis=1,
-    )
+    terms = jnp.concatenate(
+        [jnp.dot(time_act, proj, preferred_element_type=jnp.float32) for proj in (enc_proj, ctl_proj, dec_proj)],
+        axis=0,
+    ).T
+    terms = jnp.pad(terms, ((0, 0), (0, 5)))
+    acts = jnp.stack([a.reshape(C, 256) for a in (latent, hint_field, from_below, cotangent)])
+    grads = middle(acts, terms, flat(enc_conv_one, 2880), flat(enc_conv_two, 2880), weights)
     owned = reduce_grads(grads)
     return (
         owned[:, :2880].reshape(10, 3, 3, C),

time: 540 us -> 261 us (0.48); the launches traced: 534 us -> 261 us
  blocking collectives: 111 us -> 0 us
  matrix products: 96.2 us -> 3.52 us
  Pallas kernels: 162 us -> 235 us
  local copies, waits for them, and re-layouts: 82.7 us -> 19.2 us
  starting transfers between devices: 45.2 us -> 0 us
  other arithmetic: 25.9 us -> 1.32 us
  waiting for transfers between devices: 7.37 us -> 0 us
    psum x7 -> x0, blocking collectives: 111 us -> none  [the longest x4 64.7 us: group_norm(): lax.psum((jnp.sum(grouped, axis=(2, 3, 4)), jnp.sum(grouped * grouped, ax...]
    pallas_call x0 -> x1, Pallas kernels: none -> 101 us  [middle(): pl.pallas_call(mid_kernel, out_shape=jax.ShapeDtypeStruct((C, GLANES), BF...]
    conv_general_dilated x8 -> x0, matrix products: 75.3 us -> none  [conv_rows(): lax.conv_general_dilated(padded, weight, (1, 1), ((0, 0), (1, 1)), dimens...]
    ppermute x16 -> x0, starting transfers between devices: 45.2 us -> none  [the longest x5 17.4 us: extended(): before = lax.ppermute(last, axis, up)]
    slice x19 -> x1, local copies, waits for them, and re-layouts: 32.2 us -> 0.08 us  [per_device(): dec_shortcut[:, C:]]
    pallas_call x1, Pallas kernels: 90.8 us -> 62.3 us  [reduce_grads(): pl.pallas_call(reduce_kernel, out_shape=jax.ShapeDtypeStruct((4, 8, 16, 2...]
    dot_general x25 -> x3, matrix products: 19.5 us -> 3.29 us  [per_device(): jnp.dot(time_act, proj, preferred_element_type=jnp.float32)]
    concatenate x5 -> x1, local copies, waits for them, and re-layouts: 11.6 us -> 0.14 us  [per_device(): jnp.concatenate([jnp.dot(time_act, proj, preferred_element_type=jnp.float...]
  transfers between devices with their start and end apart: 16 -> 0, of which waited for: 2 -> 0; matrix products, arithmetic and copies ran while one was open for 18% -> 0% of each run, Pallas kernels for 0% -> 0%
where the time goes in v2:
time: 261 us
  Pallas kernels  235 us (90%)
  local copies, waits for them, and re-layouts  19.2 us (7%)
  matrix products  3.52 us (1%)
    pallas_call x1, Pallas kernels, middle(): pl.pallas_call(mid_kernel, out_shape=jax.ShapeDtypeStruct((C, GLANES), BF...  101 us
    pallas_call x1, Pallas kernels, gather_weights(): pl.pallas_call(gather_kernel, out_shape=jax.ShapeDtypeStruct((320, LANES)...  71.5 us
    pallas_call x1, Pallas kernels, reduce_grads(): pl.pallas_call(reduce_kernel, out_shape=jax.ShapeDtypeStruct((4, 8, 16, 2...  62.3 us
    unnamed x32, local copies, waits for them, and re-layouts  7.1 us
    reshape x6, local copies, waits for them, and re-layouts, flat(): kernel = kernel.reshape(kernel.shape[0], -1)  5.37 us

profile of v2, /device:TPU:1, one launch (start us, length us, event | category | flops | bytes accessed | tf_op | source)
XLA Modules:
  0.0 260.9 jit_solution(11368985056118116472)
XLA Ops:
  1.6 0.5 copy-done
  2.1 0.2 convolution_reduce_fusion
  2.4 1.5 fusion.6
  3.9 1.5 fusion.5
  5.4 0.3 fusion.4
  5.9 0.1 reshape.87
  6.0 0.1 reshape.88
  6.1 0.1 reshape.89
  6.3 0.1 copy.38
  6.4 0.7 pad.29.terms
  7.2 0.1 stack_reshape.13
  7.3 0.1 stack_reshape.14
  7.6 0.9 pad_maximum_fusion.acts
  8.5 0.1 reshape.91
  9.2 0.7 pad.36.src
  9.9 3.0 %copy.39 = bf16[320,3,3,320]{0,3,2,1:T(8,128)(2,1)S(1)} copy(bf16[320,3,3,320]{3,0,2,1:T(8,128)(2,1)} %param.26) | data formatting | bytes 3686400 | tf_op args[9]
  12.9 2.5 copy.43.enc_one
  15.4 3.0 %copy.40 = bf16[320,3,3,320]{0,3,2,1:T(8,128)(2,1)S(1)} copy(bf16[320,3,3,320]{3,0,2,1:T(8,128)(2,1)} %param.27) | data formatting | bytes 3686400 | tf_op args[10]
  18.4 2.4 copy.44.enc_two
  20.8 71.5 %gather_weights.1.weights = bf16[320,16384]{1,0:T(8,128)(2,1)} custom-call(bf16[8,16,512]{2,1,0:T(8,128)(2,1)} %pad.36.src), custom_call_target="tpu_custom_call" | custom-call | tf_op jit(solution)/shard_map/gather_weights/pallas_call | solution.py:183
  92.3 101.2 %middle.1.grads = bf16[320,8192]{1,0:T(8,128)(2,1)} custom-call(bf16[4,320,256]{2,1,0:T(8,128)(2,1)} %pad_maximum_fusion.acts, f32[320,8]{1,0:T(8,128)} %pad.29.terms, bf16[320,2880]{1,0:T(8,128)(2,1)} %copy.43.enc_one, bf16[320,2880]{1,0:T(8,128)(2,1)} %copy.44.enc_two, bf16[320,16384]{1,0:T(8,128)(2,1)} %gather_weights.1.weights), custom_call_target="tpu_custom_call" | custom-call | tf_op jit(solution)/shard_map/middle/pallas_call | solution.py:935
  193.5 62.3 %reduce_grads.1 = f32[4,8,16,256]{3,2,1,0:T(8,128)} custom-call(bf16[320,8192]{1,0:T(8,128)(2,1)} %middle.1.grads), custom_call_target="tpu_custom_call" | custom-call | tf_op jit(solution)/shard_map/reduce_grads/pallas_call | solution.py:385
  255.9 1.2 reshape.111
  257.1 0.3 fusion.3
  257.5 0.1 reshape.95
  257.8 0.1 reshape.96
  257.9 0.2 pad_maximum_fusion.1
  258.1 0.2 pad.55
  258.3 0.3 copy.55
  258.6 0.6 slice.43
  259.2 0.8 reshape.99
  260.0 0.8 reshape.98
  (51 shorter events, 1.4 us)
Async XLA Ops:
  0.6 1.5 copy-start
  0.6 5.1 %copy-start.11 = (bf16[10,640]{1,0:T(8,128)(2,1)S(1)}, bf16[10,640]{1,0:T(8,128)(2,1)}, u32[]{:S(2)}) copy-start(bf16[10,640]{1,0:T(8,128)(2,1)} %param.32) | copy-start | bytes 38404
  0.7 5.5 %copy-start.9 = (bf16[10,3,3,320]{3,2,1,0:T(4,128)(2,1)S(1)}, bf16[10,3,3,320]{3,2,1,0:T(4,128)(2,1)}, u32[]{:S(2)}) copy-start(bf16[10,3,3,320]{3,2,1,0:T(4,128)(2,1)} %param.31) | copy-start | bytes 172804
  0.7 5.3 %copy-start.8 = (bf16[10,3,3,320]{3,2,1,0:T(4,128)(2,1)S(1)}, bf16[10,3,3,320]{3,2,1,0:T(4,128)(2,1)}, u32[]{:S(2)}) copy-start(bf16[10,3,3,320]{3,2,1,0:T(4,128)(2,1)} %param.29) | copy-start | bytes 172804
  0.7 5.2 %copy-start.7 = (bf16[10,3,3,320]{3,2,1,0:T(4,128)(2,1)S(1)}, bf16[10,3,3,320]{3,2,1,0:T(4,128)(2,1)}, u32[]{:S(2)}) copy-start(bf16[10,3,3,320]{3,2,1,0:T(4,128)(2,1)} %param.28) | copy-start | bytes 172804
  0.7 4.7 %copy-start.1 = (bf16[1280,320]{0,1:T(8,128)(2,1)S(1)}, bf16[1280,320]{0,1:T(8,128)(2,1)}, u32[]{:S(2)}) copy-start(bf16[1280,320]{0,1:T(8,128)(2,1)} %param.23) | copy-start | bytes 2457604
  2.1 5.0 %copy-start.2 = (bf16[1,320,2,128]{3,2,1,0:T(2,128)(2,1)S(1)}, bf16[1,320,2,128]{3,2,1,0:T(2,128)(2,1)}, u32[]{:S(2)}) copy-start(bf16[1,320,2,128]{3,2,1,0:T(2,128)(2,1)} %param.17) | copy-start | bytes 491524
  2.1 5.1 %copy-start.3 = (bf16[1,320,2,128]{3,2,1,0:T(2,128)(2,1)S(1)}, bf16[1,320,2,128]{3,2,1,0:T(2,128)(2,1)}, u32[]{:S(2)}) copy-start(bf16[1,320,2,128]{3,2,1,0:T(2,128)(2,1)} %param.18) | copy-start | bytes 491524
  2.4 5.0 %copy-start.4 = (bf16[1,320,2,128]{3,2,1,0:T(2,128)(2,1)S(1)}, bf16[1,320,2,128]{3,2,1,0:T(2,128)(2,1)}, u32[]{:S(2)}) copy-start(bf16[1,320,2,128]{3,2,1,0:T(2,128)(2,1)} %param.19) | copy-start | bytes 491524
  2.4 5.1 %copy-start.5 = (bf16[1,320,2,128]{3,2,1,0:T(2,128)(2,1)S(1)}, bf16[1,320,2,128]{3,2,1,0:T(2,128)(2,1)}, u32[]{:S(2)}) copy-start(bf16[1,320,2,128]{3,2,1,0:T(2,128)(2,1)} %param.20) | copy-start | bytes 491524
  5.4 3.1 %copy-start.6 = (bf16[10,3,3,640]{3,2,1,0:T(4,128)(2,1)S(1)}, bf16[10,3,3,640]{3,2,1,0:T(4,128)(2,1)}, u32[]{:S(2)}) copy-start(bf16[10,3,3,640]{3,2,1,0:T(4,128)(2,1)} %param.30) | copy-start | bytes 345604
  5.8 2.9 %copy-start.10 = (bf16[10,320]{1,0:T(8,128)(2,1)S(1)}, bf16[10,320]{1,0:T(8,128)(2,1)}, u32[]{:S(2)}) copy-start(bf16[10,320]{1,0:T(8,128)(2,1)} %param.33) | copy-start | bytes 19204

commit v3 on v2

v3 whole, which is shorter than its diff:
```python
import math

import jax
import jax.numpy as jnp
from jax import lax
from jax.experimental import pallas as pl
from jax.experimental.pallas import tpu as pltpu
from jax.sharding import PartitionSpec as P

C = 320
EPSILON = 1e-05
MESH = pl.DeviceIdType.MESH
LANES = 16384
HALF = 4096
BF = jnp.bfloat16
F32 = jnp.float32
ROWS = 16
STEPS = C // ROWS
NT = (((1,), (1,)), ((), ()))
TN = (((0,), (0,)), ((), ()))
EXACT = lax.Precision.HIGHEST
AT_CTL_ONE = 0
AT_CTL_TWO = 2944
AT_ZERO = 5888
AT_DEC_ONE = 6272
AT_SHORT = 12032
AT_DEC_TWO = 12416


def place():
    d = lax.axis_index("dp")
    r = lax.axis_index("rows")
    return (d // 8, (d // 2) % 4, d % 2, r // 4, r % 4)


def device_of(zh, y, c, zl, x):
    return (zh * 8 + y * 2 + c, zl * 4 + x)


def remote(src, dst, send, recv, where):
    return pltpu.make_async_remote_copy(
        src_ref=src, dst_ref=dst, send_sem=send, recv_sem=recv, device_id=where, device_id_type=MESH
    )


def greet(peers):
    barrier = pltpu.get_barrier_semaphore()
    for where in peers:
        pl.semaphore_signal(barrier, inc=1, device_id=where, device_id_type=MESH)
    pl.semaphore_wait(barrier, len(peers))


def lanes_at(start, size):
    return pl.ds(pl.multiple_of(start, 128), size)


def band(i):
    return pl.ds(pl.multiple_of(i * ROWS, ROWS), ROWS)


def put_columns(col, base_of, i, strips):
    lane = lax.broadcasted_iota(jnp.int32, (ROWS, 128), 1)
    shifted_of = []
    for strip in strips:
        left = jnp.where(lane == 0, 0.0, pltpu.roll(strip, 1, axis=1))
        right = jnp.where(lane == 127, 0.0, pltpu.roll(strip, 127, axis=1))
        shifted_of.append([left.astype(BF), strip.astype(BF), right.astype(BF)])
    for p in range(3):
        for q in range(3):
            start = pl.multiple_of(base_of(3 * p + q) + i * ROWS, ROWS)
            col[pl.ds(start, ROWS), 0:128] = shifted_of[p][q]
            col[pl.ds(start, ROWS), 128:256] = shifted_of[p + 1][q]


def sig(v):
    return jax.nn.sigmoid(v)


def slope(v):
    s = sig(v)
    return s * (1.0 + v * (1.0 - s))


def dot(a, b):
    return jnp.dot(a, b, preferred_element_type=F32)


def taps_dot(kernel, col):
    total = dot(kernel[0], col[0:C, :])
    for tap in range(1, 9):
        total = total + dot(kernel[tap], col[C * tap : C * tap + C, :])
    return total


def put_sums(cols, at, i, pairs):
    for k, value in enumerate(pairs):
        cols[band(i), at + k : at + k + 1] = jnp.sum(value, axis=1, keepdims=True)


def step_kernel(
    src,
    acts,
    terms,
    enc_one_hbm,
    enc_two_hbm,
    out,
    member,
    ten,
    twenty,
    cols,
    coef,
    halo,
    halo_cot,
    inner,
    inner_halo,
    edge,
    col_t,
    col_a,
    col_b,
    col_d,
    col_g,
    back_dec_two,
    back_dec_one,
    back_ctl_two,
    zero_t,
    short_t,
    enc_raw,
    ctl_raw,
    ctl_out,
    skip,
    skip_halo,
    dec_raw,
    dec_halo,
    dec_edge,
    up_grad,
    sfg,
    sfg_edge,
    sfg_halo,
    keep_n,
    keep_skip,
    keep_dec,
    mixed,
    wide,
    wide_two,
    note,
    note_in,
    note_send,
    note_recv,
    halo_send,
    halo_recv,
    enc_one,
    enc_two,
    enc_sem,
    weights,
    parts,
    column,
    gath,
    own_sem,
    ph1_send,
    ph1_recv,
    ph2_send,
    ph2_recv,
    ph3_send,
    ph3_recv,
    ph4_send,
    ph4_recv,
    ph5_send,
    ph5_recv,
    grads,
    swap,
    half,
    far,
    near,
    near_in,
    deep,
    deep_in,
    plane,
    plane_in,
    last,
    fan,
    out_sem,
    rs1_send,
    rs1_recv,
    rs2_send,
    rs2_recv,
    rs3_send,
    rs3_recv,
    rs4_send,
    rs4_recv,
    rs5_send,
    rs5_recv,
    rs6_send,
    rs6_recv,
    rs7_send,
    rs7_recv,
):
    d = lax.axis_index("dp")
    r = lax.axis_index("rows")
    zh, y, c, zl, x = place()
    slot = y * 2 + c
    peers = [(d, (r + k) % 8) for k in range(1, 8)]
    plane_peers = []
    for k in range(1, 8):
        s = (slot + k) % 8
        plane_peers.append(device_of(zh, s // 2, s % 2, zl, x))
    z_peers = [device_of((zh + k) % 4, y, c, zl, x) for k in range(1, 4)]
    x_peers = [device_of(zh, y, c, zl, (x + k) % 4) for k in range(1, 4)]
    y_peers = [device_of(zh, (y + k) % 4, c, zl, x) for k in range(1, 4)]
    partner = device_of(zh, y, 1 - c, zl, x)
    other_z = device_of(zh, y, c, 1 - zl, x)
    greet(peers + plane_peers + z_peers)
    before = (d, (r + 7) % 8)
    after = (d, (r + 1) % 8)
    waiting = []

    def send_rows(event, top, bottom, above, below):
        first = remote(top, below, halo_send.at[event, 0], halo_recv.at[event, 0], before)
        second = remote(bottom, above, halo_send.at[event, 1], halo_recv.at[event, 1], after)
        first.start()
        second.start()
        waiting.extend([first, second])
        return (first, second)

    def arrive(pair):
        pair[0].wait_recv()
        pair[1].wait_recv()

    raw = send_rows(
        0, acts.at[0:2, :, 0:128], acts.at[0:2, :, 128:256], halo.at[0, 0:2], halo.at[1, 0:2]
    )
    first = []
    for k in range(7):
        s = (slot + k + 1) % 8
        first.append(remote(src.at[s], parts.at[slot], ph1_send.at[k], ph1_recv.at[k], plane_peers[k]))
        first[-1].start()
    waiting.extend(first)
    mine = pltpu.make_async_copy(src.at[slot], parts.at[slot], own_sem.at[4])
    mine.start()
    load_one = pltpu.make_async_copy(enc_one_hbm, enc_one, enc_sem.at[0])
    load_two = pltpu.make_async_copy(enc_two_hbm, enc_two, enc_sem.at[1])
    load_one.start()
    load_two.start()

    second = {}
    third = {}
    fourth = {}
    fifth = {}
    held = {}

    def gather_z():
        mine.wait()
        for copy in first:
            copy.wait_recv()
        for s in range(8):
            column[10 * s : 10 * s + 10, :] = parts[s, 0:10, :].astype(F32)
        home = pl.multiple_of(zh * 80, 16)
        gath[pl.ds(home, 80), :] = column[...].astype(BF)
        for g in range(4):
            block = gath.at[pl.ds(home, 80), 128 * g : 128 * g + 128]
            second[g] = []
            for k in (0, 2, 1):
                second[g].append(remote(block, block, ph2_send.at[g, k], ph2_recv.at[g, k], z_peers[k]))
                second[g][-1].start()
            waiting.extend(second[g])

    def gather_x(g):
        for copy in second[g]:
            copy.wait_recv()
        block = gath.at[:, 128 * g : 128 * g + 128]
        spot = weights.at[:, lanes_at(g * 4096 + (slot * 4 + x) * 128, 128)]
        third[g] = []
        for k in (0, 2, 1):
            third[g].append(remote(block, spot, ph3_send.at[g, k], ph3_recv.at[g, k], x_peers[k]))
            third[g][-1].start()
        waiting.extend(third[g])
        held[g] = pltpu.make_async_copy(block, spot, own_sem.at[g])
        held[g].start()

    def column_of(g, steps, at, size):
        return weights.at[:, lanes_at(g * 4096 + ((y + 4 + steps) % 4 * 2 + c) * 512 + at, size)]

    def to_partner(g, k, steps):
        block = column_of(g, steps, 0, 512)
        copy = remote(block, block, ph5_send.at[g, k], ph5_recv.at[g, k], partner)
        copy.start()
        fifth[g].append(copy)
        waiting.append(copy)

    def gather_y_start(g):
        held[g].wait()
        for copy in third[g]:
            copy.wait_recv()
        block = column_of(g, 0, 0, 512)
        fourth[g] = [
            remote(block, block, ph4_send.at[g, 0], ph4_recv.at[g, 0], y_peers[0]),
            remote(block, block, ph4_send.at[g, 1], ph4_recv.at[g, 1], y_peers[2]),
        ]
        for copy in fourth[g]:
            copy.start()
        waiting.extend(fourth[g])
        fifth[g] = []
        to_partner(g, 0, 0)

    def gather_y_relay(g):
        fourth[g][0].wait_recv()
        block = column_of(g, -1, 0, 256)
        up = remote(block, block, ph4_send.at[g, 2], ph4_recv.at[g, 2], y_peers[0])
        up.start()
        fourth[g][1].wait_recv()
        block = column_of(g, 1, 256, 256)
        down = remote(block, block, ph4_send.at[g, 3], ph4_recv.at[g, 3], y_peers[2])
        down.start()
        fourth[g].extend([up, down])
        waiting.extend([up, down])
        to_partner(g, 1, -1)
        to_partner(g, 2, 1)

    def gather_y_finish(g):
        fourth[g][2].wait_recv()
        fourth[g][3].wait_recv()
        to_partner(g, 3, 2)

    def gather_done(g):
        for copy in fifth[g]:
            copy.wait_recv()


    lane = lax.broadcasted_iota(jnp.int32, (C, 128), 1)
    channel = lax.broadcasted_iota(jnp.int32, (C, 128), 0)
    in_ten = (channel >= 10 * lane) & (channel < 10 * lane + 10)
    other = lane - 32
    in_twenty = (channel >= 20 * other) & (channel < 20 * other + 20)
    ten[...] = jnp.where(in_ten, 1.0, 0.0)
    twenty[...] = jnp.where(in_twenty, 1.0, 0.0)
    member[...] = ten[...] + twenty[...]
    cols[...] = jnp.zeros((C, 128), F32)

    def share(turn):
        sums = lax.dot_general(cols[...], member[...], TN, precision=EXACT, preferred_element_type=F32)
        note[turn] = sums[0:8]
        copies = []
        for k in range(1, 8):
            copies.append(
                remote(
                    note.at[turn],
                    note_in.at[turn, k - 1],
                    note_send.at[turn, k - 1],
                    note_recv.at[turn, k - 1],
                    peers[k - 1],
                )
            )
            copies[-1].start()
        waiting.extend(copies)
        return copies

    def collect(turn, copies):
        for copy in copies:
            copy.wait_recv()
        total = note[turn]
        for k in range(7):
            total = total + note_in[turn, k]
        return total

    which = lax.broadcasted_iota(jnp.int32, (8, 128), 1)
    per_group = jnp.where(which < 32, 1.0 / (10 * 2048), 1.0 / (20 * 2048))

    def spread(table, at, rows):
        padded = jnp.concatenate(rows + [jnp.zeros((8 - len(rows), 128), F32)], axis=0)
        coef[:, at : at + 8] = lax.dot_general(
            table[...], padded, NT, precision=EXACT, preferred_element_type=F32
        )

    def norm_rows(total, k):
        mean = total[k : k + 1] * per_group[0:1]
        square = total[k + 1 : k + 2] * per_group[0:1]
        return [mean, lax.rsqrt(square - mean * mean + EPSILON)]

    def mean_rows(total, k):
        return [total[k : k + 1] * per_group[0:1], total[k + 1 : k + 2] * per_group[0:1]]

    has_up = r > 0
    has_down = r < 7

    def masked(strips):
        return [
            jnp.where(has_up, strips[0], 0.0),
            strips[1],
            strips[2],
            jnp.where(has_down, strips[3], 0.0),
        ]

    @pl.loop(0, STEPS)
    def _(i):
        latent = acts[0, band(i), :].astype(F32)
        ctl_in = (latent + acts[1, band(i), :].astype(F32)).astype(BF).astype(F32)
        under = acts[2, band(i), :].astype(F32)
        put_sums(cols, 0, i, [latent, latent * latent, ctl_in, ctl_in * ctl_in, under, under * under])

    first_note = share(0)
    gather_z()
    late = send_rows(1, acts.at[2, :, 0:128], acts.at[2, :, 128:256], halo.at[0, 2], halo.at[1, 2])
    for target in (back_dec_two, back_dec_one, back_ctl_two):
        for tap in range(9):
            target[:, 384 * tap + 320 : 384 * tap + 384] = jnp.zeros((C, 64), BF)
    for tap in range(9):
        col_g[384 * tap + 320 : 384 * tap + 384, :] = jnp.zeros((64, 256), BF)
    grads[0, :, 2816:HALF] = jnp.zeros((C, HALF - 2816), BF)
    grads[0, 160:C, :] = jnp.zeros((160, HALF), BF)
    grads[1, :, 2816:HALF] = jnp.zeros((C, HALF - 2816), BF)
    grads[1, 160:C, :] = jnp.zeros((160, HALF), BF)

    def turn(target, start, stride):
        for tap in range(9):
            block = weights[:, start + stride * tap : start + stride * tap + 320].astype(F32)
            target[:, 384 * (8 - tap) : 384 * (8 - tap) + 320] = block.T.astype(BF)

    def turn_square(target, start):
        target[...] = weights[:, start : start + 320].astype(F32).T.astype(BF)

    total = collect(0, first_note)
    spread(ten, 0, norm_rows(total, 0) + norm_rows(total, 2))
    spread(twenty, 8, norm_rows(total, 4))
    arrive(raw)

    def plain(tap):
        return 320 * tap

    def first_act(source_of, at, col, base_of):
        @pl.loop(0, STEPS)
        def _(i):
            mean = coef[band(i), at : at + 1]
            inv = coef[band(i), at + 1 : at + 2]
            strips = []
            for strip in source_of(i):
                normed = (strip - mean) * inv
                strips.append(normed * sig(normed))
            put_columns(col, base_of, i, masked(strips))

    def latent_of(i):
        own = acts[0, band(i), :].astype(F32)
        return [halo[0, 0, band(i), :].astype(F32), own[:, 0:128], own[:, 128:256], halo[1, 0, band(i), :].astype(F32)]

    def ctl_in_of(i):
        own = acts[1, band(i), :].astype(F32)
        hint = [halo[0, 1, band(i), :].astype(F32), own[:, 0:128], own[:, 128:256], halo[1, 1, band(i), :].astype(F32)]
        return [(a + b).astype(BF).astype(F32) for a, b in zip(latent_of(i), hint)]

    gather_x(0)
    first_act(latent_of, 0, col_t, plain)
    load_one.wait()
    enc_raw[...] = taps_dot(enc_one, col_t)
    edge[0] = enc_raw[:, 0:128].astype(BF)
    edge[1] = enc_raw[:, 128:256].astype(BF)
    enc_rows = send_rows(3, edge.at[0], edge.at[1], inner_halo.at[0], inner_halo.at[1])

    @pl.loop(0, STEPS)
    def _(i):
        enc = enc_raw[band(i), :] + terms[band(i), 0:1]
        put_sums(cols, 0, i, [enc, enc * enc])

    second_note = share(1)
    gather_x(1)
    first_act(ctl_in_of, 2, col_a, plain)
    gather_y_start(0)

    def under_of(i):
        own = acts[2, band(i), :].astype(F32)
        return [halo[0, 2, band(i), :].astype(F32), own[:, 0:128], own[:, 128:256], halo[1, 2, band(i), :].astype(F32)]

    def joined_low(tap):
        return 640 * tap

    def joined_high(tap):
        return 640 * tap + 320

    def spaced(tap):
        return 384 * tap

    arrive(late)
    first_act(under_of, 8, col_d, joined_low)

    total = collect(1, second_note)
    spread(ten, 16, norm_rows(total, 0))

    def second_act(raw_ref, at_halo, term_at, at, col, keep):
        @pl.loop(0, STEPS)
        def _(i):
            mean = coef[band(i), at : at + 1]
            inv = coef[band(i), at + 1 : at + 2]
            own = raw_ref[band(i), :]
            term = terms[band(i), term_at : term_at + 1]
            strips = []
            for strip in (
                inner_halo[at_halo, band(i), :].astype(F32),
                own[:, 0:128],
                own[:, 128:256],
                inner_halo[at_halo + 1, band(i), :].astype(F32),
            ):
                strips.append((strip + term - mean) * inv)
            if keep is not None:
                keep[band(i), 0:128] = strips[1]
                keep[band(i), 128:256] = strips[2]
            put_columns(col, plain, i, masked([v * sig(v) for v in strips]))

    arrive(enc_rows)
    second_act(enc_raw, 0, 0, 16, col_t, None)
    load_two.wait()
    enc_raw[...] = taps_dot(enc_two, col_t)
    gather_y_relay(0)
    gather_y_start(1)
    gather_x(2)
    gather_y_finish(0)
    gather_done(0)
    ctl_raw[...] = dot(weights[:, AT_CTL_ONE : AT_CTL_ONE + 2880], col_a[...])
    edge[2] = ctl_raw[:, 0:128].astype(BF)
    edge[3] = ctl_raw[:, 128:256].astype(BF)
    ctl_rows = send_rows(4, edge.at[2], edge.at[3], inner_halo.at[2], inner_halo.at[3])

    @pl.loop(0, STEPS)
    def _(i):
        ctl = ctl_raw[band(i), :] + terms[band(i), 1:2]
        put_sums(cols, 0, i, [ctl, ctl * ctl])

    ctl_note = share(2)
    gather_y_relay(1)
    gather_y_start(2)
    gather_x(3)
    total = collect(2, ctl_note)
    spread(ten, 64, norm_rows(total, 0))
    arrive(ctl_rows)
    second_act(ctl_raw, 2, 1, 64, col_b, keep_n)
    gather_y_finish(1)
    gather_done(1)
    inner[...] = dot(weights[:, AT_CTL_TWO : AT_CTL_TWO + 2880], col_b[...])

    @pl.loop(0, STEPS)
    def _(i):
        latent = acts[0, band(i), :].astype(F32)
        ctl_in = (latent + acts[1, band(i), :].astype(F32)).astype(BF).astype(F32)
        ctl_out[band(i), :] = (ctl_in + inner[band(i), :]).astype(BF)

    inner[...] = dot(weights[:, AT_ZERO : AT_ZERO + 320], ctl_out[...])

    @pl.loop(0, STEPS)
    def _(i):
        latent = acts[0, band(i), :].astype(F32)
        enc_out = (latent + enc_raw[band(i), :]).astype(BF).astype(F32)
        joined = (enc_out + inner[band(i), :]).astype(BF)
        skip[0, band(i), :] = joined[:, 0:128]
        skip[1, band(i), :] = joined[:, 128:256]
        value = joined.astype(F32)
        put_sums(cols, 0, i, [value, value * value])

    skip_rows = send_rows(5, skip.at[0], skip.at[1], skip_halo.at[0], skip_halo.at[1])
    third_note = share(3)
    late_cot = send_rows(2, acts.at[3], acts.at[3], halo_cot.at[0], halo_cot.at[1])
    gather_y_relay(2)
    gather_y_start(3)
    turn(back_ctl_two, AT_CTL_TWO, 320)
    turn_square(zero_t, AT_ZERO)

    total = collect(3, third_note)
    spread(twenty, 24, norm_rows(total, 0))
    arrive(skip_rows)

    @pl.loop(0, STEPS)
    def _(i):
        mean = coef[band(i), 24:25]
        inv = coef[band(i), 25:26]
        strips = []
        for k, strip in enumerate(
            (skip_halo[0, band(i), :], skip[0, band(i), :], skip[1, band(i), :], skip_halo[1, band(i), :])
        ):
            normed = (strip.astype(F32) - mean) * inv
            keep_skip[band(i), 128 * k : 128 * k + 128] = normed
            strips.append(normed * sig(normed))
        put_columns(col_d, joined_high, i, masked(strips))

    gather_y_finish(2)
    gather_done(2)
    dec_raw[...] = dot(weights[:, AT_DEC_ONE : AT_DEC_ONE + 5760], col_d[...])
    dec_edge[0] = dec_raw[:, 0:128].astype(BF)
    dec_edge[1] = dec_raw[:, 128:256].astype(BF)
    dec_rows = send_rows(6, dec_edge.at[0], dec_edge.at[1], dec_halo.at[0], dec_halo.at[1])

    @pl.loop(0, STEPS)
    def _(i):
        value = dec_raw[band(i), :] + terms[band(i), 2:3]
        put_sums(cols, 0, i, [value, value * value])

    fourth_note = share(4)
    turn(back_dec_one, AT_DEC_ONE + 320, 640)
    gather_y_relay(3)
    gather_y_finish(3)
    arrive(late_cot)
    scale = 2.0**-8

    def cot_of(i):
        far = halo_cot[0, band(i), :].astype(F32)
        own = acts[3, band(i), :].astype(F32)
        near = halo_cot[1, band(i), :].astype(F32)
        far = jnp.where(has_up, far, 0.0) * scale
        near = jnp.where(has_down, near, 0.0) * scale
        own = own * scale
        return [far[:, 0:128], far[:, 128:256], own[:, 0:128], own[:, 128:256], near[:, 0:128], near[:, 128:256]]

    gather_done(3)
    turn(back_dec_two, AT_DEC_TWO, 320)
    turn_square(short_t, AT_SHORT)
    for part in range(2):

        @pl.loop(0, STEPS)
        def _(i):
            strips = cot_of(i)[2 * part : 2 * part + 4]
            put_columns(col_g, spaced, i, strips)

        up_grad[:, 256 * part : 256 * part + 256] = dot(back_dec_two[...], col_g[...])

    @pl.loop(0, STEPS)
    def _(i):
        for k, strip in enumerate(cot_of(i)[1:5]):
            wide[band(i), 128 * k : 128 * k + 128] = strip.astype(BF)

    mixed[...] = dot(short_t[...], wide[...])

    total = collect(4, fourth_note)
    spread(ten, 32, norm_rows(total, 0))

    def keep_dec_rows(i, strip, k):
        mean = coef[band(i), 32:33]
        inv = coef[band(i), 33:34]
        term = terms[band(i), 2:3]
        normed = (strip + term - mean) * inv
        keep_dec[band(i), 128 * k : 128 * k + 128] = normed
        upstream = up_grad[band(i), 128 * k : 128 * k + 128] * slope(normed)
        up_grad[band(i), 128 * k : 128 * k + 128] = upstream
        return (normed, upstream)

    @pl.loop(0, STEPS)
    def _(i):
        one_n, one_g = keep_dec_rows(i, dec_raw[band(i), 0:128], 1)
        two_n, two_g = keep_dec_rows(i, dec_raw[band(i), 128:256], 2)
        put_sums(cols, 0, i, [one_g + two_g, one_g * one_n + two_g * two_n])

    fifth_note = share(5)
    arrive(dec_rows)

    @pl.loop(0, STEPS)
    def _(i):
        keep_dec_rows(i, dec_halo[0, band(i), :].astype(F32), 0)
        keep_dec_rows(i, dec_halo[1, band(i), :].astype(F32), 3)

    total = collect(5, fifth_note)
    spread(ten, 40, mean_rows(total, 0))

    @pl.loop(0, STEPS)
    def _(i):
        inv = coef[band(i), 33:34]
        mean = coef[band(i), 40:41]
        cross = coef[band(i), 41:42]
        strips = []
        for k in range(4):
            lanes = slice(128 * k, 128 * k + 128)
            strips.append(inv * (up_grad[band(i), lanes] - mean - keep_dec[band(i), lanes] * cross))
        put_columns(col_g, spaced, i, masked(strips))

    sfg[...] = dot(back_dec_one[...], col_g[...])
    sfg_edge[0] = sfg[:, 0:128].astype(BF)
    sfg_edge[1] = sfg[:, 128:256].astype(BF)
    sfg_rows = send_rows(7, sfg_edge.at[0], sfg_edge.at[1], sfg_halo.at[0], sfg_halo.at[1])

    @pl.loop(0, STEPS)
    def _(i):
        normed = keep_skip[band(i), 128:384]
        value = sfg[band(i), :] * slope(normed)
        up_grad[band(i), 128:384] = value
        put_sums(cols, 0, i, [value, value * normed])

    sixth_note = share(6)
    arrive(sfg_rows)

    @pl.loop(0, STEPS)
    def _(i):
        for at, lanes in ((0, slice(0, 128)), (1, slice(384, 512))):
            up_grad[band(i), lanes] = sfg_halo[at, band(i), :].astype(F32) * slope(keep_skip[band(i), lanes])

    total = collect(6, sixth_note)
    spread(twenty, 48, mean_rows(total, 0))

    @pl.loop(0, STEPS)
    def _(i):
        inv = coef[band(i), 25:26]
        mean = coef[band(i), 48:49]
        cross = coef[band(i), 49:50]
        value = inv * (up_grad[band(i), :] - mean - keep_skip[band(i), :] * cross) + mixed[band(i), :]
        wide[band(i), :] = value.astype(BF)

    up_grad[...] = dot(zero_t[...], wide[...])

    @pl.loop(0, STEPS)
    def _(i):
        strips = []
        for k in range(4):
            strips.append(up_grad[band(i), 128 * k : 128 * k + 128].astype(BF).astype(F32))
        wide_two[band(i), 0:128] = strips[1].astype(BF)
        wide_two[band(i), 128:256] = strips[2].astype(BF)
        put_columns(col_g, spaced, i, masked(strips))

    sfg[...] = dot(back_ctl_two[...], col_g[...])

    @pl.loop(0, STEPS)
    def _(i):
        normed = keep_n[band(i), :]
        value = sfg[band(i), :] * slope(normed)
        sfg[band(i), :] = value
        put_sums(cols, 0, i, [value, value * normed])

    seventh_note = share(7)

    def store_grads(k, value, at):
        count = value.shape[1]
        grads[k, 0:160, at : at + count] = value[0:160].astype(BF)
        for start in range(0, count, 128):
            tile = (at + start) // 128
            spot = (tile // 16 * 16 + tile % 4 * 4 + tile // 4 % 4) * 128
            size = min(128, count - start)
            grads[k, 160:C, spot : spot + size] = value[160:C, start : start + size].astype(BF)

    swaps = {}
    pairs = {}
    fours = {}

    def reduce_core(k):
        swaps[k] = remote(
            grads.at[k, :, lanes_at((1 - c) * 2048, 2048)], swap.at[k], rs1_send.at[k], rs1_recv.at[k], partner
        )
        swaps[k].start()
        waiting.append(swaps[k])

    def reduce_far(k):
        swaps[k].wait_recv()

        @pl.loop(0, STEPS)
        def _(i):
            total = grads[k, band(i), lanes_at(c * 2048, 2048)].astype(F32) + swap[k, band(i), :].astype(F32)
            half[k, band(i), :] = total.astype(BF)

        pairs[k] = []
        for j in (1, 3, 2):
            ya = (y + j) % 4
            xb = (x + j) % 4
            pairs[k].append(
                remote(
                    half.at[k, 0:160, lanes_at(ya * 512, 512)],
                    far.at[k, 0, j - 1],
                    rs2_send.at[k, 0, j - 1],
                    rs2_recv.at[k, 0, j - 1],
                    y_peers[j - 1],
                )
            )
            pairs[k].append(
                remote(
                    half.at[k, 160:C, lanes_at(xb * 512, 512)],
                    far.at[k, 1, j - 1],
                    rs2_send.at[k, 1, j - 1],
                    rs2_recv.at[k, 1, j - 1],
                    x_peers[j - 1],
                )
            )
        for copy in pairs[k]:
            copy.start()
        waiting.extend(pairs[k])

    def reduce_near(k):
        for copy in pairs[k]:
            copy.wait_recv()

        @pl.loop(0, STEPS // 2)
        def _(i):
            for which, where in ((0, y), (1, x)):
                rows = pl.ds(pl.multiple_of(160 * which + i * ROWS, ROWS), ROWS)
                total = half[k, rows, lanes_at(where * 512, 512)].astype(F32)
                for j in range(3):
                    total = total + far[k, which, j, band(i), :].astype(F32)
                near[k, which, band(i), :] = total.astype(BF)

        fours[k] = []
        for j in (1, 3, 2):
            xa = (x + j) % 4
            yb = (y + j) % 4
            fours[k].append(
                remote(
                    near.at[k, 0, :, lanes_at(xa * 128, 128)],
                    near_in.at[k, 0, j - 1],
                    rs3_send.at[k, 0, j - 1],
                    rs3_recv.at[k, 0, j - 1],
                    x_peers[j - 1],
                )
            )
            fours[k].append(
                remote(
                    near.at[k, 1, :, lanes_at(yb * 128, 128)],
                    near_in.at[k, 1, j - 1],
                    rs3_send.at[k, 1, j - 1],
                    rs3_recv.at[k, 1, j - 1],
                    y_peers[j - 1],
                )
            )
        for copy in fours[k]:
            copy.start()
        waiting.extend(fours[k])

    def reduce_deep(k):
        for copy in fours[k]:
            copy.wait_recv()
        for which, where in ((0, x), (1, y)):
            total = near[k, which, :, lanes_at(where * 128, 128)].astype(F32)
            for j in range(3):
                total = total + near_in[k, which, j].astype(F32)
            deep[160 * which : 160 * which + 160, 128 * k : 128 * k + 128] = total.astype(BF)

    two_value = lax.dot_general(wide_two[...], col_b[...], NT, preferred_element_type=F32)
    store_grads(0, two_value, 0)
    zero_value = lax.dot_general(wide[:, 128:384], ctl_out[...], NT, preferred_element_type=F32)
    store_grads(0, zero_value, 2944)
    reduce_core(0)
    total = collect(7, seventh_note)
    spread(ten, 56, mean_rows(total, 0))

    @pl.loop(0, STEPS)
    def _(i):
        inv = coef[band(i), 65:66]
        mean = coef[band(i), 56:57]
        cross = coef[band(i), 57:58]
        value = inv * (sfg[band(i), :] - mean - keep_n[band(i), :] * cross)
        wide_two[band(i), :] = value.astype(BF)

    reduce_far(0)
    one_value = lax.dot_general(wide_two[...], col_a[...], NT, preferred_element_type=F32)
    store_grads(1, one_value, 0)
    reduce_core(1)
    reduce_far(1)
    reduce_near(0)
    reduce_near(1)
    reduce_deep(0)
    reduce_deep(1)
    ring = []
    for k in (0, 2, 1):
        zt = (zh + k + 1) % 4
        ring.append(
            remote(
                deep.at[pl.ds(pl.multiple_of(zt * 80, 16), 80)],
                deep_in.at[k],
                rs4_send.at[k],
                rs4_recv.at[k],
                z_peers[k],
            )
        )
        ring[-1].start()
    for copy in ring:
        copy.wait_recv()
    total = deep[pl.ds(pl.multiple_of(zh * 80, 16), 80), :].astype(F32)
    for k in range(3):
        total = total + deep_in[k].astype(F32)
    plane[...] = total
    cross = remote(plane, plane_in, rs5_send.at[0], rs5_recv.at[0], other_z)
    cross.start()
    cross.wait_recv()
    last[...] = plane[...] + plane_in[...]
    for s in range(8):
        fan[s, 0:10, :] = last[10 * s : 10 * s + 10, :]
        fan[s, 10:16, :] = jnp.zeros((6, 256), F32)
    sixth = []
    for k in range(7):
        s = (slot + k + 1) % 8
        sixth.append(remote(fan.at[s], out.at[x, slot], rs6_send.at[k], rs6_recv.at[k], plane_peers[k]))
        sixth[-1].start()
    mine = pltpu.make_async_copy(fan.at[slot], out.at[x, slot], out_sem.at[0])
    mine.start()
    mine.wait()
    for copy in sixth:
        copy.wait_recv()
    seventh = []
    for k in range(3):
        seventh.append(remote(out.at[x], out.at[x], rs7_send.at[k], rs7_recv.at[k], x_peers[k]))
        seventh[-1].start()
    for copy in seventh:
        copy.wait_recv()
    for copy in waiting + ring + [cross] + sixth + seventh:
        copy.wait_send()


def run_step(shard, acts, terms, enc_one, enc_two):
    x = lax.axis_index("rows") % 4
    pieces = shard.reshape(10, 4, 4, 2, 4, 128)
    pieces = lax.dynamic_index_in_dim(pieces, x, 4, keepdims=False)
    pieces = jnp.transpose(pieces, (2, 3, 0, 1, 4)).reshape(8, 10, 512)
    pieces = jnp.pad(pieces, ((0, 0), (0, 6), (0, 0)))
    dma = pltpu.SemaphoreType.DMA
    whole = pl.BlockSpec(memory_space=pltpu.VMEM)
    far_off = pl.BlockSpec(memory_space=pl.ANY)
    return pl.pallas_call(
        step_kernel,
        out_shape=jax.ShapeDtypeStruct((4, 8, 16, 256), F32),
        in_specs=[whole, whole, whole, far_off, far_off],
        out_specs=whole,
        scratch_shapes=[
            pltpu.VMEM((C, 128), F32),
            pltpu.VMEM((C, 128), F32),
            pltpu.VMEM((C, 128), F32),
            pltpu.VMEM((C, 128), F32),
            pltpu.VMEM((C, 128), F32),
            pltpu.VMEM((2, 3, C, 128), BF),
            pltpu.VMEM((2, C, 256), BF),
            pltpu.VMEM((C, 256), F32),
            pltpu.VMEM((4, C, 128), BF),
            pltpu.VMEM((4, C, 128), BF),
            pltpu.VMEM((2880, 256), BF),
            pltpu.VMEM((2880, 256), BF),
            pltpu.VMEM((2880, 256), BF),
            pltpu.VMEM((5760, 256), BF),
            pltpu.VMEM((3456, 256), BF),
            pltpu.VMEM((C, 3456), BF),
            pltpu.VMEM((C, 3456), BF),
            pltpu.VMEM((C, 3456), BF),
            pltpu.VMEM((C, C), BF),
            pltpu.VMEM((C, C), BF),
            pltpu.VMEM((C, 256), F32),
            pltpu.VMEM((C, 256), F32),
            pltpu.VMEM((C, 256), BF),
            pltpu.VMEM((2, C, 128), BF),
            pltpu.VMEM((2, C, 128), BF),
            pltpu.VMEM((C, 256), F32),
            pltpu.VMEM((2, C, 128), BF),
            pltpu.VMEM((2, C, 128), BF),
            pltpu.VMEM((C, 512), F32),
            pltpu.VMEM((C, 256), F32),
            pltpu.VMEM((2, C, 128), BF),
            pltpu.VMEM((2, C, 128), BF),
            pltpu.VMEM((C, 256), F32),
            pltpu.VMEM((C, 512), F32),
            pltpu.VMEM((C, 512), F32),
            pltpu.VMEM((C, 512), F32),
            pltpu.VMEM((C, 512), BF),
            pltpu.VMEM((C, 256), BF),
            pltpu.VMEM((8, 8, 128), F32),
            pltpu.VMEM((8, 7, 8, 128), F32),
            dma((8, 7)),
            dma((8, 7)),
            dma((8, 2)),
            dma((8, 2)),
            pltpu.VMEM((9, C, C), BF),
            pltpu.VMEM((9, C, C), BF),
            dma((2,)),
            pltpu.VMEM((C, LANES), BF),
            pltpu.VMEM((8, 16, 512), BF),
            pltpu.VMEM((80, 512), F32),
            pltpu.VMEM((C, 512), BF),
            dma((5,)),
            dma((7,)),
            dma((7,)),
            dma((4, 3)),
            dma((4, 3)),
            dma((4, 3)),
            dma((4, 3)),
            dma((4, 4)),
            dma((4, 4)),
            dma((4, 4)),
            dma((4, 4)),
            pltpu.VMEM((2, C, HALF), BF),
            pltpu.VMEM((2, C, 2048), BF),
            pltpu.VMEM((2, C, 2048), BF),
            pltpu.VMEM((2, 2, 3, 160, 512), BF),
            pltpu.VMEM((2, 2, 160, 512), BF),
            pltpu.VMEM((2, 2, 3, 160, 128), BF),
            pltpu.VMEM((C, 256), BF),
            pltpu.VMEM((3, 80, 256), BF),
            pltpu.VMEM((80, 256), F32),
            pltpu.VMEM((80, 256), F32),
            pltpu.VMEM((80, 256), F32),
            pltpu.VMEM((8, 16, 256), F32),
            dma((1,)),
            dma((2,)),
            dma((2,)),
            dma((2, 2, 3)),
            dma((2, 2, 3)),
            dma((2, 2, 3)),
            dma((2, 2, 3)),
            dma((3,)),
            dma((3,)),
            dma((1,)),
            dma((1,)),
            dma((7,)),
            dma((7,)),
            dma((3,)),
            dma((3,)),
        ],
        compiler_params=pltpu.CompilerParams(
            collective_id=0, has_side_effects=True, vmem_limit_bytes=63 * 1024 * 1024
        ),
        name="train_step",
    )(pieces, acts, terms, enc_one, enc_two)


def flat(kernel, width):
    kernel = kernel.reshape(kernel.shape[0], -1)
    return jnp.pad(kernel, ((0, 0), (0, width - kernel.shape[1])))


def per_device(
    latent,
    hint_field,
    from_below,
    cotangent,
    timesteps,
    time_weight,
    enc_proj,
    ctl_proj,
    dec_proj,
    enc_conv_one,
    enc_conv_two,
    ctl_conv_one,
    ctl_conv_two,
    dec_conv_one,
    dec_conv_two,
    dec_shortcut,
    zero_conv,
):
    shard = jnp.concatenate(
        [
            flat(ctl_conv_one, 2944),
            flat(ctl_conv_two, 2944),
            flat(zero_conv, 384),
            flat(dec_conv_one, 5760),
            flat(dec_shortcut[:, C:], 384),
            flat(dec_conv_two, LANES - AT_DEC_TWO),
        ],
        axis=1,
    )
    half_width = C // 2
    frequency = jnp.exp(-math.log(10000.0) * jnp.arange(half_width, dtype=jnp.float32) / half_width)
    angles = timesteps.astype(jnp.float32)[:, None] * frequency[None, :]
    sinusoid = jnp.concatenate([jnp.cos(angles), jnp.sin(angles)], axis=1).astype(jnp.bfloat16)
    time_embed = jnp.dot(sinusoid, time_weight, preferred_element_type=jnp.float32)
    time_act = jax.nn.silu(time_embed).astype(jnp.bfloat16)
    terms = jnp.concatenate(
        [jnp.dot(time_act, proj, preferred_element_type=jnp.float32) for proj in (enc_proj, ctl_proj, dec_proj)],
        axis=0,
    ).T
    terms = jnp.pad(terms, ((0, 0), (0, 5)))
    acts = jnp.stack([a.reshape(C, 256) for a in (latent, hint_field, from_below, cotangent)])
    enc_one = jnp.transpose(enc_conv_one, (1, 2, 0, 3)).reshape(9, C, C)
    enc_two = jnp.transpose(enc_conv_two, (1, 2, 0, 3)).reshape(9, C, C)
    pieces = run_step(shard, acts, terms, enc_one, enc_two)
    pieces = pieces[:, :, :10, :].reshape(4, 4, 2, 10, 2, 128)
    owned = jnp.transpose(pieces, (3, 4, 2, 1, 0, 5)).reshape(10, 2, HALF)
    return (
        owned[:, 1, :2880].reshape(10, 3, 3, C),
        owned[:, 0, :2880].reshape(10, 3, 3, C),
        owned[:, 0, 2944:3264],
    )


def solution(mesh):
    in_specs = (
        P("dp", None, "rows", None),
        P("dp", None, "rows", None),
        P("dp", None, "rows", None),
        P("dp", None, "rows", None),
        P("dp"),
        P(),
        P(),
        P(),
        P(),
        P(),
        P(),
        P("dp", None, None, None),
        P("dp", None, None, None),
        P("dp", None, None, None),
        P("dp", None, None, None),
        P("dp", None),
        P("dp", None),
    )
    out_specs = (P("dp", None, None, None), P("dp", None, None, None), P("dp", None))
    return jax.shard_map(
        per_device, mesh=mesh, in_specs=in_specs, out_specs=out_specs, check_vma=False
    )
```

time: 261 us -> 201 us (0.77)
  Pallas kernels: 235 us -> 179 us
    pallas_call x3 -> x1, Pallas kernels: 235 us -> 179 us  [run_step(): pl.pallas_call(step_kernel, out_shape=jax.ShapeDtypeStruct((4, 8, 16, 256...]
    unnamed x32 -> x18, local copies, waits for them, and re-layouts: 7.1 us -> 1.43 us
    another operation x4, local copies, waits for them, and re-layouts: 0.44 us -> 4.32 us  [per_device(): jnp.stack([a.reshape(C, 256) for a in (latent, hint_field, from_below, co...]
    reshape x6 -> x4, local copies, waits for them, and re-layouts: 5.37 us -> 4.15 us  [flat(): kernel = kernel.reshape(kernel.shape[0], -1)]
where the time goes in v3:
time: 201 us; the launch traced here: 200 us
  Pallas kernels  179 us (89%)
  local copies, waits for them, and re-layouts  16.7 us (8%)
  other arithmetic  2.18 us (1%)
    pallas_call x1, Pallas kernels, run_step(): pl.pallas_call(step_kernel, out_shape=jax.ShapeDtypeStruct((4, 8, 16, 256...  179 us
    another operation x4, local copies, waits for them, and re-layouts, per_device(): jnp.stack([a.reshape(C, 256) for a in (latent, hint_field, from_below, co...  4.32 us
    reshape x4, local copies, waits for them, and re-layouts, flat(): kernel = kernel.reshape(kernel.shape[0], -1)  4.15 us

profile of v3, /device:TPU:1, one launch (start us, length us, event | category | flops | bytes accessed | tf_op | source)
XLA Modules:
  0.0 200.4 jit_solution(340890062452567571)
XLA Ops:
  0.6 0.0 copy-start
  0.7 1.1 reshape.70
  1.8 1.0 reshape.71
  2.8 0.7 constant_dynamic-update-slice_fusion.2
  3.5 1.0 reshape.72
  4.6 0.8 slice.15
  5.4 1.0 reshape.73
  6.4 0.2 reshape.74
  6.7 0.2 constant_dynamic-slice_fusion
  7.0 0.7 pad.31.src
  7.7 0.1 stack_reshape.15
  7.8 0.8 stack_reshape.14
  8.6 1.8 stack_reshape.13
  10.4 1.7 stack_reshape.12
  12.0 2.0 pad_maximum_fusion.acts
  14.7 0.1 sine_convert_fusion
  14.7 0.1 pad_maximum_fusion.2
  14.8 0.2 convolution_reduce_fusion
  15.1 0.3 fusion.2
  15.4 0.3 fusion.1
  15.7 0.3 fusion
  16.1 0.1 pad_maximum_fusion.1
  16.1 0.1 copy.31
  16.3 0.7 pad.32.terms
  17.0 178.8 %train_step.1 = f32[4,8,16,256]{3,2,1,0:T(8,128)} custom-call(bf16[8,16,512]{2,1,0:T(8,128)(2,1)} %pad.31.src, bf16[4,320,256]{2,1,0:T(8,128)(2,1)} %pad_maximum_fusion.acts, f32[320,8]{1,0:T(8,128)} %pad.32.terms, bf16[9,320,320]{2,1,0:T(8,128)(2,1)} %bitcast.29, bf16[9,320,320]{2,1,0:T(8,128)(2,1)} %bitcast.30), custom_call_target="tpu_custom_call" | custom-call | tf_op jit(solution)/shard_map/train_step/pallas_call | solution.py:902
  195.8 1.2 reshape.91
  197.0 0.2 copy.33
  197.2 0.2 reshape.79
  197.5 0.6 slice_reduce_fusion
  198.1 0.8 reshape_squeeze.6
  198.9 0.8 reshape_squeeze.7
  199.8 0.6 copy.40
  (23 shorter events, 0.3 us)
Async XLA Ops:
  0.6 14.2 %copy-start = (bf16[320,1280]{1,0:T(8,128)(2,1)S(1)}, bf16[320,1280]{1,0:T(8,128)(2,1)}, u32[]{:S(2)}) copy-start(bf16[320,1280]{1,0:T(8,128)(2,1)} %param.22) | copy-start | bytes 2457604
  0.6 7.0 %copy-start.4 = (bf16[1,320,2,128]{3,2,1,0:T(2,128)(2,1)S(1)}, bf16[1,320,2,128]{3,2,1,0:T(2,128)(2,1)}, u32[]{:S(2)}) copy-start(bf16[1,320,2,128]{3,2,1,0:T(2,128)(2,1)} %param.20) | copy-start | bytes 491524
  0.7 7.1 %copy-start.5 = (bf16[1,320,2,128]{3,2,1,0:T(2,128)(2,1)S(1)}, bf16[1,320,2,128]{3,2,1,0:T(2,128)(2,1)}, u32[]{:S(2)}) copy-start(bf16[1,320,2,128]{3,2,1,0:T(2,128)(2,1)} %param.19) | copy-start | bytes 491524
  6.9 8.2 %copy-start.1 = (bf16[1280,320]{0,1:T(8,128)(2,1)S(1)}, bf16[1280,320]{0,1:T(8,128)(2,1)}, u32[]{:S(2)}) copy-start(bf16[1280,320]{0,1:T(8,128)(2,1)} %param.25) | copy-start | bytes 2457604
  7.7 7.7 %copy-start.2 = (bf16[1280,320]{0,1:T(8,128)(2,1)S(1)}, bf16[1280,320]{0,1:T(8,128)(2,1)}, u32[]{:S(2)}) copy-start(bf16[1280,320]{0,1:T(8,128)(2,1)} %param.24) | copy-start | bytes 2457604
  8.6 7.1 %copy-start.3 = (bf16[1280,320]{0,1:T(8,128)(2,1)S(1)}, bf16[1280,320]{0,1:T(8,128)(2,1)}, u32[]{:S(2)}) copy-start(bf16[1280,320]{0,1:T(8,128)(2,1)} %param.23) | copy-start | bytes 2457604

commit v4 on v3

--- a/solution.py
+++ b/solution.py
@@ -55,7 +55,15 @@
 
 
 def band(i):
-    return pl.ds(pl.multiple_of(i * ROWS, ROWS), ROWS)
+    return slice(i * ROWS, i * ROWS + ROWS)
+
+
+def each(count):
+    def run(body):
+        for i in range(count):
+            body(i)
+
+    return run
 
 
 def put_columns(col, base_of, i, strips):
@@ -67,9 +75,9 @@
         shifted_of.append([left.astype(BF), strip.astype(BF), right.astype(BF)])
     for p in range(3):
         for q in range(3):
-            start = pl.multiple_of(base_of(3 * p + q) + i * ROWS, ROWS)
-            col[pl.ds(start, ROWS), 0:128] = shifted_of[p][q]
-            col[pl.ds(start, ROWS), 128:256] = shifted_of[p + 1][q]
+            start = base_of(3 * p + q) + i * ROWS
+            col[start : start + ROWS, 0:128] = shifted_of[p][q]
+            col[start : start + ROWS, 128:256] = shifted_of[p + 1][q]
 
 
 def sig(v):
@@ -98,12 +106,26 @@
 
 
 def step_kernel(
-    src,
-    acts,
-    terms,
+    sinus,
+    latent_ref,
+    hint_ref,
+    under_ref,
+    cot_ref,
+    shard_ctl_one,
+    shard_ctl_two,
+    shard_dec_one,
+    shard_dec_two,
+    shard_short,
+    shard_zero,
+    time_weight_hbm,
+    enc_proj_hbm,
+    ctl_proj_hbm,
+    dec_proj_hbm,
     enc_one_hbm,
     enc_two_hbm,
-    out,
+    one_out,
+    two_out,
+    zero_out,
     member,
     ten,
     twenty,
@@ -148,6 +170,11 @@
     note_recv,
     halo_send,
     halo_recv,
+    terms,
+    time_weight,
+    projections,
+    stage,
+    src,
     enc_one,
     enc_two,
     enc_sem,
@@ -171,13 +198,13 @@
     half,
     far,
     near,
+    passing,
     near_in,
     deep,
     deep_in,
-    plane,
-    plane_in,
     last,
     fan,
+    pool,
     out_sem,
     rs1_send,
     rs1_recv,
@@ -187,8 +214,6 @@
     rs3_recv,
     rs4_send,
     rs4_recv,
-    rs5_send,
-    rs5_recv,
     rs6_send,
     rs6_recv,
     rs7_send,
@@ -208,7 +233,63 @@
     y_peers = [device_of(zh, (y + k) % 4, c, zl, x) for k in range(1, 4)]
     partner = device_of(zh, y, 1 - c, zl, x)
     other_z = device_of(zh, y, c, 1 - zl, x)
-    greet(peers + plane_peers + z_peers)
+    z_all = [device_of((zh + k // 2) % 4, y, c, (zl + k) % 2, x) for k in range(1, 8)]
+    everyone = peers + plane_peers + z_all[1:]
+    barrier = pltpu.get_barrier_semaphore()
+    for where in everyone:
+        pl.semaphore_signal(barrier, inc=1, device_id=where, device_id_type=MESH)
+    loads = []
+    for k, (source, target) in enumerate(
+        (
+            (time_weight_hbm, time_weight),
+            (enc_proj_hbm, projections.at[0]),
+            (ctl_proj_hbm, projections.at[1]),
+            (dec_proj_hbm, projections.at[2]),
+            (enc_one_hbm, enc_one),
+            (enc_two_hbm, enc_two),
+        )
+    ):
+        loads.append(pltpu.make_async_copy(source, target, enc_sem.at[k]))
+        loads[-1].start()
+    load_one, load_two = loads[4:]
+
+    stage[...] = jnp.zeros((16, LANES), BF)
+    for kernel, start, count, width in (
+        (shard_ctl_one, AT_CTL_ONE, 9, C),
+        (shard_ctl_two, AT_CTL_TWO, 9, C),
+        (shard_dec_one, AT_DEC_ONE, 9, 2 * C),
+        (shard_dec_two, AT_DEC_TWO, 9, C),
+    ):
+        for tap in range(count):
+            stage[0:10, start + width * tap : start + width * tap + width] = kernel[tap]
+    stage[0:10, AT_ZERO : AT_ZERO + C] = shard_zero[...]
+    stage[0:10, AT_SHORT : AT_SHORT + C] = shard_short[:, C : 2 * C]
+    for s in range(8):
+        for g in range(4):
+            src[s, :, 128 * g : 128 * g + 128] = stage[:, lanes_at(g * 4096 + (s * 4 + x) * 128, 128)]
+
+    lane = lax.broadcasted_iota(jnp.int32, (C, 128), 1)
+    channel = lax.broadcasted_iota(jnp.int32, (C, 128), 0)
+    in_ten = (channel >= 10 * lane) & (channel < 10 * lane + 10)
+    other = lane - 32
+    in_twenty = (channel >= 20 * other) & (channel < 20 * other + 20)
+    ten[...] = jnp.where(in_ten, 1.0, 0.0)
+    twenty[...] = jnp.where(in_twenty, 1.0, 0.0)
+    member[...] = ten[...] + twenty[...]
+    cols[...] = jnp.zeros((C, 128), F32)
+
+    @each(STEPS)
+    def _(i):
+        sums = [0.0] * 6
+        for h in range(2):
+            latent = latent_ref[h, band(i), :].astype(F32)
+            ctl_in = (latent + hint_ref[h, band(i), :].astype(F32)).astype(BF).astype(F32)
+            under = under_ref[h, band(i), :].astype(F32)
+            for k, value in enumerate((latent, latent * latent, ctl_in, ctl_in * ctl_in, under, under * under)):
+                sums[k] = sums[k] + value
+        put_sums(cols, 0, i, sums)
+
+    pl.semaphore_wait(barrier, len(everyone))
     before = (d, (r + 7) % 8)
     after = (d, (r + 1) % 8)
     waiting = []
@@ -225,9 +306,8 @@
         pair[0].wait_recv()
         pair[1].wait_recv()
 
-    raw = send_rows(
-        0, acts.at[0:2, :, 0:128], acts.at[0:2, :, 128:256], halo.at[0, 0:2], halo.at[1, 0:2]
-    )
+    raw = send_rows(0, latent_ref.at[0], latent_ref.at[1], halo.at[0, 0], halo.at[1, 0])
+    raw_hint = send_rows(8, hint_ref.at[0], hint_ref.at[1], halo.at[0, 1], halo.at[1, 1])
     first = []
     for k in range(7):
         s = (slot + k + 1) % 8
@@ -236,10 +316,6 @@
     waiting.extend(first)
     mine = pltpu.make_async_copy(src.at[slot], parts.at[slot], own_sem.at[4])
     mine.start()
-    load_one = pltpu.make_async_copy(enc_one_hbm, enc_one, enc_sem.at[0])
-    load_two = pltpu.make_async_copy(enc_two_hbm, enc_two, enc_sem.at[1])
-    load_one.start()
-    load_two.start()
 
     second = {}
     third = {}
@@ -324,16 +400,6 @@
         for copy in fifth[g]:
             copy.wait_recv()
 
-
-    lane = lax.broadcasted_iota(jnp.int32, (C, 128), 1)
-    channel = lax.broadcasted_iota(jnp.int32, (C, 128), 0)
-    in_ten = (channel >= 10 * lane) & (channel < 10 * lane + 10)
-    other = lane - 32
-    in_twenty = (channel >= 20 * other) & (channel < 20 * other + 20)
-    ten[...] = jnp.where(in_ten, 1.0, 0.0)
-    twenty[...] = jnp.where(in_twenty, 1.0, 0.0)
-    member[...] = ten[...] + twenty[...]
-    cols[...] = jnp.zeros((C, 128), F32)
 
     def share(turn):
         sums = lax.dot_general(cols[...], member[...], TN, precision=EXACT, preferred_element_type=F32)
@@ -389,16 +455,16 @@
             jnp.where(has_down, strips[3], 0.0),
         ]
 
-    @pl.loop(0, STEPS)
-    def _(i):
-        latent = acts[0, band(i), :].astype(F32)
-        ctl_in = (latent + acts[1, band(i), :].astype(F32)).astype(BF).astype(F32)
-        under = acts[2, band(i), :].astype(F32)
-        put_sums(cols, 0, i, [latent, latent * latent, ctl_in, ctl_in * ctl_in, under, under * under])
-
     first_note = share(0)
     gather_z()
-    late = send_rows(1, acts.at[2, :, 0:128], acts.at[2, :, 128:256], halo.at[0, 2], halo.at[1, 2])
+    late = send_rows(1, under_ref.at[0], under_ref.at[1], halo.at[0, 2], halo.at[1, 2])
+    for load in loads[0:4]:
+        load.wait()
+    embed = dot(sinus[...], time_weight[...])
+    embed = (embed * sig(embed)).astype(BF)
+    for k in range(3):
+        term = lax.dot_general(projections[k], embed, NT, preferred_element_type=F32)
+        terms[:, k : k + 1] = term[:, 0:1]
     for target in (back_dec_two, back_dec_one, back_ctl_two):
         for tap in range(9):
             target[:, 384 * tap + 320 : 384 * tap + 384] = jnp.zeros((C, 64), BF)
@@ -421,12 +487,13 @@
     spread(ten, 0, norm_rows(total, 0) + norm_rows(total, 2))
     spread(twenty, 8, norm_rows(total, 4))
     arrive(raw)
+    arrive(raw_hint)
 
     def plain(tap):
         return 320 * tap
 
     def first_act(source_of, at, col, base_of):
-        @pl.loop(0, STEPS)
+        @each(STEPS)
         def _(i):
             mean = coef[band(i), at : at + 1]
             inv = coef[band(i), at + 1 : at + 2]
@@ -437,12 +504,20 @@
             put_columns(col, base_of, i, masked(strips))
 
     def latent_of(i):
-        own = acts[0, band(i), :].astype(F32)
-        return [halo[0, 0, band(i), :].astype(F32), own[:, 0:128], own[:, 128:256], halo[1, 0, band(i), :].astype(F32)]
+        return [
+            halo[0, 0, band(i), :].astype(F32),
+            latent_ref[0, band(i), :].astype(F32),
+            latent_ref[1, band(i), :].astype(F32),
+            halo[1, 0, band(i), :].astype(F32),
+        ]
 
     def ctl_in_of(i):
-        own = acts[1, band(i), :].astype(F32)
-        hint = [halo[0, 1, band(i), :].astype(F32), own[:, 0:128], own[:, 128:256], halo[1, 1, band(i), :].astype(F32)]
+        hint = [
+            halo[0, 1, band(i), :].astype(F32),
+            hint_ref[0, band(i), :].astype(F32),
+            hint_ref[1, band(i), :].astype(F32),
+            halo[1, 1, band(i), :].astype(F32),
+        ]
         return [(a + b).astype(BF).astype(F32) for a, b in zip(latent_of(i), hint)]
 
     gather_x(0)
@@ -453,7 +528,7 @@
     edge[1] = enc_raw[:, 128:256].astype(BF)
     enc_rows = send_rows(3, edge.at[0], edge.at[1], inner_halo.at[0], inner_halo.at[1])
 
-    @pl.loop(0, STEPS)
+    @each(STEPS)
     def _(i):
         enc = enc_raw[band(i), :] + terms[band(i), 0:1]
         put_sums(cols, 0, i, [enc, enc * enc])
@@ -464,8 +539,12 @@
     gather_y_start(0)
 
     def under_of(i):
-        own = acts[2, band(i), :].astype(F32)
-        return [halo[0, 2, band(i), :].astype(F32), own[:, 0:128], own[:, 128:256], halo[1, 2, band(i), :].astype(F32)]
+        return [
+            halo[0, 2, band(i), :].astype(F32),
+            under_ref[0, band(i), :].astype(F32),
+            under_ref[1, band(i), :].astype(F32),
+            halo[1, 2, band(i), :].astype(F32),
+        ]
 
     def joined_low(tap):
         return 640 * tap
@@ -483,7 +562,7 @@
     spread(ten, 16, norm_rows(total, 0))
 
     def second_act(raw_ref, at_halo, term_at, at, col, keep):
-        @pl.loop(0, STEPS)
+        @each(STEPS)
         def _(i):
             mean = coef[band(i), at : at + 1]
             inv = coef[band(i), at + 1 : at + 2]
@@ -516,7 +595,7 @@
     edge[3] = ctl_raw[:, 128:256].astype(BF)
     ctl_rows = send_rows(4, edge.at[2], edge.at[3], inner_halo.at[2], inner_halo.at[3])
 
-    @pl.loop(0, STEPS)
+    @each(STEPS)
     def _(i):
         ctl = ctl_raw[band(i), :] + terms[band(i), 1:2]
         put_sums(cols, 0, i, [ctl, ctl * ctl])
@@ -533,27 +612,30 @@
     gather_done(1)
     inner[...] = dot(weights[:, AT_CTL_TWO : AT_CTL_TWO + 2880], col_b[...])
 
-    @pl.loop(0, STEPS)
-    def _(i):
-        latent = acts[0, band(i), :].astype(F32)
-        ctl_in = (latent + acts[1, band(i), :].astype(F32)).astype(BF).astype(F32)
-        ctl_out[band(i), :] = (ctl_in + inner[band(i), :]).astype(BF)
+    @each(STEPS)
+    def _(i):
+        own = ctl_in_of(i)
+        ctl_out[band(i), 0:128] = (own[1] + inner[band(i), 0:128]).astype(BF)
+        ctl_out[band(i), 128:256] = (own[2] + inner[band(i), 128:256]).astype(BF)
 
     inner[...] = dot(weights[:, AT_ZERO : AT_ZERO + 320], ctl_out[...])
 
-    @pl.loop(0, STEPS)
-    def _(i):
-        latent = acts[0, band(i), :].astype(F32)
-        enc_out = (latent + enc_raw[band(i), :]).astype(BF).astype(F32)
-        joined = (enc_out + inner[band(i), :]).astype(BF)
-        skip[0, band(i), :] = joined[:, 0:128]
-        skip[1, band(i), :] = joined[:, 128:256]
-        value = joined.astype(F32)
-        put_sums(cols, 0, i, [value, value * value])
+    @each(STEPS)
+    def _(i):
+        sums = [0.0, 0.0]
+        for h in range(2):
+            lanes = slice(128 * h, 128 * h + 128)
+            latent = latent_ref[h, band(i), :].astype(F32)
+            enc_out = (latent + enc_raw[band(i), lanes]).astype(BF).astype(F32)
+            joined = (enc_out + inner[band(i), lanes]).astype(BF)
+            skip[h, band(i), :] = joined
+            value = joined.astype(F32)
+            sums = [sums[0] + value, sums[1] + value * value]
+        put_sums(cols, 0, i, sums)
 
     skip_rows = send_rows(5, skip.at[0], skip.at[1], skip_halo.at[0], skip_halo.at[1])
     third_note = share(3)
-    late_cot = send_rows(2, acts.at[3], acts.at[3], halo_cot.at[0], halo_cot.at[1])
+    late_cot = send_rows(2, cot_ref, cot_ref, halo_cot.at[0], halo_cot.at[1])
     gather_y_relay(2)
     gather_y_start(3)
     turn(back_ctl_two, AT_CTL_TWO, 320)
@@ -563,7 +645,7 @@
     spread(twenty, 24, norm_rows(total, 0))
     arrive(skip_rows)
 
-    @pl.loop(0, STEPS)
+    @each(STEPS)
     def _(i):
         mean = coef[band(i), 24:25]
         inv = coef[band(i), 25:26]
@@ -583,7 +665,7 @@
     dec_edge[1] = dec_raw[:, 128:256].astype(BF)
     dec_rows = send_rows(6, dec_edge.at[0], dec_edge.at[1], dec_halo.at[0], dec_halo.at[1])
 
-    @pl.loop(0, STEPS)
+    @each(STEPS)
     def _(i):
         value = dec_raw[band(i), :] + terms[band(i), 2:3]
         put_sums(cols, 0, i, [value, value * value])
@@ -596,27 +678,24 @@
     scale = 2.0**-8
 
     def cot_of(i):
-        far = halo_cot[0, band(i), :].astype(F32)
-        own = acts[3, band(i), :].astype(F32)
-        near = halo_cot[1, band(i), :].astype(F32)
-        far = jnp.where(has_up, far, 0.0) * scale
-        near = jnp.where(has_down, near, 0.0) * scale
-        own = own * scale
-        return [far[:, 0:128], far[:, 128:256], own[:, 0:128], own[:, 128:256], near[:, 0:128], near[:, 128:256]]
+        far_rows = [jnp.where(has_up, halo_cot[0, h, band(i), :].astype(F32), 0.0) for h in range(2)]
+        own = [cot_ref[h, band(i), :].astype(F32) for h in range(2)]
+        near_rows = [jnp.where(has_down, halo_cot[1, h, band(i), :].astype(F32), 0.0) for h in range(2)]
+        return [strip * scale for strip in far_rows + own + near_rows]
 
     gather_done(3)
     turn(back_dec_two, AT_DEC_TWO, 320)
     turn_square(short_t, AT_SHORT)
     for part in range(2):
 
-        @pl.loop(0, STEPS)
+        @each(STEPS)
         def _(i):
             strips = cot_of(i)[2 * part : 2 * part + 4]
             put_columns(col_g, spaced, i, strips)
 
         up_grad[:, 256 * part : 256 * part + 256] = dot(back_dec_two[...], col_g[...])
 
-    @pl.loop(0, STEPS)
+    @each(STEPS)
     def _(i):
         for k, strip in enumerate(cot_of(i)[1:5]):
             wide[band(i), 128 * k : 128 * k + 128] = strip.astype(BF)
@@ -636,7 +715,7 @@
         up_grad[band(i), 128 * k : 128 * k + 128] = upstream
         return (normed, upstream)
 
-    @pl.loop(0, STEPS)
+    @each(STEPS)
     def _(i):
         one_n, one_g = keep_dec_rows(i, dec_raw[band(i), 0:128], 1)
         two_n, two_g = keep_dec_rows(i, dec_raw[band(i), 128:256], 2)
@@ -645,7 +724,7 @@
     fifth_note = share(5)
     arrive(dec_rows)
 
-    @pl.loop(0, STEPS)
+    @each(STEPS)
     def _(i):
         keep_dec_rows(i, dec_halo[0, band(i), :].astype(F32), 0)
         keep_dec_rows(i, dec_halo[1, band(i), :].astype(F32), 3)
@@ -653,7 +732,7 @@
     total = collect(5, fifth_note)
     spread(ten, 40, mean_rows(total, 0))
 
-    @pl.loop(0, STEPS)
+    @each(STEPS)
     def _(i):
         inv = coef[band(i), 33:34]
         mean = coef[band(i), 40:41]
@@ -669,7 +748,7 @@
     sfg_edge[1] = sfg[:, 128:256].astype(BF)
     sfg_rows = send_rows(7, sfg_edge.at[0], sfg_edge.at[1], sfg_halo.at[0], sfg_halo.at[1])
 
-    @pl.loop(0, STEPS)
+    @each(STEPS)
     def _(i):
         normed = keep_skip[band(i), 128:384]
         value = sfg[band(i), :] * slope(normed)
@@ -679,7 +758,7 @@
     sixth_note = share(6)
     arrive(sfg_rows)
 
-    @pl.loop(0, STEPS)
+    @each(STEPS)
     def _(i):
         for at, lanes in ((0, slice(0, 128)), (1, slice(384, 512))):
             up_grad[band(i), lanes] = sfg_halo[at, band(i), :].astype(F32) * slope(keep_skip[band(i), lanes])
@@ -687,7 +766,7 @@
     total = collect(6, sixth_note)
     spread(twenty, 48, mean_rows(total, 0))
 
-    @pl.loop(0, STEPS)
+    @each(STEPS)
     def _(i):
         inv = coef[band(i), 25:26]
         mean = coef[band(i), 48:49]
@@ -697,7 +776,7 @@
 
     up_grad[...] = dot(zero_t[...], wide[...])
 
-    @pl.loop(0, STEPS)
+    @each(STEPS)
     def _(i):
         strips = []
         for k in range(4):
@@ -705,17 +784,6 @@
         wide_two[band(i), 0:128] = strips[1].astype(BF)
         wide_two[band(i), 128:256] = strips[2].astype(BF)
         put_columns(col_g, spaced, i, masked(strips))
-
-    sfg[...] = dot(back_ctl_two[...], col_g[...])
-
-    @pl.loop(0, STEPS)
-    def _(i):
-        normed = keep_n[band(i), :]
-        value = sfg[band(i), :] * slope(normed)
-        sfg[band(i), :] = value
-        put_sums(cols, 0, i, [value, value * normed])
-
-    seventh_note = share(7)
 
     def store_grads(k, value, at):
         count = value.shape[1]
@@ -740,49 +808,62 @@
     def reduce_far(k):
         swaps[k].wait_recv()
 
-        @pl.loop(0, STEPS)
+        @each(STEPS)
         def _(i):
             total = grads[k, band(i), lanes_at(c * 2048, 2048)].astype(F32) + swap[k, band(i), :].astype(F32)
             half[k, band(i), :] = total.astype(BF)
 
         pairs[k] = []
-        for j in (1, 3, 2):
-            ya = (y + j) % 4
-            xb = (x + j) % 4
-            pairs[k].append(
-                remote(
-                    half.at[k, 0:160, lanes_at(ya * 512, 512)],
-                    far.at[k, 0, j - 1],
-                    rs2_send.at[k, 0, j - 1],
-                    rs2_recv.at[k, 0, j - 1],
-                    y_peers[j - 1],
+        for axis, (where, ring_peers) in enumerate(((y, y_peers), (x, x_peers))):
+            rows = slice(160 * axis, 160 * axis + 160)
+            for j, (steps, part, target) in enumerate(((1, 256, 0), (2, 0, 0), (3, 0, 2), (2, 256, 2))):
+                block = half.at[k, rows, lanes_at((where + steps) % 4 * 512 + part, 256)]
+                pairs[k].append(
+                    remote(
+                        block,
+                        far.at[k, axis, j],
+                        rs2_send.at[k, axis, j],
+                        rs2_recv.at[k, axis, j],
+                        ring_peers[target],
+                    )
                 )
-            )
-            pairs[k].append(
-                remote(
-                    half.at[k, 160:C, lanes_at(xb * 512, 512)],
-                    far.at[k, 1, j - 1],
-                    rs2_send.at[k, 1, j - 1],
-                    rs2_recv.at[k, 1, j - 1],
-                    x_peers[j - 1],
+                pairs[k][-1].start()
+        waiting.extend(pairs[k])
+
+    relays = {}
+
+    def reduce_relay(k):
+        relays[k] = []
+        for axis, (where, ring_peers) in enumerate(((y, y_peers), (x, x_peers))):
+            rows = slice(160 * axis, 160 * axis + 160)
+            for j, (steps, part, target, source) in enumerate(((1, 0, 0, 1), (3, 256, 2, 3))):
+                pairs[k][4 * axis + source].wait_recv()
+                own = half[k, rows, lanes_at((where + steps) % 4 * 512 + part, 256)].astype(F32)
+                passing[k, axis, j] = (own + far[k, axis, source].astype(F32)).astype(BF)
+                relays[k].append(
+                    remote(
+                        passing.at[k, axis, j],
+                        far.at[k, axis, 4 + j],
+                        rs2_send.at[k, axis, 4 + j],
+                        rs2_recv.at[k, axis, 4 + j],
+                        ring_peers[target],
+                    )
                 )
-            )
-        for copy in pairs[k]:
-            copy.start()
-        waiting.extend(pairs[k])
+                relays[k][-1].start()
+        waiting.extend(relays[k])
 
     def reduce_near(k):
-        for copy in pairs[k]:
+        for axis in range(2):
+            pairs[k][4 * axis].wait_recv()
+            pairs[k][4 * axis + 2].wait_recv()
+        for copy in relays[k]:
             copy.wait_recv()
-
-        @pl.loop(0, STEPS // 2)
-        def _(i):
-            for which, where in ((0, y), (1, x)):
-                rows = pl.ds(pl.multiple_of(160 * which + i * ROWS, ROWS), ROWS)
-                total = half[k, rows, lanes_at(where * 512, 512)].astype(F32)
-                for j in range(3):
-                    total = total + far[k, which, j, band(i), :].astype(F32)
-                near[k, which, band(i), :] = total.astype(BF)
+        for axis, where in ((0, y), (1, x)):
+            rows = slice(160 * axis, 160 * axis + 160)
+            for part, direct, relayed in ((0, 2, 4), (256, 0, 5)):
+                total = half[k, rows, lanes_at(where * 512 + part, 256)].astype(F32)
+                total = total + far[k, axis, direct].astype(F32) + far[k, axis, relayed].astype(F32)
+                near[k, axis, :, part : part + 256] = total.astype(BF)
 
         fours[k] = []
         for j in (1, 3, 2):
@@ -824,10 +905,21 @@
     zero_value = lax.dot_general(wide[:, 128:384], ctl_out[...], NT, preferred_element_type=F32)
     store_grads(0, zero_value, 2944)
     reduce_core(0)
+    sfg[...] = dot(back_ctl_two[...], col_g[...])
+
+    @each(STEPS)
+    def _(i):
+        normed = keep_n[band(i), :]
+        value = sfg[band(i), :] * slope(normed)
+        sfg[band(i), :] = value
+        put_sums(cols, 0, i, [value, value * normed])
+
+    seventh_note = share(7)
+    reduce_far(0)
     total = collect(7, seventh_note)
     spread(ten, 56, mean_rows(total, 0))
 
-    @pl.loop(0, STEPS)
+    @each(STEPS)
     def _(i):
         inv = coef[band(i), 65:66]
         mean = coef[band(i), 56:57]
@@ -835,75 +927,87 @@
         value = inv * (sfg[band(i), :] - mean - keep_n[band(i), :] * cross)
         wide_two[band(i), :] = value.astype(BF)
 
-    reduce_far(0)
     one_value = lax.dot_general(wide_two[...], col_a[...], NT, preferred_element_type=F32)
     store_grads(1, one_value, 0)
     reduce_core(1)
+    reduce_relay(0)
     reduce_far(1)
     reduce_near(0)
+    reduce_relay(1)
+    reduce_deep(0)
     reduce_near(1)
-    reduce_deep(0)
     reduce_deep(1)
     ring = []
-    for k in (0, 2, 1):
-        zt = (zh + k + 1) % 4
+    for k in range(1, 8):
+        zt = (zh + k // 2) % 4
+        lt = (zl + k) % 2
         ring.append(
             remote(
-                deep.at[pl.ds(pl.multiple_of(zt * 80, 16), 80)],
-                deep_in.at[k],
-                rs4_send.at[k],
-                rs4_recv.at[k],
-                z_peers[k],
+                deep.at[pl.ds(pl.multiple_of(zt * 80, 16), 80), lanes_at(lt * 128, 128)],
+                deep_in.at[k - 1],
+                rs4_send.at[k - 1],
+                rs4_recv.at[k - 1],
+                z_all[k - 1],
             )
         )
         ring[-1].start()
-    for copy in ring:
-        copy.wait_recv()
-    total = deep[pl.ds(pl.multiple_of(zh * 80, 16), 80), :].astype(F32)
-    for k in range(3):
+    total = deep[pl.ds(pl.multiple_of(zh * 80, 16), 80), lanes_at(zl * 128, 128)].astype(F32)
+    for k in range(7):
+        ring[k].wait_recv()
         total = total + deep_in[k].astype(F32)
-    plane[...] = total
-    cross = remote(plane, plane_in, rs5_send.at[0], rs5_recv.at[0], other_z)
-    cross.start()
-    cross.wait_recv()
-    last[...] = plane[...] + plane_in[...]
+    last[...] = total
     for s in range(8):
-        fan[s, 0:10, :] = last[10 * s : 10 * s + 10, :]
-        fan[s, 10:16, :] = jnp.zeros((6, 256), F32)
+        spaced_rows = jnp.concatenate([last[10 * s : 10 * s + 10, :], jnp.zeros((6, 128), F32)], axis=0)
+        fan[s] = spaced_rows.astype(BF)
     sixth = []
     for k in range(7):
         s = (slot + k + 1) % 8
-        sixth.append(remote(fan.at[s], out.at[x, slot], rs6_send.at[k], rs6_recv.at[k], plane_peers[k]))
+        sixth.append(remote(fan.at[s], pool.at[r, slot], rs6_send.at[k], rs6_recv.at[k], plane_peers[k]))
         sixth[-1].start()
-    mine = pltpu.make_async_copy(fan.at[slot], out.at[x, slot], out_sem.at[0])
+    mine = pltpu.make_async_copy(fan.at[slot], pool.at[r, slot], out_sem.at[0])
     mine.start()
     mine.wait()
     for copy in sixth:
         copy.wait_recv()
     seventh = []
-    for k in range(3):
-        seventh.append(remote(out.at[x], out.at[x], rs7_send.at[k], rs7_recv.at[k], x_peers[k]))
+    for k in range(1, 8):
+        seventh.append(
+            remote(pool.at[r], pool.at[r], rs7_send.at[k - 1], rs7_recv.at[k - 1], peers[k - 1])
+        )
         seventh[-1].start()
     for copy in seventh:
         copy.wait_recv()
-    for copy in waiting + ring + [cross] + sixth + seventh:
+    for which, target, count in ((0, two_out, 23), (1, one_out, 23), (0, None, 26)):
+        for tile in range(23 if target is None else 0, count):
+            core, row_at, column_at = tile // 16, tile // 4 % 4, tile % 4
+            value = pool[which * 4 + column_at, row_at * 2 + core, 0:10, :].astype(F32)
+            if target is None:
+                size = min(128, C - (tile - 23) * 128)
+                zero_out[:, (tile - 23) * 128 : (tile - 23) * 128 + size] = value[:, 0:size]
+                continue
+            at = tile * 128
+            while at < min(tile * 128 + 128, 2880):
+                tap, offset = divmod(at, C)
+                size = min(C - offset, tile * 128 + 128 - at)
+                target[tap, :, offset : offset + size] = value[:, at - tile * 128 : at - tile * 128 + size]
+                at += size
+    for copy in waiting + ring + sixth + seventh:
         copy.wait_send()
 
 
-def run_step(shard, acts, terms, enc_one, enc_two):
-    x = lax.axis_index("rows") % 4
-    pieces = shard.reshape(10, 4, 4, 2, 4, 128)
-    pieces = lax.dynamic_index_in_dim(pieces, x, 4, keepdims=False)
-    pieces = jnp.transpose(pieces, (2, 3, 0, 1, 4)).reshape(8, 10, 512)
-    pieces = jnp.pad(pieces, ((0, 0), (0, 6), (0, 0)))
+def run_step(small, large):
     dma = pltpu.SemaphoreType.DMA
     whole = pl.BlockSpec(memory_space=pltpu.VMEM)
     far_off = pl.BlockSpec(memory_space=pl.ANY)
     return pl.pallas_call(
         step_kernel,
-        out_shape=jax.ShapeDtypeStruct((4, 8, 16, 256), F32),
-        in_specs=[whole, whole, whole, far_off, far_off],
-        out_specs=whole,
+        out_shape=(
+            jax.ShapeDtypeStruct((9, 10, C), F32),
+            jax.ShapeDtypeStruct((9, 10, C), F32),
+            jax.ShapeDtypeStruct((10, C), F32),
+        ),
+        in_specs=[whole] * len(small) + [far_off] * len(large),
+        out_specs=(whole, whole, whole),
         scratch_shapes=[
             pltpu.VMEM((C, 128), F32),
             pltpu.VMEM((C, 128), F32),
@@ -911,7 +1015,7 @@
             pltpu.VMEM((C, 128), F32),
             pltpu.VMEM((C, 128), F32),
             pltpu.VMEM((2, 3, C, 128), BF),
-            pltpu.VMEM((2, C, 256), BF),
+            pltpu.VMEM((2, 2, C, 128), BF),
             pltpu.VMEM((C, 256), F32),
             pltpu.VMEM((4, C, 128), BF),
             pltpu.VMEM((4, C, 128), BF),
@@ -947,11 +1051,16 @@
             pltpu.VMEM((8, 7, 8, 128), F32),
             dma((8, 7)),
             dma((8, 7)),
-            dma((8, 2)),
-            dma((8, 2)),
+            dma((9, 2)),
+            dma((9, 2)),
+            pltpu.VMEM((C, 128), F32),
+            pltpu.VMEM((C, 1280), BF),
+            pltpu.VMEM((3, C, 1280), BF),
+            pltpu.VMEM((16, LANES), BF),
+            pltpu.VMEM((8, 16, 512), BF),
             pltpu.VMEM((9, C, C), BF),
             pltpu.VMEM((9, C, C), BF),
-            dma((2,)),
+            dma((6,)),
             pltpu.VMEM((C, LANES), BF),
             pltpu.VMEM((8, 16, 512), BF),
             pltpu.VMEM((80, 512), F32),
@@ -970,41 +1079,34 @@
             pltpu.VMEM((2, C, HALF), BF),
             pltpu.VMEM((2, C, 2048), BF),
             pltpu.VMEM((2, C, 2048), BF),
-            pltpu.VMEM((2, 2, 3, 160, 512), BF),
+            pltpu.VMEM((2, 2, 6, 160, 256), BF),
             pltpu.VMEM((2, 2, 160, 512), BF),
+            pltpu.VMEM((2, 2, 2, 160, 256), BF),
             pltpu.VMEM((2, 2, 3, 160, 128), BF),
             pltpu.VMEM((C, 256), BF),
-            pltpu.VMEM((3, 80, 256), BF),
-            pltpu.VMEM((80, 256), F32),
-            pltpu.VMEM((80, 256), F32),
-            pltpu.VMEM((80, 256), F32),
-            pltpu.VMEM((8, 16, 256), F32),
+            pltpu.VMEM((7, 80, 128), BF),
+            pltpu.VMEM((80, 128), F32),
+            pltpu.VMEM((8, 16, 128), BF),
+            pltpu.VMEM((8, 8, 16, 128), BF),
             dma((1,)),
             dma((2,)),
             dma((2,)),
+            dma((2, 2, 6)),
+            dma((2, 2, 6)),
             dma((2, 2, 3)),
             dma((2, 2, 3)),
-            dma((2, 2, 3)),
-            dma((2, 2, 3)),
-            dma((3,)),
-            dma((3,)),
-            dma((1,)),
-            dma((1,)),
             dma((7,)),
             dma((7,)),
-            dma((3,)),
-            dma((3,)),
+            dma((7,)),
+            dma((7,)),
+            dma((7,)),
+            dma((7,)),
         ],
         compiler_params=pltpu.CompilerParams(
             collective_id=0, has_side_effects=True, vmem_limit_bytes=63 * 1024 * 1024
         ),
         name="train_step",
-    )(pieces, acts, terms, enc_one, enc_two)
-
-
-def flat(kernel, width):
-    kernel = kernel.reshape(kernel.shape[0], -1)
-    return jnp.pad(kernel, ((0, 0), (0, width - kernel.shape[1])))
+    )(*small, *large)
 
 
 def per_device(
@@ -1026,39 +1128,36 @@
     dec_shortcut,
     zero_conv,
 ):
-    shard = jnp.concatenate(
-        [
-            flat(ctl_conv_one, 2944),
-            flat(ctl_conv_two, 2944),
-            flat(zero_conv, 384),
-            flat(dec_conv_one, 5760),
-            flat(dec_shortcut[:, C:], 384),
-            flat(dec_conv_two, LANES - AT_DEC_TWO),
-        ],
-        axis=1,
-    )
     half_width = C // 2
     frequency = jnp.exp(-math.log(10000.0) * jnp.arange(half_width, dtype=jnp.float32) / half_width)
     angles = timesteps.astype(jnp.float32)[:, None] * frequency[None, :]
     sinusoid = jnp.concatenate([jnp.cos(angles), jnp.sin(angles)], axis=1).astype(jnp.bfloat16)
-    time_embed = jnp.dot(sinusoid, time_weight, preferred_element_type=jnp.float32)
-    time_act = jax.nn.silu(time_embed).astype(jnp.bfloat16)
-    terms = jnp.concatenate(
-        [jnp.dot(time_act, proj, preferred_element_type=jnp.float32) for proj in (enc_proj, ctl_proj, dec_proj)],
-        axis=0,
-    ).T
-    terms = jnp.pad(terms, ((0, 0), (0, 5)))
-    acts = jnp.stack([a.reshape(C, 256) for a in (latent, hint_field, from_below, cotangent)])
-    enc_one = jnp.transpose(enc_conv_one, (1, 2, 0, 3)).reshape(9, C, C)
-    enc_two = jnp.transpose(enc_conv_two, (1, 2, 0, 3)).reshape(9, C, C)
-    pieces = run_step(shard, acts, terms, enc_one, enc_two)
-    pieces = pieces[:, :, :10, :].reshape(4, 4, 2, 10, 2, 128)
-    owned = jnp.transpose(pieces, (3, 4, 2, 1, 0, 5)).reshape(10, 2, HALF)
-    return (
-        owned[:, 1, :2880].reshape(10, 3, 3, C),
-        owned[:, 0, :2880].reshape(10, 3, 3, C),
-        owned[:, 0, 2944:3264],
+    def by_row(field):
+        return jnp.transpose(field[0], (1, 0, 2))
+
+    def by_tap(kernel):
+        return jnp.transpose(kernel, (1, 2, 0, 3)).reshape(9, kernel.shape[0], kernel.shape[3])
+
+    def from_tap(grad):
+        return jnp.transpose(grad.reshape(3, 3, 10, C), (2, 0, 1, 3))
+
+    one_grad, two_grad, zero_grad = run_step(
+        (
+            jnp.broadcast_to(sinusoid, (16, C)),
+            by_row(latent),
+            by_row(hint_field),
+            by_row(from_below),
+            by_row(cotangent),
+            by_tap(ctl_conv_one),
+            by_tap(ctl_conv_two),
+            by_tap(dec_conv_one),
+            by_tap(dec_conv_two),
+            dec_shortcut,
+            zero_conv,
+        ),
+        (time_weight, enc_proj.T, ctl_proj.T, dec_proj.T, by_tap(enc_conv_one), by_tap(enc_conv_two)),
     )
+    return (from_tap(one_grad), from_tap(two_grad), zero_grad)
 
 
 def solution(mesh):

time: 201 us -> 164 us (0.82)
  Pallas kernels: 179 us -> 148 us
  other arithmetic: 2.18 us -> 0.13 us
    pallas_call x1, Pallas kernels: 179 us -> 148 us  [run_step(): pl.pallas_call(step_kernel, out_shape=(jax.ShapeDtypeStruct((9, 10, C), F...]
    transpose x1 -> x6, local copies, waits for them, and re-layouts: 0.21 us -> 9.77 us  [the longest x4 6.25 us: by_tap(): jnp.transpose(kernel, (1, 2, 0, 3))]
    another operation x6 -> x0, local copies, waits for them, and re-layouts: 5.95 us -> none  [the longest x4 4.32 us: per_device(): jnp.stack([a.reshape(C, 256) for a in (latent, hint_field, from_below, co...]
    reshape x9 -> x2, local copies, waits for them, and re-layouts: 5.9 us -> 3.37 us  [from_tap(): return jnp.transpose(grad.reshape(3, 3, 10, C), (2, 0, 1, 3))]
where the time goes in v4:
time: 164 us
  Pallas kernels  148 us (90%)
  local copies, waits for them, and re-layouts  15.1 us (9%)
    pallas_call x1, Pallas kernels, run_step(): pl.pallas_call(step_kernel, out_shape=(jax.ShapeDtypeStruct((9, 10, C), F...  148 us
    transpose x4, local copies, waits for them, and re-layouts, by_tap(): jnp.transpose(kernel, (1, 2, 0, 3))  6.25 us
    transpose x2, local copies, waits for them, and re-layouts, by_row(): return jnp.transpose(field[0], (1, 0, 2))  3.53 us
    reshape x2, local copies, waits for them, and re-layouts, from_tap(): return jnp.transpose(grad.reshape(3, 3, 10, C), (2, 0, 1, 3))  3.37 us

profile of v4, /device:TPU:1, one launch (start us, length us, event | category | flops | bytes accessed | tf_op | source)
XLA Modules:
  0.0 164.1 jit_solution(15405822407120273466)
XLA Ops:
  1.3 0.1 sine_convert_fusion
  1.3 0.1 pad_maximum_fusion
  1.4 0.6 broadcast_in_dim.2.sinus
  2.0 1.6 copy.24
  3.6 1.5 copy.25
  5.1 1.5 copy.27
  6.7 1.6 copy.26
  8.3 1.8 %copy_bitcast_fusion.4 = (bf16[2,320,128]{2,1,0:T(8,128)(2,1)}, bf16[2,320,128]{2,1,0:T(8,128)(2,1)}) fusion(bf16[1,320,2,128]{3,2,1,0:T(2,128)(2,1)} %param.18, bf16[1,320,2,128]{3,2,1,0:T(2,128)(2,1)} %param.17), kind=kLoop, calls=%fused_computation.4 | loop fusion | bytes 655360 | tf_op jit(solution)/shard_map/transpose | solution.py:1136
  10.0 1.8 %copy_bitcast_fusion.2 = (bf16[2,320,128]{2,1,0:T(8,128)(2,1)}, bf16[2,320,128]{2,1,0:T(8,128)(2,1)}) fusion(bf16[1,320,2,128]{3,2,1,0:T(2,128)(2,1)} %param.20, bf16[1,320,2,128]{3,2,1,0:T(2,128)(2,1)} %param.19), kind=kLoop, calls=%fused_computation.2 | loop fusion | bytes 655360 | tf_op jit(solution)/shard_map/transpose | solution.py:1136
  11.8 147.6 %train_step.1 = (f32[9,10,320]{2,1,0:T(8,128)}, f32[9,10,320]{2,1,0:T(8,128)}, f32[10,320]{1,0:T(8,128)}) custom-call(bf16[16,320]{1,0:T(8,128)(2,1)} %broadcast_in_dim.2.sinus, bf16[2,320,128]{2,1,0:T(8,128)(2,1)} %get-tuple-element.14.latent_ref, bf16[2,320,128]{2,1,0:T(8,128)(2,1)} %get-tuple-element.13.hint_ref, ...), custom_call_target="tpu_custom_call" | custom-call | tf_op jit(solution)/shard_map/train_step/pallas_call | solution.py:1002
  159.4 1.7 %copy.37 = f32[3,3,10,320]{3,1,0,2:T(4,128)} copy(f32[3,3,10,320]{3,2,1,0:T(8,128)} %bitcast.52) | data formatting | bytes 230400 | tf_op jit(solution)/shard_map/reshape | solution.py:1142
  161.1 1.7 %copy.36 = f32[3,3,10,320]{3,1,0,2:T(4,128)} copy(f32[3,3,10,320]{3,2,1,0:T(8,128)} %bitcast.51) | data formatting | bytes 230400 | tf_op jit(solution)/shard_map/reshape | solution.py:1142
  162.7 1.3 copy.40

commit v5 on v4

--- a/solution.py
+++ b/solution.py
@@ -98,6 +98,13 @@
     for tap in range(1, 9):
         total = total + dot(kernel[tap], col[C * tap : C * tap + C, :])
     return total
+
+
+def three_parts(value):
+    high = value.astype(BF).astype(F32)
+    rest = value - high
+    middle = rest.astype(BF).astype(F32)
+    return [high, middle, rest - middle]
 
 
 def put_sums(cols, at, i, pairs):
@@ -170,7 +177,6 @@
     note_recv,
     halo_send,
     halo_recv,
-    terms,
     time_weight,
     projections,
     stage,
@@ -205,6 +211,8 @@
     last,
     fan,
     pool,
+    tight,
+    opened,
     out_sem,
     rs1_send,
     rs1_recv,
@@ -266,16 +274,20 @@
     stage[0:10, AT_SHORT : AT_SHORT + C] = shard_short[:, C : 2 * C]
     for s in range(8):
         for g in range(4):
-            src[s, :, 128 * g : 128 * g + 128] = stage[:, lanes_at(g * 4096 + (s * 4 + x) * 128, 128)]
+            tile = (x * 2 + s % 2) * 4 + s // 2 if g % 2 else s * 4 + x
+            src[s, :, 128 * g : 128 * g + 128] = stage[:, lanes_at(g * 4096 + tile * 128, 128)]
 
     lane = lax.broadcasted_iota(jnp.int32, (C, 128), 1)
     channel = lax.broadcasted_iota(jnp.int32, (C, 128), 0)
     in_ten = (channel >= 10 * lane) & (channel < 10 * lane + 10)
     other = lane - 32
     in_twenty = (channel >= 20 * other) & (channel < 20 * other + 20)
-    ten[...] = jnp.where(in_ten, 1.0, 0.0)
-    twenty[...] = jnp.where(in_twenty, 1.0, 0.0)
-    member[...] = ten[...] + twenty[...]
+    one_ten = jnp.where(in_ten, 1.0, 0.0)
+    one_twenty = jnp.where(in_twenty, 1.0, 0.0)
+    member[...] = (one_ten + one_twenty).astype(BF)
+    for k in range(3):
+        ten[:, 128 * k : 128 * k + 128] = one_ten.astype(BF)
+        twenty[:, 128 * k : 128 * k + 128] = one_twenty.astype(BF)
     cols[...] = jnp.zeros((C, 128), F32)
 
     @each(STEPS)
@@ -339,21 +351,24 @@
                 second[g][-1].start()
             waiting.extend(second[g])
 
-    def gather_x(g):
+    def gather_short(g):
         for copy in second[g]:
             copy.wait_recv()
         block = gath.at[:, 128 * g : 128 * g + 128]
-        spot = weights.at[:, lanes_at(g * 4096 + (slot * 4 + x) * 128, 128)]
+        tile = (x * 2 + c) * 4 + y if g % 2 else slot * 4 + x
+        short_peers = y_peers if g % 2 else x_peers
+        spot = weights.at[:, lanes_at(g * 4096 + tile * 128, 128)]
         third[g] = []
         for k in (0, 2, 1):
-            third[g].append(remote(block, spot, ph3_send.at[g, k], ph3_recv.at[g, k], x_peers[k]))
+            third[g].append(remote(block, spot, ph3_send.at[g, k], ph3_recv.at[g, k], short_peers[k]))
             third[g][-1].start()
         waiting.extend(third[g])
         held[g] = pltpu.make_async_copy(block, spot, own_sem.at[g])
         held[g].start()
 
     def column_of(g, steps, at, size):
-        return weights.at[:, lanes_at(g * 4096 + ((y + 4 + steps) % 4 * 2 + c) * 512 + at, size)]
+        where = x if g % 2 else y
+        return weights.at[:, lanes_at(g * 4096 + ((where + 4 + steps) % 4 * 2 + c) * 512 + at, size)]
 
     def to_partner(g, k, steps):
         block = column_of(g, steps, 0, 512)
@@ -362,14 +377,17 @@
         fifth[g].append(copy)
         waiting.append(copy)
 
-    def gather_y_start(g):
+    def long_peers(g):
+        return x_peers if g % 2 else y_peers
+
+    def gather_long(g):
         held[g].wait()
         for copy in third[g]:
             copy.wait_recv()
         block = column_of(g, 0, 0, 512)
         fourth[g] = [
-            remote(block, block, ph4_send.at[g, 0], ph4_recv.at[g, 0], y_peers[0]),
-            remote(block, block, ph4_send.at[g, 1], ph4_recv.at[g, 1], y_peers[2]),
+            remote(block, block, ph4_send.at[g, 0], ph4_recv.at[g, 0], long_peers(g)[0]),
+            remote(block, block, ph4_send.at[g, 1], ph4_recv.at[g, 1], long_peers(g)[2]),
         ]
         for copy in fourth[g]:
             copy.start()
@@ -377,21 +395,21 @@
         fifth[g] = []
         to_partner(g, 0, 0)
 
-    def gather_y_relay(g):
+    def gather_relay(g):
         fourth[g][0].wait_recv()
         block = column_of(g, -1, 0, 256)
-        up = remote(block, block, ph4_send.at[g, 2], ph4_recv.at[g, 2], y_peers[0])
+        up = remote(block, block, ph4_send.at[g, 2], ph4_recv.at[g, 2], long_peers(g)[0])
         up.start()
         fourth[g][1].wait_recv()
         block = column_of(g, 1, 256, 256)
-        down = remote(block, block, ph4_send.at[g, 3], ph4_recv.at[g, 3], y_peers[2])
+        down = remote(block, block, ph4_send.at[g, 3], ph4_recv.at[g, 3], long_peers(g)[2])
         down.start()
         fourth[g].extend([up, down])
         waiting.extend([up, down])
         to_partner(g, 1, -1)
         to_partner(g, 2, 1)
 
-    def gather_y_finish(g):
+    def gather_finish(g):
         fourth[g][2].wait_recv()
         fourth[g][3].wait_recv()
         to_partner(g, 3, 2)
@@ -402,8 +420,9 @@
 
 
     def share(turn):
-        sums = lax.dot_general(cols[...], member[...], TN, precision=EXACT, preferred_element_type=F32)
-        note[turn] = sums[0:8]
+        turned = cols[:, 0:8].T
+        sums = dot(jnp.concatenate(three_parts(turned), axis=0).astype(BF), member[...])
+        note[turn] = sums[0:8] + sums[8:16] + sums[16:24]
         copies = []
         for k in range(1, 8):
             copies.append(
@@ -431,10 +450,20 @@
     per_group = jnp.where(which < 32, 1.0 / (10 * 2048), 1.0 / (20 * 2048))
 
     def spread(table, at, rows):
-        padded = jnp.concatenate(rows + [jnp.zeros((8 - len(rows), 128), F32)], axis=0)
-        coef[:, at : at + 8] = lax.dot_general(
-            table[...], padded, NT, precision=EXACT, preferred_element_type=F32
+        wide_rows = [
+            jnp.broadcast_to(jnp.concatenate(three_parts(row), axis=1), (128, 384)).astype(BF) for row in rows
+        ]
+        columns = lax.dot_general(
+            table[...], jnp.concatenate(wide_rows, axis=0), NT, preferred_element_type=F32
         )
+        for k in range(len(rows)):
+            coef[at + k] = columns[:, 128 * k : 128 * k + 128]
+
+    def raw_sums(raw_ref, term_at, i):
+        term = coef[term_at, band(i), :]
+        one = raw_ref[band(i), 0:128] + term
+        two = raw_ref[band(i), 128:256] + term
+        put_sums(cols, 0, i, [one + two, one * one + two * two])
 
     def norm_rows(total, k):
         mean = total[k : k + 1] * per_group[0:1]
@@ -456,15 +485,15 @@
         ]
 
     first_note = share(0)
-    gather_z()
     late = send_rows(1, under_ref.at[0], under_ref.at[1], halo.at[0, 2], halo.at[1, 2])
+    late_cot = send_rows(2, cot_ref, cot_ref, halo_cot.at[0], halo_cot.at[1])
     for load in loads[0:4]:
         load.wait()
     embed = dot(sinus[...], time_weight[...])
     embed = (embed * sig(embed)).astype(BF)
     for k in range(3):
         term = lax.dot_general(projections[k], embed, NT, preferred_element_type=F32)
-        terms[:, k : k + 1] = term[:, 0:1]
+        coef[20 + k] = jnp.broadcast_to(term[:, 0:1], (C, 128))
     for target in (back_dec_two, back_dec_one, back_ctl_two):
         for tap in range(9):
             target[:, 384 * tap + 320 : 384 * tap + 384] = jnp.zeros((C, 64), BF)
@@ -483,9 +512,10 @@
     def turn_square(target, start):
         target[...] = weights[:, start : start + 320].astype(F32).T.astype(BF)
 
+    gather_z()
     total = collect(0, first_note)
     spread(ten, 0, norm_rows(total, 0) + norm_rows(total, 2))
-    spread(twenty, 8, norm_rows(total, 4))
+    spread(twenty, 4, norm_rows(total, 4))
     arrive(raw)
     arrive(raw_hint)
 
@@ -495,8 +525,8 @@
     def first_act(source_of, at, col, base_of):
         @each(STEPS)
         def _(i):
-            mean = coef[band(i), at : at + 1]
-            inv = coef[band(i), at + 1 : at + 2]
+            mean = coef[at, band(i), :]
+            inv = coef[at + 1, band(i), :]
             strips = []
             for strip in source_of(i):
                 normed = (strip - mean) * inv
@@ -520,7 +550,6 @@
         ]
         return [(a + b).astype(BF).astype(F32) for a, b in zip(latent_of(i), hint)]
 
-    gather_x(0)
     first_act(latent_of, 0, col_t, plain)
     load_one.wait()
     enc_raw[...] = taps_dot(enc_one, col_t)
@@ -530,13 +559,11 @@
 
     @each(STEPS)
     def _(i):
-        enc = enc_raw[band(i), :] + terms[band(i), 0:1]
-        put_sums(cols, 0, i, [enc, enc * enc])
+        raw_sums(enc_raw, 20, i)
 
     second_note = share(1)
-    gather_x(1)
+    gather_short(0)
     first_act(ctl_in_of, 2, col_a, plain)
-    gather_y_start(0)
 
     def under_of(i):
         return [
@@ -556,18 +583,21 @@
         return 384 * tap
 
     arrive(late)
-    first_act(under_of, 8, col_d, joined_low)
-
+    first_act(under_of, 4, col_d, joined_low)
+
+    gather_short(1)
+    gather_long(0)
+    gather_short(2)
     total = collect(1, second_note)
-    spread(ten, 16, norm_rows(total, 0))
+    spread(ten, 6, norm_rows(total, 0))
 
     def second_act(raw_ref, at_halo, term_at, at, col, keep):
         @each(STEPS)
         def _(i):
-            mean = coef[band(i), at : at + 1]
-            inv = coef[band(i), at + 1 : at + 2]
+            mean = coef[at, band(i), :]
+            inv = coef[at + 1, band(i), :]
             own = raw_ref[band(i), :]
-            term = terms[band(i), term_at : term_at + 1]
+            term = coef[20 + term_at, band(i), :]
             strips = []
             for strip in (
                 inner_halo[at_halo, band(i), :].astype(F32),
@@ -582,13 +612,14 @@
             put_columns(col, plain, i, masked([v * sig(v) for v in strips]))
 
     arrive(enc_rows)
-    second_act(enc_raw, 0, 0, 16, col_t, None)
+    second_act(enc_raw, 0, 0, 6, col_t, None)
     load_two.wait()
     enc_raw[...] = taps_dot(enc_two, col_t)
-    gather_y_relay(0)
-    gather_y_start(1)
-    gather_x(2)
-    gather_y_finish(0)
+    gather_long(1)
+    gather_relay(0)
+    gather_short(3)
+    gather_long(2)
+    gather_finish(0)
     gather_done(0)
     ctl_raw[...] = dot(weights[:, AT_CTL_ONE : AT_CTL_ONE + 2880], col_a[...])
     edge[2] = ctl_raw[:, 0:128].astype(BF)
@@ -597,18 +628,16 @@
 
     @each(STEPS)
     def _(i):
-        ctl = ctl_raw[band(i), :] + terms[band(i), 1:2]
-        put_sums(cols, 0, i, [ctl, ctl * ctl])
+        raw_sums(ctl_raw, 21, i)
 
     ctl_note = share(2)
-    gather_y_relay(1)
-    gather_y_start(2)
-    gather_x(3)
+    gather_relay(1)
     total = collect(2, ctl_note)
-    spread(ten, 64, norm_rows(total, 0))
+    spread(ten, 8, norm_rows(total, 0))
     arrive(ctl_rows)
-    second_act(ctl_raw, 2, 1, 64, col_b, keep_n)
-    gather_y_finish(1)
+    second_act(ctl_raw, 2, 1, 8, col_b, keep_n)
+    gather_long(3)
+    gather_finish(1)
     gather_done(1)
     inner[...] = dot(weights[:, AT_CTL_TWO : AT_CTL_TWO + 2880], col_b[...])
 
@@ -635,20 +664,19 @@
 
     skip_rows = send_rows(5, skip.at[0], skip.at[1], skip_halo.at[0], skip_halo.at[1])
     third_note = share(3)
-    late_cot = send_rows(2, cot_ref, cot_ref, halo_cot.at[0], halo_cot.at[1])
-    gather_y_relay(2)
-    gather_y_start(3)
     turn(back_ctl_two, AT_CTL_TWO, 320)
     turn_square(zero_t, AT_ZERO)
+    gather_relay(2)
+    gather_relay(3)
 
     total = collect(3, third_note)
-    spread(twenty, 24, norm_rows(total, 0))
+    spread(twenty, 10, norm_rows(total, 0))
     arrive(skip_rows)
 
     @each(STEPS)
     def _(i):
-        mean = coef[band(i), 24:25]
-        inv = coef[band(i), 25:26]
+        mean = coef[10, band(i), :]
+        inv = coef[11, band(i), :]
         strips = []
         for k, strip in enumerate(
             (skip_halo[0, band(i), :], skip[0, band(i), :], skip[1, band(i), :], skip_halo[1, band(i), :])
@@ -658,7 +686,7 @@
             strips.append(normed * sig(normed))
         put_columns(col_d, joined_high, i, masked(strips))
 
-    gather_y_finish(2)
+    gather_finish(2)
     gather_done(2)
     dec_raw[...] = dot(weights[:, AT_DEC_ONE : AT_DEC_ONE + 5760], col_d[...])
     dec_edge[0] = dec_raw[:, 0:128].astype(BF)
@@ -667,13 +695,11 @@
 
     @each(STEPS)
     def _(i):
-        value = dec_raw[band(i), :] + terms[band(i), 2:3]
-        put_sums(cols, 0, i, [value, value * value])
+        raw_sums(dec_raw, 22, i)
 
     fourth_note = share(4)
     turn(back_dec_one, AT_DEC_ONE + 320, 640)
-    gather_y_relay(3)
-    gather_y_finish(3)
+    gather_finish(3)
     arrive(late_cot)
     scale = 2.0**-8
 
@@ -703,12 +729,12 @@
     mixed[...] = dot(short_t[...], wide[...])
 
     total = collect(4, fourth_note)
-    spread(ten, 32, norm_rows(total, 0))
+    spread(ten, 12, norm_rows(total, 0))
 
     def keep_dec_rows(i, strip, k):
-        mean = coef[band(i), 32:33]
-        inv = coef[band(i), 33:34]
-        term = terms[band(i), 2:3]
+        mean = coef[12, band(i), :]
+        inv = coef[13, band(i), :]
+        term = coef[22, band(i), :]
         normed = (strip + term - mean) * inv
         keep_dec[band(i), 128 * k : 128 * k + 128] = normed
         upstream = up_grad[band(i), 128 * k : 128 * k + 128] * slope(normed)
@@ -730,13 +756,13 @@
         keep_dec_rows(i, dec_halo[1, band(i), :].astype(F32), 3)
 
     total = collect(5, fifth_note)
-    spread(ten, 40, mean_rows(total, 0))
-
-    @each(STEPS)
-    def _(i):
-        inv = coef[band(i), 33:34]
-        mean = coef[band(i), 40:41]
-        cross = coef[band(i), 41:42]
+    spread(ten, 14, mean_rows(total, 0))
+
+    @each(STEPS)
+    def _(i):
+        inv = coef[13, band(i), :]
+        mean = coef[14, band(i), :]
+        cross = coef[15, band(i), :]
         strips = []
         for k in range(4):
             lanes = slice(128 * k, 128 * k + 128)
@@ -764,15 +790,17 @@
             up_grad[band(i), lanes] = sfg_halo[at, band(i), :].astype(F32) * slope(keep_skip[band(i), lanes])
 
     total = collect(6, sixth_note)
-    spread(twenty, 48, mean_rows(total, 0))
-
-    @each(STEPS)
-    def _(i):
-        inv = coef[band(i), 25:26]
-        mean = coef[band(i), 48:49]
-        cross = coef[band(i), 49:50]
-        value = inv * (up_grad[band(i), :] - mean - keep_skip[band(i), :] * cross) + mixed[band(i), :]
-        wide[band(i), :] = value.astype(BF)
+    spread(twenty, 16, mean_rows(total, 0))
+
+    @each(STEPS)
+    def _(i):
+        inv = coef[11, band(i), :]
+        mean = coef[16, band(i), :]
+        cross = coef[17, band(i), :]
+        for k in range(4):
+            lanes = slice(128 * k, 128 * k + 128)
+            value = inv * (up_grad[band(i), lanes] - mean - keep_skip[band(i), lanes] * cross) + mixed[band(i), lanes]
+            wide[band(i), lanes] = value.astype(BF)
 
     up_grad[...] = dot(zero_t[...], wide[...])
 
@@ -917,15 +945,16 @@
     seventh_note = share(7)
     reduce_far(0)
     total = collect(7, seventh_note)
-    spread(ten, 56, mean_rows(total, 0))
-
-    @each(STEPS)
-    def _(i):
-        inv = coef[band(i), 65:66]
-        mean = coef[band(i), 56:57]
-        cross = coef[band(i), 57:58]
-        value = inv * (sfg[band(i), :] - mean - keep_n[band(i), :] * cross)
-        wide_two[band(i), :] = value.astype(BF)
+    spread(ten, 18, mean_rows(total, 0))
+
+    @each(STEPS)
+    def _(i):
+        inv = coef[9, band(i), :]
+        mean = coef[18, band(i), :]
+        cross = coef[19, band(i), :]
+        for lanes in (slice(0, 128), slice(128, 256)):
+            value = inv * (sfg[band(i), lanes] - mean - keep_n[band(i), lanes] * cross)
+            wide_two[band(i), lanes] = value.astype(BF)
 
     one_value = lax.dot_general(wide_two[...], col_a[...], NT, preferred_element_type=F32)
     store_grads(1, one_value, 0)
@@ -962,25 +991,30 @@
     sixth = []
     for k in range(7):
         s = (slot + k + 1) % 8
-        sixth.append(remote(fan.at[s], pool.at[r, slot], rs6_send.at[k], rs6_recv.at[k], plane_peers[k]))
+        sixth.append(remote(fan.at[s], pool.at[slot], rs6_send.at[k], rs6_recv.at[k], plane_peers[k]))
         sixth[-1].start()
-    mine = pltpu.make_async_copy(fan.at[slot], pool.at[r, slot], out_sem.at[0])
+    mine = pltpu.make_async_copy(fan.at[slot], pool.at[slot], out_sem.at[0])
     mine.start()
     mine.wait()
     for copy in sixth:
         copy.wait_recv()
+    for s in range(8):
+        last[10 * s : 10 * s + 10, :] = pool[s, 0:10, :].astype(F32)
+    tight[r] = last[...].astype(BF)
     seventh = []
     for k in range(1, 8):
         seventh.append(
-            remote(pool.at[r], pool.at[r], rs7_send.at[k - 1], rs7_recv.at[k - 1], peers[k - 1])
+            remote(tight.at[r], tight.at[r], rs7_send.at[k - 1], rs7_recv.at[k - 1], peers[k - 1])
         )
         seventh[-1].start()
     for copy in seventh:
         copy.wait_recv()
+    opened[...] = tight[...].astype(F32)
     for which, target, count in ((0, two_out, 23), (1, one_out, 23), (0, None, 26)):
         for tile in range(23 if target is None else 0, count):
             core, row_at, column_at = tile // 16, tile // 4 % 4, tile % 4
-            value = pool[which * 4 + column_at, row_at * 2 + core, 0:10, :].astype(F32)
+            at = 10 * (row_at * 2 + core)
+            value = opened[which * 4 + column_at, at : at + 10, :]
             if target is None:
                 size = min(128, C - (tile - 23) * 128)
                 zero_out[:, (tile - 23) * 128 : (tile - 23) * 128 + size] = value[:, 0:size]
@@ -1009,11 +1043,11 @@
         in_specs=[whole] * len(small) + [far_off] * len(large),
         out_specs=(whole, whole, whole),
         scratch_shapes=[
+            pltpu.VMEM((C, 128), BF),
+            pltpu.VMEM((C, 384), BF),
+            pltpu.VMEM((C, 384), BF),
             pltpu.VMEM((C, 128), F32),
-            pltpu.VMEM((C, 128), F32),
-            pltpu.VMEM((C, 128), F32),
-            pltpu.VMEM((C, 128), F32),
-            pltpu.VMEM((C, 128), F32),
+            pltpu.VMEM((23, C, 128), F32),
             pltpu.VMEM((2, 3, C, 128), BF),
             pltpu.VMEM((2, 2, C, 128), BF),
             pltpu.VMEM((C, 256), F32),
@@ -1053,7 +1087,6 @@
             dma((8, 7)),
             dma((9, 2)),
             dma((9, 2)),
-            pltpu.VMEM((C, 128), F32),
             pltpu.VMEM((C, 1280), BF),
             pltpu.VMEM((3, C, 1280), BF),
             pltpu.VMEM((16, LANES), BF),
@@ -1087,7 +1120,9 @@
             pltpu.VMEM((7, 80, 128), BF),
             pltpu.VMEM((80, 128), F32),
             pltpu.VMEM((8, 16, 128), BF),
-            pltpu.VMEM((8, 8, 16, 128), BF),
+            pltpu.VMEM((8, 16, 128), BF),
+            pltpu.VMEM((8, 80, 128), BF),
+            pltpu.VMEM((8, 80, 128), F32),
             dma((1,)),
             dma((2,)),
             dma((2,)),

time: 164 us -> 156 us (0.951)
  Pallas kernels: 148 us -> 139 us
    pallas_call x1, Pallas kernels: 148 us -> 139 us  [run_step(): pl.pallas_call(step_kernel, out_shape=(jax.ShapeDtypeStruct((9, 10, C), F...]
where the time goes in v5:
time: 156 us
  Pallas kernels  139 us (89%)
  local copies, waits for them, and re-layouts  15.1 us (10%)
    pallas_call x1, Pallas kernels, run_step(): pl.pallas_call(step_kernel, out_shape=(jax.ShapeDtypeStruct((9, 10, C), F...  139 us
    transpose x4, local copies, waits for them, and re-layouts, by_tap(): jnp.transpose(kernel, (1, 2, 0, 3))  6.25 us
    transpose x2, local copies, waits for them, and re-layouts, by_row(): return jnp.transpose(field[0], (1, 0, 2))  3.53 us
    reshape x2, local copies, waits for them, and re-layouts, from_tap(): return jnp.transpose(grad.reshape(3, 3, 10, C), (2, 0, 1, 3))  3.37 us

profile of v5, /device:TPU:1, one launch (start us, length us, event | category | flops | bytes accessed | tf_op | source)
XLA Modules:
  0.0 155.8 jit_solution(14244606326978312047)
XLA Ops:
  1.3 0.1 sine_convert_fusion
  1.3 0.1 pad_maximum_fusion
  1.4 0.6 broadcast_in_dim.2.sinus
  2.0 1.6 %copy.24 = bf16[3,3,10,320]{3,2,1,0:T(8,128)(2,1)} copy(bf16[3,3,10,320]{3,1,0,2:T(4,128)(2,1)} %bitcast.56) | data formatting | bytes 115200 | tf_op jit(solution)/shard_map/transpose | solution.py:1174
  3.6 1.5 copy.25
  5.1 1.5 copy.27
  6.7 1.6 %copy.26 = bf16[3,3,10,640]{3,2,1,0:T(8,128)(2,1)} copy(bf16[3,3,10,640]{3,1,0,2:T(4,128)(2,1)} %bitcast.55) | data formatting | bytes 230400 | tf_op jit(solution)/shard_map/transpose | solution.py:1174
  8.3 1.8 %copy_bitcast_fusion.4 = (bf16[2,320,128]{2,1,0:T(8,128)(2,1)}, bf16[2,320,128]{2,1,0:T(8,128)(2,1)}) fusion(bf16[1,320,2,128]{3,2,1,0:T(2,128)(2,1)} %param.18, bf16[1,320,2,128]{3,2,1,0:T(2,128)(2,1)} %param.17), kind=kLoop, calls=%fused_computation.4 | loop fusion | bytes 655360 | tf_op jit(solution)/shard_map/transpose | solution.py:1171
  10.0 1.8 %copy_bitcast_fusion.2 = (bf16[2,320,128]{2,1,0:T(8,128)(2,1)}, bf16[2,320,128]{2,1,0:T(8,128)(2,1)}) fusion(bf16[1,320,2,128]{3,2,1,0:T(2,128)(2,1)} %param.20, bf16[1,320,2,128]{3,2,1,0:T(2,128)(2,1)} %param.19), kind=kLoop, calls=%fused_computation.2 | loop fusion | bytes 655360 | tf_op jit(solution)/shard_map/transpose | solution.py:1171
  11.8 139.3 %train_step.1 = (f32[9,10,320]{2,1,0:T(8,128)}, f32[9,10,320]{2,1,0:T(8,128)}, f32[10,320]{1,0:T(8,128)}) custom-call(bf16[16,320]{1,0:T(8,128)(2,1)} %broadcast_in_dim.2.sinus, bf16[2,320,128]{2,1,0:T(8,128)(2,1)} %get-tuple-element.14.latent_ref, bf16[2,320,128]{2,1,0:T(8,128)(2,1)} %get-tuple-element.13.hint_ref, ...), custom_call_target="tpu_custom_call" | custom-call | tf_op jit(solution)/shard_map/train_step/pallas_call | solution.py:1036
  151.1 1.7 %copy.37 = f32[3,3,10,320]{3,1,0,2:T(4,128)} copy(f32[3,3,10,320]{3,2,1,0:T(8,128)} %bitcast.52) | data formatting | bytes 230400 | tf_op jit(solution)/shard_map/reshape | solution.py:1177
  152.8 1.7 %copy.36 = f32[3,3,10,320]{3,1,0,2:T(4,128)} copy(f32[3,3,10,320]{3,2,1,0:T(8,128)} %bitcast.51) | data formatting | bytes 230400 | tf_op jit(solution)/shard_map/reshape | solution.py:1177
  154.5 1.3 copy.40

commit v6 on v5

--- a/solution.py
+++ b/solution.py
@@ -269,7 +269,7 @@
         (shard_dec_two, AT_DEC_TWO, 9, C),
     ):
         for tap in range(count):
-            stage[0:10, start + width * tap : start + width * tap + width] = kernel[tap]
+            stage[0:10, start + width * tap : start + width * tap + width] = kernel[:, tap // 3, tap % 3, :]
     stage[0:10, AT_ZERO : AT_ZERO + C] = shard_zero[...]
     stage[0:10, AT_SHORT : AT_SHORT + C] = shard_short[:, C : 2 * C]
     for s in range(8):
@@ -485,8 +485,6 @@
         ]
 
     first_note = share(0)
-    late = send_rows(1, under_ref.at[0], under_ref.at[1], halo.at[0, 2], halo.at[1, 2])
-    late_cot = send_rows(2, cot_ref, cot_ref, halo_cot.at[0], halo_cot.at[1])
     for load in loads[0:4]:
         load.wait()
     embed = dot(sinus[...], time_weight[...])
@@ -513,6 +511,8 @@
         target[...] = weights[:, start : start + 320].astype(F32).T.astype(BF)
 
     gather_z()
+    late = send_rows(1, under_ref.at[0], under_ref.at[1], halo.at[0, 2], halo.at[1, 2])
+    late_cot = send_rows(2, cot_ref, cot_ref, halo_cot.at[0], halo_cot.at[1])
     total = collect(0, first_note)
     spread(ten, 0, norm_rows(total, 0) + norm_rows(total, 2))
     spread(twenty, 4, norm_rows(total, 4))
@@ -1183,10 +1183,10 @@
             by_row(hint_field),
             by_row(from_below),
             by_row(cotangent),
-            by_tap(ctl_conv_one),
-            by_tap(ctl_conv_two),
-            by_tap(dec_conv_one),
-            by_tap(dec_conv_two),
+            ctl_conv_one,
+            ctl_conv_two,
+            dec_conv_one,
+            dec_conv_two,
             dec_shortcut,
             zero_conv,
         ),

time: 156 us -> 151 us (0.968)
  local copies, waits for them, and re-layouts: 15.1 us -> 8.84 us
    transpose x4 -> x0, local copies, waits for them, and re-layouts: 6.25 us -> none  [by_tap(): jnp.transpose(kernel, (1, 2, 0, 3))]
where the time goes in v6:
time: 151 us
  Pallas kernels  140 us (93%)
  local copies, waits for them, and re-layouts  8.84 us (6%)
    pallas_call x1, Pallas kernels, run_step(): pl.pallas_call(step_kernel, out_shape=(jax.ShapeDtypeStruct((9, 10, C), F...  140 us
    transpose x2, local copies, waits for them, and re-layouts, by_row(): return jnp.transpose(field[0], (1, 0, 2))  3.52 us
    reshape x2, local copies, waits for them, and re-layouts, from_tap(): return jnp.transpose(grad.reshape(3, 3, 10, C), (2, 0, 1, 3))  3.37 us

profile of v6, /device:TPU:1, one launch (start us, length us, event | category | flops | bytes accessed | tf_op | source)
XLA Modules:
  0.0 150.5 jit_solution(629699514469195177)
XLA Ops:
  1.3 0.1 sine_convert_fusion
  1.3 0.1 pad_maximum_fusion
  1.4 0.6 broadcast_in_dim.2.sinus
  2.0 1.8 %copy_bitcast_fusion.4 = (bf16[2,320,128]{2,1,0:T(8,128)(2,1)}, bf16[2,320,128]{2,1,0:T(8,128)(2,1)}) fusion(bf16[1,320,2,128]{3,2,1,0:T(2,128)(2,1)} %param.18, bf16[1,320,2,128]{3,2,1,0:T(2,128)(2,1)} %param.17), kind=kLoop, calls=%fused_computation.4 | loop fusion | bytes 655360 | tf_op jit(solution)/shard_map/transpose | solution.py:1171
  3.8 1.8 %copy_bitcast_fusion.2 = (bf16[2,320,128]{2,1,0:T(8,128)(2,1)}, bf16[2,320,128]{2,1,0:T(8,128)(2,1)}) fusion(bf16[1,320,2,128]{3,2,1,0:T(2,128)(2,1)} %param.20, bf16[1,320,2,128]{3,2,1,0:T(2,128)(2,1)} %param.19), kind=kLoop, calls=%fused_computation.2 | loop fusion | bytes 655360 | tf_op jit(solution)/shard_map/transpose | solution.py:1171
  5.5 140.3 %train_step.1 = (f32[9,10,320]{2,1,0:T(8,128)}, f32[9,10,320]{2,1,0:T(8,128)}, f32[10,320]{1,0:T(8,128)}) custom-call(bf16[16,320]{1,0:T(8,128)(2,1)} %broadcast_in_dim.2.sinus, bf16[2,320,128]{2,1,0:T(8,128)(2,1)} %get-tuple-element.14.latent_ref, bf16[2,320,128]{2,1,0:T(8,128)(2,1)} %get-tuple-element.13.hint_ref, ...), custom_call_target="tpu_custom_call" | custom-call | tf_op jit(solution)/shard_map/train_step/pallas_call | solution.py:1036
  145.8 1.7 %copy.33 = f32[3,3,10,320]{3,1,0,2:T(4,128)} copy(f32[3,3,10,320]{3,2,1,0:T(8,128)} %bitcast.40) | data formatting | bytes 230400 | tf_op jit(solution)/shard_map/reshape | solution.py:1177
  147.5 1.7 %copy.32 = f32[3,3,10,320]{3,1,0,2:T(4,128)} copy(f32[3,3,10,320]{3,2,1,0:T(8,128)} %bitcast.39) | data formatting | bytes 230400 | tf_op jit(solution)/shard_map/reshape | solution.py:1177
  149.2 1.3 copy.36

commit v7 on v6

--- a/solution.py
+++ b/solution.py
@@ -512,7 +512,6 @@
 
     gather_z()
     late = send_rows(1, under_ref.at[0], under_ref.at[1], halo.at[0, 2], halo.at[1, 2])
-    late_cot = send_rows(2, cot_ref, cot_ref, halo_cot.at[0], halo_cot.at[1])
     total = collect(0, first_note)
     spread(ten, 0, norm_rows(total, 0) + norm_rows(total, 2))
     spread(twenty, 4, norm_rows(total, 4))
@@ -582,8 +581,6 @@
     def spaced(tap):
         return 384 * tap
 
-    arrive(late)
-    first_act(under_of, 4, col_d, joined_low)
 
     gather_short(1)
     gather_long(0)
@@ -616,6 +613,8 @@
     load_two.wait()
     enc_raw[...] = taps_dot(enc_two, col_t)
     gather_long(1)
+    arrive(late)
+    first_act(under_of, 4, col_d, joined_low)
     gather_relay(0)
     gather_short(3)
     gather_long(2)
@@ -632,6 +631,7 @@
 
     ctl_note = share(2)
     gather_relay(1)
+    late_cot = send_rows(2, cot_ref, cot_ref, halo_cot.at[0], halo_cot.at[1])
     total = collect(2, ctl_note)
     spread(ten, 8, norm_rows(total, 0))
     arrive(ctl_rows)

time: 151 us -> 151 us (level)
  no operation moved by 1% of the time
where the time goes in v7:
time: 151 us; the launch traced here: 150 us
  Pallas kernels  140 us (93%)
  local copies, waits for them, and re-layouts  8.84 us (6%)
    pallas_call x1, Pallas kernels, run_step(): pl.pallas_call(step_kernel, out_shape=(jax.ShapeDtypeStruct((9, 10, C), F...  140 us
    transpose x2, local copies, waits for them, and re-layouts, by_row(): return jnp.transpose(field[0], (1, 0, 2))  3.52 us
    reshape x2, local copies, waits for them, and re-layouts, from_tap(): return jnp.transpose(grad.reshape(3, 3, 10, C), (2, 0, 1, 3))  3.37 us

profile of v7, /device:TPU:1, one launch (start us, length us, event | category | flops | bytes accessed | tf_op | source)
XLA Modules:
  0.0 150.3 jit_solution(10735186501273910721)
XLA Ops:
  1.3 0.1 sine_convert_fusion
  1.3 0.1 pad_maximum_fusion
  1.4 0.6 broadcast_in_dim.2.sinus
  2.0 1.8 %copy_bitcast_fusion.4 = (bf16[2,320,128]{2,1,0:T(8,128)(2,1)}, bf16[2,320,128]{2,1,0:T(8,128)(2,1)}) fusion(bf16[1,320,2,128]{3,2,1,0:T(2,128)(2,1)} %param.18, bf16[1,320,2,128]{3,2,1,0:T(2,128)(2,1)} %param.17), kind=kLoop, calls=%fused_computation.4 | loop fusion | bytes 655360 | tf_op jit(solution)/shard_map/transpose | solution.py:1171
  3.8 1.8 %copy_bitcast_fusion.2 = (bf16[2,320,128]{2,1,0:T(8,128)(2,1)}, bf16[2,320,128]{2,1,0:T(8,128)(2,1)}) fusion(bf16[1,320,2,128]{3,2,1,0:T(2,128)(2,1)} %param.20, bf16[1,320,2,128]{3,2,1,0:T(2,128)(2,1)} %param.19), kind=kLoop, calls=%fused_computation.2 | loop fusion | bytes 655360 | tf_op jit(solution)/shard_map/transpose | solution.py:1171
  5.5 140.0 %train_step.1 = (f32[9,10,320]{2,1,0:T(8,128)}, f32[9,10,320]{2,1,0:T(8,128)}, f32[10,320]{1,0:T(8,128)}) custom-call(bf16[16,320]{1,0:T(8,128)(2,1)} %broadcast_in_dim.2.sinus, bf16[2,320,128]{2,1,0:T(8,128)(2,1)} %get-tuple-element.14.latent_ref, bf16[2,320,128]{2,1,0:T(8,128)(2,1)} %get-tuple-element.13.hint_ref, ...), custom_call_target="tpu_custom_call" | custom-call | tf_op jit(solution)/shard_map/train_step/pallas_call | solution.py:1036
  145.6 1.7 %copy.33 = f32[3,3,10,320]{3,1,0,2:T(4,128)} copy(f32[3,3,10,320]{3,2,1,0:T(8,128)} %bitcast.40) | data formatting | bytes 230400 | tf_op jit(solution)/shard_map/reshape | solution.py:1177
  147.3 1.7 %copy.32 = f32[3,3,10,320]{3,1,0,2:T(4,128)} copy(f32[3,3,10,320]{3,2,1,0:T(8,128)} %bitcast.39) | data formatting | bytes 230400 | tf_op jit(solution)/shard_map/reshape | solution.py:1177
  149.0 1.3 copy.36
